TPU v7x, 32 devices: a whole 2x2x4 slice. The times are simulated.
32 devices in a mesh: row: 4 (over y, x), col: 8 (over z, core).
Axes of the slice: x: 2, y: 2, z: 4, core: 2. Of those that a mesh axis runs over, the one named last changes fastest.
Arguments:
- rhs: float32 [1536, 3072], P('row', 'col'), may hold values from -6 to 6
- a_coupling: bfloat16 [3, 1536, 3072], P(None, 'row', 'col'), may hold values from -0.3125 to 0.3125
- b_coupling: bfloat16 [3, 1536, 3072], P(None, 'row', 'col'), may hold values from -0.3125 to 0.3125
- a_basis: float32 [1536, 384], P('row'), may hold values from -0.3125 to 0.3125
- b_basis: float32 [3072, 384], P('col'), may hold values from -0.3125 to 0.3125
- a_vals: float32 [1536], P('row'), may hold values from 0.25 to 4
- b_vals: float32 [3072], P('col'), may hold values from 0.25 to 4
Outputs:
- solution: bfloat16 [1536, 3072], P('row', 'col')
- rhs_next: float32 [1536, 3072], P('row', 'col')
All inputs are finite; a program needn't handle non-finite values.
Results may differ from a plain program's by a relative error of at most 0.0037.
Values may be sent and summed in bfloat16 or wider, within the bound.
No kernel may reach another device: no remote copies, remote signals or barrier semaphores. Data moves between devices by JAX's collectives and lax.ppermute only.
A program may use at most 64 MiB of HBM per device.

v0:
```python
import functools

import jax
import jax.numpy as jnp
from jax import lax
from jax.experimental import pallas as pl
from jax.experimental.pallas import tpu as pltpu
from jax.sharding import PartitionSpec as P


AXES = ("row", "col")
VMEM_SPEC = pl.BlockSpec(memory_space=pltpu.VMEM)
FAR_SPEC = pl.BlockSpec(memory_space=pltpu.HBM)


def plan(rows_n, cols_n, offset, gap, up_gap):
    rights, ups = [], []
    for i in range(rows_n):
        m = i + offset
        if 0 <= m < cols_n:
            targets = range(m + gap, cols_n)
            for chip in sorted({j // 2 for j in targets}, reverse=True):
                rights.append(((i, m), [(i, j) for j in targets if j // 2 == chip]))
            ups += [((i, m), (k, m)) for k in range(i - up_gap, -1, -1)]
    ops, forwards = [], []
    while rights or ups:
        used_from, used_to, op = set(), set(), []

        def take(source, target, kind):
            if source in used_from or target in used_to:
                return False
            used_from.add(source)
            used_to.add(target)
            op.append((source, target, kind, None))
            return True

        for item in list(rights):
            source, targets = item
            waiting = [t for _, t in ups]
            for target in sorted(targets, key=lambda t: t in waiting):
                if take(source, target, "left"):
                    rights.remove(item)
                    forwards += [(target, other, "left", len(ops)) for other in targets if other != target]
                    break
        for item in list(ups):
            if take(*item, "down"):
                ups.remove(item)
        ops.append(op)
    return ops + [forwards] if forwards else ops


def one_of(me, ids):
    hit = me < 0
    for each in sorted(ids):
        hit = hit | (me == each)
    return hit


def place(cols_n):
    return lax.axis_index("row") * cols_n + lax.axis_index("col")


def level_of(rows_n):
    return rows_n - 1 - lax.axis_index("row") + lax.axis_index("col")


def dot(a, b):
    return lax.dot_general(a, b, (((1,), (0,)), ((), ())), preferred_element_type=jnp.float32)


def split(x):
    high = x.astype(jnp.bfloat16)
    return high, (x - high.astype(jnp.float32)).astype(jnp.bfloat16)


def put_left(ref, pair):
    n = pair[0].shape[1]
    ref[:, 0:n] = pair[0]
    ref[:, n : 2 * n] = pair[0]
    ref[:, 2 * n : 3 * n] = pair[1]


def put_right(ref, pair):
    n = pair[0].shape[0]
    ref[0:n] = pair[0]
    ref[n : 2 * n] = pair[1]
    ref[2 * n : 3 * n] = pair[0]


def dot_t(a, b):
    return lax.dot_general(a, b, (((1,), (1,)), ((), ())), preferred_element_type=jnp.float32)


def solve(state, uk, utk, vk, vl, inverse, lhs, mid):
    put_left(lhs, split(state))
    part = dot(lhs[...], vk[...])
    put_right(mid, split(part))
    part = dot(utk[...], mid[...]) * inverse[...]
    put_left(lhs, split(part))
    part = dot_t(lhs[...], vl[...])
    put_right(mid, split(part))
    return dot(uk[...], mid[...]).astype(jnp.bfloat16)


def put_lanes(ref, pair):
    n = pair[0].shape[1]
    ref[:, 0:n] = pair[0]
    ref[:, n : 2 * n] = pair[1]
    ref[:, 2 * n : 3 * n] = pair[0]


def set_inverse(inverse, av, bv):
    n = inverse.shape[0]
    alpha = jnp.transpose(jnp.broadcast_to(av[...][None, :], (128, n)))
    beta = bv[...][None, :]
    for c in range(0, n, 128):
        inverse[:, c : c + 128] = 1.0 / (alpha + beta[:, c : c + 128])


def set_right_basis(v, vk, vl):
    pair = split(v[...])
    put_right(vk, pair)
    put_lanes(vl, pair)


def set_left_basis(u, uk, utk):
    high, low = split(u[...])
    put_left(uk, (high, low))
    put_left(utk, (high.T, low.T))


def copies(pairs, sem):
    moves = [pltpu.make_async_copy(source, target, sem.at[n]) for n, (source, target) in enumerate(pairs)]
    for move in moves:
        move.start()
    return moves


def begin(rows_n, first, rhs, u_far, v_far, a_vals, b_vals, f0, s, u, v, av, bv, uk, utk, vk, vl, inverse, lhs, mid, sem):
    @pl.when(level_of(rows_n) == first)
    def _():
        moves = copies(((v_far, v), (rhs, s), (u_far, u), (a_vals, av), (b_vals, bv)), sem)
        moves[0].wait()
        set_right_basis(v, vk, vl)
        for move in moves[1:]:
            move.wait()
        set_left_basis(u, uk, utk)
        set_inverse(inverse, av, bv)
        f0[...] = solve(s[...], uk, utk, vk, vl, inverse, lhs, mid)


def prepare(rows_n, first, rhs, a_c, b_c, u_far, v_far, a_vals, b_vals, uk, utk, vk, vl, inverse, s, ca, cb, u, v, av, bv, sem):
    level = level_of(rows_n)

    @pl.when((level > first) & (level <= first + 2))
    def _():
        moves = copies(((v_far, v), (u_far, u), (a_vals, av), (b_vals, bv), (rhs, s), (a_c.at[0], ca), (b_c.at[0], cb)), sem)
        moves[0].wait()
        set_right_basis(v, vk, vl)
        moves[1].wait()
        set_left_basis(u, uk, utk)
        moves[2].wait()
        moves[3].wait()
        set_inverse(inverse, av, bv)
        for move in moves[4:]:
            move.wait()


def second(rows_n, first, down, left, uk, utk, vk, vl, inverse, s, ca, cb, f1, lhs, mid):
    @pl.when(level_of(rows_n) == first + 1)
    def _():
        state = s[...] - (dot(ca[...], down[...]) + dot(left[...], cb[...]))
        f1[...] = solve(state, uk, utk, vk, vl, inverse, lhs, mid)


def third_early(rows_n, first, rhs, a_c, b_c, down, direct, on_chip, s1, a1, b1, a0, b0, sem):
    even = lax.rem(lax.axis_index("col"), 2) == 0

    @pl.when(level_of(rows_n) == first + 2)
    def _():
        moves = copies(((rhs, s1), (a_c.at[0], a0), (b_c.at[0], b0), (a_c.at[1], a1), (b_c.at[1], b1)), sem)
        for move in moves:
            move.wait()
        left = jnp.where(even, direct[...], on_chip[...])
        s1[...] -= dot(a0[...], down[...]) + dot(left, b0[...])


def third(rows_n, first, down, left, uk, utk, vk, vl, inverse, s1, a1, b1, f2, lhs, mid):
    @pl.when(level_of(rows_n) == first + 2)
    def _():
        state = s1[...] - (dot(a1[...], down[...]) + dot(left[...], b1[...]))
        f2[...] = solve(state, uk, utk, vk, vl, inverse, lhs, mid)


def subtract(cols_n, ops, arrived, got, state, coup_a, coup_b, out, kinds=("down", "left")):
    out[...] = state[...]
    for kind in kinds:
        hits = pick(cols_n, ops, kind, arrived, got)

        @pl.when(hits)
        def _():
            out[...] -= dot(got[...], coup_b[...]) if kind == "left" else dot(coup_a[...], got[...])


def middle(rows_n, cols_n, first, ops, rhs, a_c, b_c, *rest):
    arrived, (s1, a1, b1, a2, b2, s, a0, b0, got, sem) = rest[: len(ops)], rest[len(ops) :]

    @pl.when(level_of(rows_n) > first + 2)
    def _():
        pairs = ((rhs, s), (a_c.at[0], a0), (b_c.at[0], b0), (a_c.at[1], a1), (b_c.at[1], b1), (a_c.at[2], a2), (b_c.at[2], b2))
        for move in copies(pairs, sem):
            move.wait()
        subtract(cols_n, ops, arrived, got, s, a0, b0, s1)


def middle_late(rows_n, cols_n, first, ops, s1, a1, b1, *rest):
    arrived, (s2, got) = rest[: len(ops)], rest[len(ops) :]

    @pl.when(level_of(rows_n) > first + 2)
    def _():
        subtract(cols_n, ops, arrived, got, s1, a1, b1, s2)


def pick(cols_n, ops, kind, arrived, got):
    me = place(cols_n)
    any_hit = me < 0
    for op, ref in zip(ops, arrived):
        hit = one_of(me, [t[0] * cols_n + t[1] for _, t, k, _ in op if k == kind])
        any_hit = any_hit | hit

        @pl.when(hit)
        def _():
            got[...] = ref[...]

    return any_hit


def downs(cols_n, first, rows_n, ops, s2, a2, *rest):
    arrived, (s3, got) = rest[: len(ops)], rest[len(ops) :]

    @pl.when(level_of(rows_n) > first + 2)
    def _():
        subtract(cols_n, ops, arrived, got, s2, a2, None, s3, ("down",))


def finish(rows_n, cols_n, first, ops, f0, f1, f2, s3, b2, *rest):
    arrived, (out, nxt, got, mine, zeros, sem) = rest[: len(ops)], rest[len(ops) :]
    level = level_of(rows_n)
    n = s3.shape[0]
    step = n // 3
    active = level > first + 2
    for t, block in enumerate((f0, f1, f2)):

        @pl.when(level == first + t)
        def _():
            pltpu.make_async_copy(block, out, sem.at[3]).start()

    @pl.when((level < first) | active)
    def _():
        zeros[...] = jnp.zeros(zeros.shape, zeros.dtype)
        pltpu.make_async_copy(zeros, out, sem.at[3]).start()

    @pl.when(jnp.logical_not(active))
    def _():
        mine[...] = jnp.zeros(mine.shape, mine.dtype)
        for k in range(3):
            pltpu.make_async_copy(mine.at[pl.ds(k * step, step)], nxt.at[pl.ds(k * step, step)], sem.at[k]).start()

    @pl.when(active)
    def _():
        pick(cols_n, ops, "left", arrived, got)
        for k in range(3):
            rows = pl.ds(k * step, step)
            mine[rows] = s3[rows] - dot(got[rows], b2[...])
            pltpu.make_async_copy(mine.at[rows], nxt.at[rows], sem.at[k]).start()

    for k in range(3):
        pltpu.make_async_copy(mine.at[pl.ds(k * step, step)], nxt.at[pl.ds(k * step, step)], sem.at[k]).wait()
    pltpu.make_async_copy(zeros, out, sem.at[3]).wait()


def relay(cols_n, choices, own, *rest):
    *arrived, out = rest
    me = place(cols_n)
    hit = me < 0
    for ids, ref in zip(choices, arrived):
        mine = one_of(me, ids)
        hit = hit | mine

        @pl.when(mine)
        def _():
            out[...] = ref[...]

    @pl.when(jnp.logical_not(hit))
    def _():
        out[...] = own[...]


def spread(ops, cols_n, own, name, call):
    arrived = []
    for k, op in enumerate(ops):
        value = own
        earlier = sorted({f for *_, f in op if f is not None})
        if earlier:
            choices = [[s[0] * cols_n + s[1] for s, _, _, f in op if f == e] for e in earlier]
            (value,) = call(
                functools.partial(relay, cols_n, choices),
                [],
                [own, *[arrived[e] for e in earlier]],
                [jax.ShapeDtypeStruct(own.shape, own.dtype)],
                [],
                f"relay_{name}{k}",
            )
        pairs = [(s[0] * cols_n + s[1], t[0] * cols_n + t[1]) for s, t, _, _ in op]
        arrived.append(move(value, pairs))
    return arrived


def move(value, pairs):
    return lax.ppermute(value, AXES, pairs)


def solution(mesh):
    rows_n, cols_n = mesh.shape["row"], mesh.shape["col"]
    first = (rows_n + cols_n) // 2 - 2
    offset = first - rows_n + 1
    ops0 = plan(rows_n, cols_n, offset, 3, 3)
    ops1 = plan(rows_n, cols_n, offset + 1, 2, 2)
    ops2 = plan(rows_n, cols_n, offset + 2, 1, 1)

    def owners(t):
        return [(i, i + offset + t) for i in range(rows_n) if 0 <= i + offset + t < cols_n]

    def up(t, far):
        return [(i * cols_n + j, (i - far) * cols_n + j) for i, j in owners(t) if i >= far]

    def right(t, far):
        return [(i * cols_n + j, i * cols_n + j + far) for i, j in owners(t) if j + far < cols_n]

    def shards(rhs, a_c, b_c, u, v, a_vals, b_vals):
        n = rhs.shape[0]
        half, full = jnp.bfloat16, jnp.float32
        square = jax.ShapeDtypeStruct((n, n), half)
        wide, tall = jax.ShapeDtypeStruct((n, 3 * n), half), jax.ShapeDtypeStruct((3 * n, n), half)
        state = jax.ShapeDtypeStruct((n, n), full)
        loads = [pltpu.VMEM((n, n), full)] * 3 + [pltpu.VMEM((n,), full)] * 2
        basis_work = [pltpu.VMEM((n, 3 * n), half)] * 2 + [pltpu.VMEM((3 * n, n), half), pltpu.VMEM((n, 3 * n), half), pltpu.VMEM((n, n), full)]
        work = [pltpu.VMEM((n, 3 * n), half), pltpu.VMEM((3 * n, n), half)]

        def call(kernel, far, near, outs, scratch, name):
            ins = [pltpu.with_memory_space_constraint(x, pltpu.HBM) for x in far] + list(near)
            return pl.pallas_call(
                kernel,
                out_shape=outs,
                in_specs=[FAR_SPEC] * len(far) + [VMEM_SPEC] * len(near),
                out_specs=[FAR_SPEC if name == "finish" else VMEM_SPEC] * len(outs),
                scratch_shapes=scratch,
                compiler_params=pltpu.CompilerParams(vmem_limit_bytes=24 << 20),
            )(*ins)

        basis_shapes = [wide, wide, tall, wide, state]
        (f0,) = call(
            functools.partial(begin, rows_n, first),
            [rhs, u, v, a_vals, b_vals],
            [],
            [square],
            loads + basis_work + work + [pltpu.SemaphoreType.DMA((5,))],
            "begin",
        )
        down = move(f0, up(0, 1))
        left = move(f0, right(0, 1))
        down_far = move(f0, up(0, 2))
        direct, on_chip = [], []
        for i, j in owners(0):
            if j + 2 < cols_n:
                source, target = (j, direct) if j % 2 == 0 else (j + 1, on_chip)
                target.append((i * cols_n + source, i * cols_n + j + 2))
        left_far = [move(f0, direct), move(left, on_chip)]
        far0 = spread(ops0, cols_n, f0, "a", call)
        *basis, s, ca, cb = call(
            functools.partial(prepare, rows_n, first),
            [rhs, a_c, b_c, u, v, a_vals, b_vals],
            [],
            basis_shapes + [state, square, square],
            loads[1:] + [pltpu.SemaphoreType.DMA((7,))],
            "prepare",
        )
        (f1,) = call(
            functools.partial(second, rows_n, first),
            [],
            [down, left, *basis, s, ca, cb],
            [square],
            work,
            "second",
        )
        down = move(f1, up(1, 1))
        left = move(f1, right(1, 1))
        s1, a1, b1 = call(
            functools.partial(third_early, rows_n, first),
            [rhs, a_c, b_c],
            [down_far, *left_far],
            [state, square, square],
            [pltpu.VMEM((n, n), half)] * 2 + [pltpu.SemaphoreType.DMA((5,))],
            "third_early",
        )
        far1 = spread(ops1, cols_n, f1, "b", call)
        (f2,) = call(
            functools.partial(third, rows_n, first),
            [],
            [down, left, *basis, s1, a1, b1],
            [square],
            work,
            "third",
        )
        s1, a1, b1, a2, b2 = call(
            functools.partial(middle, rows_n, cols_n, first, ops0),
            [rhs, a_c, b_c],
            far0,
            [state] + [square] * 4,
            [pltpu.VMEM((n, n), full)] + [pltpu.VMEM((n, n), half)] * 3 + [pltpu.SemaphoreType.DMA((7,))],
            "middle",
        )
        (s2,) = call(
            functools.partial(middle_late, rows_n, cols_n, first, ops1),
            [],
            [s1, a1, b1, *far1],
            [state],
            [pltpu.VMEM((n, n), half)],
            "middle_late",
        )
        lasts = spread(ops2, cols_n, f2, "c", call)
        sent = [k for k, op in enumerate(ops2) if any(kind == "down" for _, _, kind, _ in op)]
        (s3,) = call(
            functools.partial(downs, cols_n, first, rows_n, [ops2[k] for k in sent]),
            [],
            [s2, a2, *[lasts[k] for k in sent]],
            [state],
            [pltpu.VMEM((n, n), half)],
            "downs",
        )
        return call(
            functools.partial(finish, rows_n, cols_n, first, ops2),
            [],
            [f0, f1, f2, s3, b2, *lasts],
            [square, state],
            [pltpu.VMEM((n, n), half), pltpu.VMEM((n, n), full), pltpu.VMEM((n, n), half), pltpu.SemaphoreType.DMA((4,))],
            "finish",
        )

    placed = (
        P("row", "col"),
        P(None, "row", "col"),
        P(None, "row", "col"),
        P("row", None),
        P("col", None),
        P("row"),
        P("col"),
    )
    return jax.shard_map(
        shards,
        mesh=mesh,
        in_specs=placed,
        out_specs=(P("row", "col"), P("row", "col")),
        check_vma=False,
    )
```

profile of v0, /device:TPU:24, one launch (start us, length us, event | category | flops | bytes accessed | tf_op | source)
XLA Modules:
  0.0 43.2 jit_solution(3834771799313088157)
XLA Ops:
  0.7 0.7 %collective-permute-start.1 = (bf16[384,384]{1,0:T(8,128)(2,1)S(1)}, bf16[384,384]{1,0:T(8,128)(2,1)S(1)}, u32[]{:S(2)}, u32[]{:S(2)}) collective-permute-start(bf16[384,384]{1,0:T(8,128)(2,1)S(1)} %shard_map.86.own.f0), channel_id=1, source_target_pairs={{1,2},{10,11},{19,20},{28,29}} | collective-permute-start | bytes 884744 | tf_op jit(solution)/shard_map/ppermute | solution.py:320
  1.4 0.7 %collective-permute-start = (bf16[384,384]{1,0:T(8,128)(2,1)S(1)}, bf16[384,384]{1,0:T(8,128)(2,1)S(1)}, u32[]{:S(2)}, u32[]{:S(2)}) collective-permute-start(bf16[384,384]{1,0:T(8,128)(2,1)S(1)} %shard_map.86.own.f0), channel_id=1, source_target_pairs={{10,2},{19,11},{28,20}} | collective-permute-start | bytes 884744 | tf_op jit(solution)/shard_map/ppermute | solution.py:320
  2.1 0.7 %collective-permute-start.4 = (bf16[384,384]{1,0:T(8,128)(2,1)S(1)}, bf16[384,384]{1,0:T(8,128)(2,1)S(1)}, u32[]{:S(2)}, u32[]{:S(2)}) collective-permute-start(bf16[384,384]{1,0:T(8,128)(2,1)S(1)} %shard_map.86.own.f0), channel_id=1, source_target_pairs={{19,3},{28,12}} | collective-permute-start | bytes 884744 | tf_op jit(solution)/shard_map/ppermute | solution.py:320
  2.8 0.7 %collective-permute-start.5 = (bf16[384,384]{1,0:T(8,128)(2,1)S(1)}, bf16[384,384]{1,0:T(8,128)(2,1)S(1)}, u32[]{:S(2)}, u32[]{:S(2)}) collective-permute-start(bf16[384,384]{1,0:T(8,128)(2,1)S(1)} %shard_map.86.own.f0), channel_id=1, source_target_pairs={{10,12},{28,30}} | collective-permute-start | bytes 884744 | tf_op jit(solution)/shard_map/ppermute | solution.py:320
  3.6 0.7 %collective-permute-start.6 = (bf16[384,384]{1,0:T(8,128)(2,1)S(1)}, bf16[384,384]{1,0:T(8,128)(2,1)S(1)}, u32[]{:S(2)}, u32[]{:S(2)}) collective-permute-start(bf16[384,384]{1,0:T(8,128)(2,1)S(1)} %collective-permute-done.1.left), channel_id=1, source_target_pairs={{2,3},{20,21}} | collective-permute-start | bytes 884744 | tf_op jit(solution)/shard_map/ppermute | solution.py:320
  4.3 0.7 %collective-permute-start.2 = (bf16[384,384]{1,0:T(8,128)(2,1)S(1)}, bf16[384,384]{1,0:T(8,128)(2,1)S(1)}, u32[]{:S(2)}, u32[]{:S(2)}) collective-permute-start(bf16[384,384]{1,0:T(8,128)(2,1)S(1)} %shard_map.88.own.f1), channel_id=1, source_target_pairs={{11,3},{20,12},{29,21}} | collective-permute-start | bytes 884744 | tf_op jit(solution)/shard_map/ppermute | solution.py:320
  5.0 0.7 %collective-permute-start.3 = (bf16[384,384]{1,0:T(8,128)(2,1)S(1)}, bf16[384,384]{1,0:T(8,128)(2,1)S(1)}, u32[]{:S(2)}, u32[]{:S(2)}) collective-permute-start(bf16[384,384]{1,0:T(8,128)(2,1)S(1)} %shard_map.88.own.f1), channel_id=1, source_target_pairs={{2,3},{11,12},{20,21},{29,30}} | collective-permute-start | bytes 884744 | tf_op jit(solution)/shard_map/ppermute | solution.py:320
  5.7 1.3 %collective-permute-start.7 = (bf16[384,384]{1,0:T(8,128)(2,1)S(1)}, bf16[384,384]{1,0:T(8,128)(2,1)S(1)}, u32[]{:S(2)}, u32[]{:S(2)}) collective-permute-start(bf16[384,384]{1,0:T(8,128)(2,1)S(1)} %shard_map.86.own.f0), channel_id=1, source_target_pairs={{1,6},{10,14},{19,22},{28,31}} | collective-permute-start | bytes 884744 | tf_op jit(solution)/shard_map/ppermute | solution.py:320
  7.0 0.7 %collective-permute-start.8 = (bf16[384,384]{1,0:T(8,128)(2,1)S(1)}, bf16[384,384]{1,0:T(8,128)(2,1)S(1)}, u32[]{:S(2)}, u32[]{:S(2)}) collective-permute-start(bf16[384,384]{1,0:T(8,128)(2,1)S(1)} %shard_map.86.own.f0), channel_id=1, source_target_pairs={{1,5},{10,13},{28,4}} | collective-permute-start | bytes 884744 | tf_op jit(solution)/shard_map/ppermute | solution.py:320
  7.7 1.3 %collective-permute-start.10 = (bf16[384,384]{1,0:T(8,128)(2,1)S(1)}, bf16[384,384]{1,0:T(8,128)(2,1)S(1)}, u32[]{:S(2)}, u32[]{:S(2)}) collective-permute-start(bf16[384,384]{1,0:T(8,128)(2,1)S(1)} %shard_map.88.own.f1), channel_id=1, source_target_pairs={{2,6},{11,14},{20,22},{29,31}} | collective-permute-start | bytes 884744 | tf_op jit(solution)/shard_map/ppermute | solution.py:320
  9.1 0.7 %collective-permute-start.11 = (bf16[384,384]{1,0:T(8,128)(2,1)S(1)}, bf16[384,384]{1,0:T(8,128)(2,1)S(1)}, u32[]{:S(2)}, u32[]{:S(2)}) collective-permute-start(bf16[384,384]{1,0:T(8,128)(2,1)S(1)} %shard_map.88.own.f1), channel_id=1, source_target_pairs={{2,4},{11,13},{29,5}} | collective-permute-start | bytes 884744 | tf_op jit(solution)/shard_map/ppermute | solution.py:320
  9.8 0.7 %collective-permute-start.14 = (bf16[384,384]{1,0:T(8,128)(2,1)S(1)}, bf16[384,384]{1,0:T(8,128)(2,1)S(1)}, u32[]{:S(2)}, u32[]{:S(2)}) collective-permute-start(bf16[384,384]{1,0:T(8,128)(2,1)S(1)} %shard_map.90.own.f2), channel_id=1, source_target_pairs={{3,4},{12,13},{21,5},{30,22}} | collective-permute-start | bytes 884744 | tf_op jit(solution)/shard_map/ppermute | solution.py:320
  10.5 5.7 %collective-permute-done.7.rest_0_ = bf16[384,384]{1,0:T(8,128)(2,1)S(1)} collective-permute-done((bf16[384,384]{1,0:T(8,128)(2,1)S(1)}, bf16[384,384]{1,0:T(8,128)(2,1)S(1)}, u32[]{:S(2)}, u32[]{:S(2)}) %collective-permute-start.7) | collective-permute-done | bytes 294944 | tf_op jit(solution)/shard_map/ppermute | solution.py:320
  16.2 0.7 %collective-permute-start.17 = (bf16[384,384]{1,0:T(8,128)(2,1)S(1)}, bf16[384,384]{1,0:T(8,128)(2,1)S(1)}, u32[]{:S(2)}, u32[]{:S(2)}) collective-permute-start(bf16[384,384]{1,0:T(8,128)(2,1)S(1)} %shard_map.90.own.f2), channel_id=1, source_target_pairs={{3,7},{12,15},{21,23},{30,31}} | collective-permute-start | bytes 884744 | tf_op jit(solution)/shard_map/ppermute | solution.py:320
  16.9 1.3 %collective-permute-start.9 = (bf16[384,384]{1,0:T(8,128)(2,1)S(1)}, bf16[384,384]{1,0:T(8,128)(2,1)S(1)}, u32[]{:S(2)}, u32[]{:S(2)}) collective-permute-start(bf16[384,384]{1,0:T(8,128)(2,1)S(1)} %shard_map.91), channel_id=1, source_target_pairs={{6,7},{14,15},{22,23},{5,4}} | collective-permute-start | bytes 884744 | tf_op jit(solution)/shard_map/ppermute | solution.py:320
  18.3 7.8 %collective-permute-done.10.rest_0_ = bf16[384,384]{1,0:T(8,128)(2,1)S(1)} collective-permute-done((bf16[384,384]{1,0:T(8,128)(2,1)S(1)}, bf16[384,384]{1,0:T(8,128)(2,1)S(1)}, u32[]{:S(2)}, u32[]{:S(2)}) %collective-permute-start.10) | collective-permute-done | bytes 294944 | tf_op jit(solution)/shard_map/ppermute | solution.py:320
  26.1 0.7 %collective-permute-start.12 = (bf16[384,384]{1,0:T(8,128)(2,1)S(1)}, bf16[384,384]{1,0:T(8,128)(2,1)S(1)}, u32[]{:S(2)}, u32[]{:S(2)}) collective-permute-start(bf16[384,384]{1,0:T(8,128)(2,1)S(1)} %shard_map.88.own.f1), channel_id=1, source_target_pairs={{20,4},{29,13}} | collective-permute-start | bytes 884744 | tf_op jit(solution)/shard_map/ppermute | solution.py:320
  26.8 1.3 %collective-permute-start.13 = (bf16[384,384]{1,0:T(8,128)(2,1)S(1)}, bf16[384,384]{1,0:T(8,128)(2,1)S(1)}, u32[]{:S(2)}, u32[]{:S(2)}) collective-permute-start(bf16[384,384]{1,0:T(8,128)(2,1)S(1)} %shard_map.93), channel_id=1, source_target_pairs={{6,7},{14,15},{22,23},{4,5}} | collective-permute-start | bytes 884744 | tf_op jit(solution)/shard_map/ppermute | solution.py:320
  28.2 0.7 %collective-permute-start.15 = (bf16[384,384]{1,0:T(8,128)(2,1)S(1)}, bf16[384,384]{1,0:T(8,128)(2,1)S(1)}, u32[]{:S(2)}, u32[]{:S(2)}) collective-permute-start(bf16[384,384]{1,0:T(8,128)(2,1)S(1)} %shard_map.90.own.f2), channel_id=1, source_target_pairs={{12,4},{21,13},{30,14}} | collective-permute-start | bytes 884744 | tf_op jit(solution)/shard_map/ppermute | solution.py:320
  28.9 1.3 %collective-permute-start.16 = (bf16[384,384]{1,0:T(8,128)(2,1)S(1)}, bf16[384,384]{1,0:T(8,128)(2,1)S(1)}, u32[]{:S(2)}, u32[]{:S(2)}) collective-permute-start(bf16[384,384]{1,0:T(8,128)(2,1)S(1)} %shard_map.90.own.f2), channel_id=1, source_target_pairs={{30,6}} | collective-permute-start | bytes 884744 | tf_op jit(solution)/shard_map/ppermute | solution.py:320
  30.2 1.3 %collective-permute-start.18 = (bf16[384,384]{1,0:T(8,128)(2,1)S(1)}, bf16[384,384]{1,0:T(8,128)(2,1)S(1)}, u32[]{:S(2)}, u32[]{:S(2)}) collective-permute-start(bf16[384,384]{1,0:T(8,128)(2,1)S(1)} %shard_map.96), channel_id=1, source_target_pairs={{7,6},{15,14},{23,22},{4,5}} | collective-permute-start | bytes 884744 | tf_op jit(solution)/shard_map/ppermute | solution.py:320
  31.5 2.1 %shard_map.92 = (f32[384,384]{1,0:T(8,128)S(1)}, bf16[384,384]{1,0:T(8,128)(2,1)S(1)}, bf16[384,384]{1,0:T(8,128)(2,1)S(1)}, bf16[384,384]{1,0:T(8,128)(2,1)S(1)}, bf16[384,384]{1,0:T(8,128)(2,1)S(1)}) custom-call(f32[384,384]{1,0:T(8,128)} %rhs.7, bf16[3,384,384]{2,1,0:T(8,128)(2,1)} %a_c.5, bf16[3,384,384]{2,1,0:T(8,128)(2,1)} %b_c.5, ...), custom_call_target="tpu_custom_call" | custom-call | tf_op jit(solution)/shard_map/pallas_call | solution.py:352
  34.1 7.5 %collective-permute-done.16.rest_2_.rest_3_ = bf16[384,384]{1,0:T(8,128)(2,1)S(1)} collective-permute-done((bf16[384,384]{1,0:T(8,128)(2,1)S(1)}, bf16[384,384]{1,0:T(8,128)(2,1)S(1)}, u32[]{:S(2)}, u32[]{:S(2)}) %collective-permute-start.16) | collective-permute-done | bytes 294944 | tf_op jit(solution)/shard_map/ppermute | solution.py:320
  42.0 1.2 %shard_map.97 = (bf16[384,384]{1,0:T(8,128)(2,1)}, f32[384,384]{1,0:T(8,128)}) custom-call(bf16[384,384]{1,0:T(8,128)(2,1)S(1)} %shard_map.86.own.f0, bf16[384,384]{1,0:T(8,128)(2,1)S(1)} %shard_map.88.own.f1, bf16[384,384]{1,0:T(8,128)(2,1)S(1)} %shard_map.90.own.f2, f32[384,384]{1,0:T(8,128)S(1)} %shard_map.95.s3, ...), custom_call_target="tpu_custom_call" | custom-call | tf_op jit(solution)/shard_map/pallas_call | solution.py:352
  (26 shorter events, 1.3 us)
Async XLA Ops:
  0.7 2.8 %collective-permute-start.1 = (bf16[384,384]{1,0:T(8,128)(2,1)S(1)}, bf16[384,384]{1,0:T(8,128)(2,1)S(1)}, u32[]{:S(2)}, u32[]{:S(2)}) collective-permute-start(bf16[384,384]{1,0:T(8,128)(2,1)S(1)} %shard_map.86.own.f0), channel_id=1, source_target_pairs={{1,2},{10,11},{19,20},{28,29}} | collective-permute-start | bytes 884744 | tf_op jit(solution)/shard_map/ppermute | solution.py:320
  1.4 2.9 %collective-permute-start = (bf16[384,384]{1,0:T(8,128)(2,1)S(1)}, bf16[384,384]{1,0:T(8,128)(2,1)S(1)}, u32[]{:S(2)}, u32[]{:S(2)}) collective-permute-start(bf16[384,384]{1,0:T(8,128)(2,1)S(1)} %shard_map.86.own.f0), channel_id=1, source_target_pairs={{10,2},{19,11},{28,20}} | collective-permute-start | bytes 884744 | tf_op jit(solution)/shard_map/ppermute | solution.py:320
  2.1 3.6 %collective-permute-start.4 = (bf16[384,384]{1,0:T(8,128)(2,1)S(1)}, bf16[384,384]{1,0:T(8,128)(2,1)S(1)}, u32[]{:S(2)}, u32[]{:S(2)}) collective-permute-start(bf16[384,384]{1,0:T(8,128)(2,1)S(1)} %shard_map.86.own.f0), channel_id=1, source_target_pairs={{19,3},{28,12}} | collective-permute-start | bytes 884744 | tf_op jit(solution)/shard_map/ppermute | solution.py:320
  2.8 4.2 %collective-permute-start.5 = (bf16[384,384]{1,0:T(8,128)(2,1)S(1)}, bf16[384,384]{1,0:T(8,128)(2,1)S(1)}, u32[]{:S(2)}, u32[]{:S(2)}) collective-permute-start(bf16[384,384]{1,0:T(8,128)(2,1)S(1)} %shard_map.86.own.f0), channel_id=1, source_target_pairs={{10,12},{28,30}} | collective-permute-start | bytes 884744 | tf_op jit(solution)/shard_map/ppermute | solution.py:320
  3.6 4.1 %collective-permute-start.6 = (bf16[384,384]{1,0:T(8,128)(2,1)S(1)}, bf16[384,384]{1,0:T(8,128)(2,1)S(1)}, u32[]{:S(2)}, u32[]{:S(2)}) collective-permute-start(bf16[384,384]{1,0:T(8,128)(2,1)S(1)} %collective-permute-done.1.left), channel_id=1, source_target_pairs={{2,3},{20,21}} | collective-permute-start | bytes 884744 | tf_op jit(solution)/shard_map/ppermute | solution.py:320
  4.3 4.8 %collective-permute-start.2 = (bf16[384,384]{1,0:T(8,128)(2,1)S(1)}, bf16[384,384]{1,0:T(8,128)(2,1)S(1)}, u32[]{:S(2)}, u32[]{:S(2)}) collective-permute-start(bf16[384,384]{1,0:T(8,128)(2,1)S(1)} %shard_map.88.own.f1), channel_id=1, source_target_pairs={{11,3},{20,12},{29,21}} | collective-permute-start | bytes 884744 | tf_op jit(solution)/shard_map/ppermute | solution.py:320
  5.0 4.8 %collective-permute-start.3 = (bf16[384,384]{1,0:T(8,128)(2,1)S(1)}, bf16[384,384]{1,0:T(8,128)(2,1)S(1)}, u32[]{:S(2)}, u32[]{:S(2)}) collective-permute-start(bf16[384,384]{1,0:T(8,128)(2,1)S(1)} %shard_map.88.own.f1), channel_id=1, source_target_pairs={{2,3},{11,12},{20,21},{29,30}} | collective-permute-start | bytes 884744 | tf_op jit(solution)/shard_map/ppermute | solution.py:320
  5.7 10.5 %collective-permute-start.7 = (bf16[384,384]{1,0:T(8,128)(2,1)S(1)}, bf16[384,384]{1,0:T(8,128)(2,1)S(1)}, u32[]{:S(2)}, u32[]{:S(2)}) collective-permute-start(bf16[384,384]{1,0:T(8,128)(2,1)S(1)} %shard_map.86.own.f0), channel_id=1, source_target_pairs={{1,6},{10,14},{19,22},{28,31}} | collective-permute-start | bytes 884744 | tf_op jit(solution)/shard_map/ppermute | solution.py:320
  7.0 9.9 %collective-permute-start.8 = (bf16[384,384]{1,0:T(8,128)(2,1)S(1)}, bf16[384,384]{1,0:T(8,128)(2,1)S(1)}, u32[]{:S(2)}, u32[]{:S(2)}) collective-permute-start(bf16[384,384]{1,0:T(8,128)(2,1)S(1)} %shard_map.86.own.f0), channel_id=1, source_target_pairs={{1,5},{10,13},{28,4}} | collective-permute-start | bytes 884744 | tf_op jit(solution)/shard_map/ppermute | solution.py:320
  7.7 18.4 %collective-permute-start.10 = (bf16[384,384]{1,0:T(8,128)(2,1)S(1)}, bf16[384,384]{1,0:T(8,128)(2,1)S(1)}, u32[]{:S(2)}, u32[]{:S(2)}) collective-permute-start(bf16[384,384]{1,0:T(8,128)(2,1)S(1)} %shard_map.88.own.f1), channel_id=1, source_target_pairs={{2,6},{11,14},{20,22},{29,31}} | collective-permute-start | bytes 884744 | tf_op jit(solution)/shard_map/ppermute | solution.py:320
  9.1 17.7 %collective-permute-start.11 = (bf16[384,384]{1,0:T(8,128)(2,1)S(1)}, bf16[384,384]{1,0:T(8,128)(2,1)S(1)}, u32[]{:S(2)}, u32[]{:S(2)}) collective-permute-start(bf16[384,384]{1,0:T(8,128)(2,1)S(1)} %shard_map.88.own.f1), channel_id=1, source_target_pairs={{2,4},{11,13},{29,5}} | collective-permute-start | bytes 884744 | tf_op jit(solution)/shard_map/ppermute | solution.py:320
  9.8 18.4 %collective-permute-start.14 = (bf16[384,384]{1,0:T(8,128)(2,1)S(1)}, bf16[384,384]{1,0:T(8,128)(2,1)S(1)}, u32[]{:S(2)}, u32[]{:S(2)}) collective-permute-start(bf16[384,384]{1,0:T(8,128)(2,1)S(1)} %shard_map.90.own.f2), channel_id=1, source_target_pairs={{3,4},{12,13},{21,5},{30,22}} | collective-permute-start | bytes 884744 | tf_op jit(solution)/shard_map/ppermute | solution.py:320
  16.2 12.6 %collective-permute-start.17 = (bf16[384,384]{1,0:T(8,128)(2,1)S(1)}, bf16[384,384]{1,0:T(8,128)(2,1)S(1)}, u32[]{:S(2)}, u32[]{:S(2)}) collective-permute-start(bf16[384,384]{1,0:T(8,128)(2,1)S(1)} %shard_map.90.own.f2), channel_id=1, source_target_pairs={{3,7},{12,15},{21,23},{30,31}} | collective-permute-start | bytes 884744 | tf_op jit(solution)/shard_map/ppermute | solution.py:320
  16.9 13.3 %collective-permute-start.9 = (bf16[384,384]{1,0:T(8,128)(2,1)S(1)}, bf16[384,384]{1,0:T(8,128)(2,1)S(1)}, u32[]{:S(2)}, u32[]{:S(2)}) collective-permute-start(bf16[384,384]{1,0:T(8,128)(2,1)S(1)} %shard_map.91), channel_id=1, source_target_pairs={{6,7},{14,15},{22,23},{5,4}} | collective-permute-start | bytes 884744 | tf_op jit(solution)/shard_map/ppermute | solution.py:320
  26.1 7.5 %collective-permute-start.12 = (bf16[384,384]{1,0:T(8,128)(2,1)S(1)}, bf16[384,384]{1,0:T(8,128)(2,1)S(1)}, u32[]{:S(2)}, u32[]{:S(2)}) collective-permute-start(bf16[384,384]{1,0:T(8,128)(2,1)S(1)} %shard_map.88.own.f1), channel_id=1, source_target_pairs={{20,4},{29,13}} | collective-permute-start | bytes 884744 | tf_op jit(solution)/shard_map/ppermute | solution.py:320
  26.8 6.8 %collective-permute-start.13 = (bf16[384,384]{1,0:T(8,128)(2,1)S(1)}, bf16[384,384]{1,0:T(8,128)(2,1)S(1)}, u32[]{:S(2)}, u32[]{:S(2)}) collective-permute-start(bf16[384,384]{1,0:T(8,128)(2,1)S(1)} %shard_map.93), channel_id=1, source_target_pairs={{6,7},{14,15},{22,23},{4,5}} | collective-permute-start | bytes 884744 | tf_op jit(solution)/shard_map/ppermute | solution.py:320
  28.2 5.9 %collective-permute-start.15 = (bf16[384,384]{1,0:T(8,128)(2,1)S(1)}, bf16[384,384]{1,0:T(8,128)(2,1)S(1)}, u32[]{:S(2)}, u32[]{:S(2)}) collective-permute-start(bf16[384,384]{1,0:T(8,128)(2,1)S(1)} %shard_map.90.own.f2), channel_id=1, source_target_pairs={{12,4},{21,13},{30,14}} | collective-permute-start | bytes 884744 | tf_op jit(solution)/shard_map/ppermute | solution.py:320
  28.9 12.7 %collective-permute-start.16 = (bf16[384,384]{1,0:T(8,128)(2,1)S(1)}, bf16[384,384]{1,0:T(8,128)(2,1)S(1)}, u32[]{:S(2)}, u32[]{:S(2)}) collective-permute-start(bf16[384,384]{1,0:T(8,128)(2,1)S(1)} %shard_map.90.own.f2), channel_id=1, source_target_pairs={{30,6}} | collective-permute-start | bytes 884744 | tf_op jit(solution)/shard_map/ppermute | solution.py:320
  30.2 11.8 %collective-permute-start.18 = (bf16[384,384]{1,0:T(8,128)(2,1)S(1)}, bf16[384,384]{1,0:T(8,128)(2,1)S(1)}, u32[]{:S(2)}, u32[]{:S(2)}) collective-permute-start(bf16[384,384]{1,0:T(8,128)(2,1)S(1)} %shard_map.96), channel_id=1, source_target_pairs={{7,6},{15,14},{23,22},{4,5}} | collective-permute-start | bytes 884744 | tf_op jit(solution)/shard_map/ppermute | solution.py:320
where the time goes:
time: 43.5 us; the launch traced here: 43.2 us
  waiting for transfers between devices  21.1 us (49%)
  starting transfers between devices  16.6 us (38%)
  Pallas kernels  4.5 us (10%)
  between operations  0.99 us (2%)
    ppermute x19, waiting for transfers between devices, move(): return lax.ppermute(value, AXES, pairs)  21.1 us
    ppermute x19, starting transfers between devices, move(): return lax.ppermute(value, AXES, pairs)  16.6 us
    pallas_call x12, Pallas kernels, call(): pl.pallas_call(kernel, out_shape=outs, in_specs=[FAR_SPEC] * len(far) + [...  4.5 us
  transfers between devices with their start and end apart: 19, of which 3 were waited for; matrix products, arithmetic and copies ran while one was open for 0% of the time, Pallas kernels for 8%

commit v1 on v0

--- a/solution.py
+++ b/solution.py
@@ -14,37 +14,30 @@
 
 
 def plan(rows_n, cols_n, offset, gap, up_gap):
-    rights, ups = [], []
+    rights, ups, last = [], [], []
     for i in range(rows_n):
         m = i + offset
         if 0 <= m < cols_n:
             targets = range(m + gap, cols_n)
             for chip in sorted({j // 2 for j in targets}, reverse=True):
-                rights.append(((i, m), [(i, j) for j in targets if j // 2 == chip]))
-            ups += [((i, m), (k, m)) for k in range(i - up_gap, -1, -1)]
+                some = [(i, j) for j in targets if j // 2 == chip]
+                (last if chip == m // 2 else rights).append(((i, m), some, "left"))
+            ups += [((i, m), [(k, m)], "down") for k in range(i - up_gap + 1)]
+    todo = rights + ups + last
     ops, forwards = [], []
-    while rights or ups:
+    while todo:
         used_from, used_to, op = set(), set(), []
-
-        def take(source, target, kind):
-            if source in used_from or target in used_to:
-                return False
-            used_from.add(source)
-            used_to.add(target)
-            op.append((source, target, kind, None))
-            return True
-
-        for item in list(rights):
-            source, targets = item
-            waiting = [t for _, t in ups]
+        waiting = {targets[0] for _, targets, kind in todo if kind == "down"}
+        for item in list(todo):
+            source, targets, kind = item
             for target in sorted(targets, key=lambda t: t in waiting):
-                if take(source, target, "left"):
-                    rights.remove(item)
-                    forwards += [(target, other, "left", len(ops)) for other in targets if other != target]
+                if source not in used_from and target not in used_to:
+                    used_from.add(source)
+                    used_to.add(target)
+                    op.append((source, target, kind, None))
+                    todo.remove(item)
+                    forwards += [(target, other, kind, len(ops)) for other in targets if other != target]
                     break
-        for item in list(ups):
-            if take(*item, "down"):
-                ups.remove(item)
         ops.append(op)
     return ops + [forwards] if forwards else ops
 
@@ -149,12 +142,12 @@
         f0[...] = solve(s[...], uk, utk, vk, vl, inverse, lhs, mid)
 
 
-def prepare(rows_n, first, rhs, a_c, b_c, u_far, v_far, a_vals, b_vals, uk, utk, vk, vl, inverse, s, ca, cb, u, v, av, bv, sem):
+def prepare(rows_n, first, rhs, a_c, b_c, u_far, v_far, a_vals, b_vals, uk, utk, vk, vl, inverse, s, a0, b0, a1, b1, u, v, av, bv, sem):
     level = level_of(rows_n)
 
     @pl.when((level > first) & (level <= first + 2))
     def _():
-        moves = copies(((v_far, v), (u_far, u), (a_vals, av), (b_vals, bv), (rhs, s), (a_c.at[0], ca), (b_c.at[0], cb)), sem)
+        moves = copies(((v_far, v), (u_far, u), (a_vals, av), (b_vals, bv), (rhs, s), (a_c.at[0], a0), (b_c.at[0], b0), (a_c.at[1], a1), (b_c.at[1], b1)), sem)
         moves[0].wait()
         set_right_basis(v, vk, vl)
         moves[1].wait()
@@ -173,16 +166,13 @@
         f1[...] = solve(state, uk, utk, vk, vl, inverse, lhs, mid)
 
 
-def third_early(rows_n, first, rhs, a_c, b_c, down, direct, on_chip, s1, a1, b1, a0, b0, sem):
+def third_early(rows_n, first, down, direct, on_chip, s, a0, b0, s1):
     even = lax.rem(lax.axis_index("col"), 2) == 0
 
     @pl.when(level_of(rows_n) == first + 2)
     def _():
-        moves = copies(((rhs, s1), (a_c.at[0], a0), (b_c.at[0], b0), (a_c.at[1], a1), (b_c.at[1], b1)), sem)
-        for move in moves:
-            move.wait()
         left = jnp.where(even, direct[...], on_chip[...])
-        s1[...] -= dot(a0[...], down[...]) + dot(left, b0[...])
+        s1[...] = s[...] - (dot(a0[...], down[...]) + dot(left, b0[...]))
 
 
 def third(rows_n, first, down, left, uk, utk, vk, vl, inverse, s1, a1, b1, f2, lhs, mid):
@@ -377,30 +367,30 @@
                 target.append((i * cols_n + source, i * cols_n + j + 2))
         left_far = [move(f0, direct), move(left, on_chip)]
         far0 = spread(ops0, cols_n, f0, "a", call)
-        *basis, s, ca, cb = call(
+        *basis, s, a0, b0, a1, b1 = call(
             functools.partial(prepare, rows_n, first),
             [rhs, a_c, b_c, u, v, a_vals, b_vals],
             [],
-            basis_shapes + [state, square, square],
-            loads[1:] + [pltpu.SemaphoreType.DMA((7,))],
+            basis_shapes + [state] + [square] * 4,
+            loads[1:] + [pltpu.SemaphoreType.DMA((9,))],
             "prepare",
         )
         (f1,) = call(
             functools.partial(second, rows_n, first),
             [],
-            [down, left, *basis, s, ca, cb],
+            [down, left, *basis, s, a0, b0],
             [square],
             work,
             "second",
         )
         down = move(f1, up(1, 1))
         left = move(f1, right(1, 1))
-        s1, a1, b1 = call(
+        (s1,) = call(
             functools.partial(third_early, rows_n, first),
-            [rhs, a_c, b_c],
-            [down_far, *left_far],
-            [state, square, square],
-            [pltpu.VMEM((n, n), half)] * 2 + [pltpu.SemaphoreType.DMA((5,))],
+            [],
+            [down_far, *left_far, s, a0, b0],
+            [state],
+            [],
             "third_early",
         )
         far1 = spread(ops1, cols_n, f1, "b", call)

time: 43.5 us -> 43.4 us (level)
  the two profiles are of different devices: /device:TPU:24 before, /device:TPU:16 now
where the time goes in v1:
time: 43.4 us; the launch traced here: 43.1 us
  waiting for transfers between devices  19.1 us (44%)
  starting transfers between devices  17.8 us (41%)
  Pallas kernels  5.13 us (12%)
  between operations  0.98 us (2%)
    ppermute x19, waiting for transfers between devices, move(): return lax.ppermute(value, AXES, pairs)  19.1 us
    ppermute x19, starting transfers between devices, move(): return lax.ppermute(value, AXES, pairs)  17.8 us
    pallas_call x12, Pallas kernels, call(): pl.pallas_call(kernel, out_shape=outs, in_specs=[FAR_SPEC] * len(far) + [...  5.13 us
  transfers between devices with their start and end apart: 19, of which 4 were waited for; matrix products, arithmetic and copies ran while one was open for 0% of the time, Pallas kernels for 9%

profile of v1, /device:TPU:16, one launch (start us, length us, event | category | flops | bytes accessed | tf_op | source)
XLA Modules:
  0.0 43.1 jit_solution(1173512558070936467)
XLA Ops:
  0.7 0.7 %collective-permute-start.1 = (bf16[384,384]{1,0:T(8,128)(2,1)S(1)}, bf16[384,384]{1,0:T(8,128)(2,1)S(1)}, u32[]{:S(2)}, u32[]{:S(2)}) collective-permute-start(bf16[384,384]{1,0:T(8,128)(2,1)S(1)} %shard_map.86.own.f0), channel_id=1, source_target_pairs={{1,2},{10,11},{19,20},{28,29}} | collective-permute-start | bytes 884744 | tf_op jit(solution)/shard_map/ppermute | solution.py:310
  1.4 0.7 %collective-permute-start = (bf16[384,384]{1,0:T(8,128)(2,1)S(1)}, bf16[384,384]{1,0:T(8,128)(2,1)S(1)}, u32[]{:S(2)}, u32[]{:S(2)}) collective-permute-start(bf16[384,384]{1,0:T(8,128)(2,1)S(1)} %shard_map.86.own.f0), channel_id=1, source_target_pairs={{10,2},{19,11},{28,20}} | collective-permute-start | bytes 884744 | tf_op jit(solution)/shard_map/ppermute | solution.py:310
  2.1 0.7 %collective-permute-start.4 = (bf16[384,384]{1,0:T(8,128)(2,1)S(1)}, bf16[384,384]{1,0:T(8,128)(2,1)S(1)}, u32[]{:S(2)}, u32[]{:S(2)}) collective-permute-start(bf16[384,384]{1,0:T(8,128)(2,1)S(1)} %shard_map.86.own.f0), channel_id=1, source_target_pairs={{19,3},{28,12}} | collective-permute-start | bytes 884744 | tf_op jit(solution)/shard_map/ppermute | solution.py:310
  2.8 0.7 %collective-permute-start.5 = (bf16[384,384]{1,0:T(8,128)(2,1)S(1)}, bf16[384,384]{1,0:T(8,128)(2,1)S(1)}, u32[]{:S(2)}, u32[]{:S(2)}) collective-permute-start(bf16[384,384]{1,0:T(8,128)(2,1)S(1)} %shard_map.86.own.f0), channel_id=1, source_target_pairs={{10,12},{28,30}} | collective-permute-start | bytes 884744 | tf_op jit(solution)/shard_map/ppermute | solution.py:310
  3.6 0.7 %collective-permute-start.6 = (bf16[384,384]{1,0:T(8,128)(2,1)S(1)}, bf16[384,384]{1,0:T(8,128)(2,1)S(1)}, u32[]{:S(2)}, u32[]{:S(2)}) collective-permute-start(bf16[384,384]{1,0:T(8,128)(2,1)S(1)} %collective-permute-done.1.left), channel_id=1, source_target_pairs={{2,3},{20,21}} | collective-permute-start | bytes 884744 | tf_op jit(solution)/shard_map/ppermute | solution.py:310
  4.3 0.7 %collective-permute-start.2 = (bf16[384,384]{1,0:T(8,128)(2,1)S(1)}, bf16[384,384]{1,0:T(8,128)(2,1)S(1)}, u32[]{:S(2)}, u32[]{:S(2)}) collective-permute-start(bf16[384,384]{1,0:T(8,128)(2,1)S(1)} %shard_map.88.own.f1), channel_id=1, source_target_pairs={{11,3},{20,12},{29,21}} | collective-permute-start | bytes 884744 | tf_op jit(solution)/shard_map/ppermute | solution.py:310
  5.0 0.7 %collective-permute-start.3 = (bf16[384,384]{1,0:T(8,128)(2,1)S(1)}, bf16[384,384]{1,0:T(8,128)(2,1)S(1)}, u32[]{:S(2)}, u32[]{:S(2)}) collective-permute-start(bf16[384,384]{1,0:T(8,128)(2,1)S(1)} %shard_map.88.own.f1), channel_id=1, source_target_pairs={{2,3},{11,12},{20,21},{29,30}} | collective-permute-start | bytes 884744 | tf_op jit(solution)/shard_map/ppermute | solution.py:310
  5.7 0.7 %collective-permute-start.7 = (bf16[384,384]{1,0:T(8,128)(2,1)S(1)}, bf16[384,384]{1,0:T(8,128)(2,1)S(1)}, u32[]{:S(2)}, u32[]{:S(2)}) collective-permute-start(bf16[384,384]{1,0:T(8,128)(2,1)S(1)} %shard_map.86.own.f0), channel_id=1, source_target_pairs={{1,6},{10,14},{19,22},{28,31}} | collective-permute-start | bytes 884744 | tf_op jit(solution)/shard_map/ppermute | solution.py:310
  6.4 1.3 %collective-permute-start.8 = (bf16[384,384]{1,0:T(8,128)(2,1)S(1)}, bf16[384,384]{1,0:T(8,128)(2,1)S(1)}, u32[]{:S(2)}, u32[]{:S(2)}) collective-permute-start(bf16[384,384]{1,0:T(8,128)(2,1)S(1)} %shard_map.86.own.f0), channel_id=1, source_target_pairs={{1,5},{10,13},{28,4}} | collective-permute-start | bytes 884744 | tf_op jit(solution)/shard_map/ppermute | solution.py:310
  7.7 0.7 %collective-permute-start.10 = (bf16[384,384]{1,0:T(8,128)(2,1)S(1)}, bf16[384,384]{1,0:T(8,128)(2,1)S(1)}, u32[]{:S(2)}, u32[]{:S(2)}) collective-permute-start(bf16[384,384]{1,0:T(8,128)(2,1)S(1)} %shard_map.88.own.f1), channel_id=1, source_target_pairs={{2,6},{11,14},{20,22},{29,31}} | collective-permute-start | bytes 884744 | tf_op jit(solution)/shard_map/ppermute | solution.py:310
  8.4 1.3 %collective-permute-start.11 = (bf16[384,384]{1,0:T(8,128)(2,1)S(1)}, bf16[384,384]{1,0:T(8,128)(2,1)S(1)}, u32[]{:S(2)}, u32[]{:S(2)}) collective-permute-start(bf16[384,384]{1,0:T(8,128)(2,1)S(1)} %shard_map.88.own.f1), channel_id=1, source_target_pairs={{2,4},{11,13},{29,5}} | collective-permute-start | bytes 884744 | tf_op jit(solution)/shard_map/ppermute | solution.py:310
  9.8 0.7 %collective-permute-start.14 = (bf16[384,384]{1,0:T(8,128)(2,1)S(1)}, bf16[384,384]{1,0:T(8,128)(2,1)S(1)}, u32[]{:S(2)}, u32[]{:S(2)}) collective-permute-start(bf16[384,384]{1,0:T(8,128)(2,1)S(1)} %shard_map.90.own.f2), channel_id=1, source_target_pairs={{3,7},{12,15},{21,23},{30,6}} | collective-permute-start | bytes 884744 | tf_op jit(solution)/shard_map/ppermute | solution.py:310
  10.5 1.3 %collective-permute-start.15 = (bf16[384,384]{1,0:T(8,128)(2,1)S(1)}, bf16[384,384]{1,0:T(8,128)(2,1)S(1)}, u32[]{:S(2)}, u32[]{:S(2)}) collective-permute-start(bf16[384,384]{1,0:T(8,128)(2,1)S(1)} %shard_map.90.own.f2), channel_id=1, source_target_pairs={{3,4},{21,5},{30,14},{12,13}} | collective-permute-start | bytes 884744 | tf_op jit(solution)/shard_map/ppermute | solution.py:310
  11.8 12.3 %collective-permute-done.8.rest_1_ = bf16[384,384]{1,0:T(8,128)(2,1)S(1)} collective-permute-done((bf16[384,384]{1,0:T(8,128)(2,1)S(1)}, bf16[384,384]{1,0:T(8,128)(2,1)S(1)}, u32[]{:S(2)}, u32[]{:S(2)}) %collective-permute-start.8) | collective-permute-done | bytes 294944 | tf_op jit(solution)/shard_map/ppermute | solution.py:310
  24.1 1.3 %collective-permute-start.9 = (bf16[384,384]{1,0:T(8,128)(2,1)S(1)}, bf16[384,384]{1,0:T(8,128)(2,1)S(1)}, u32[]{:S(2)}, u32[]{:S(2)}) collective-permute-start(bf16[384,384]{1,0:T(8,128)(2,1)S(1)} %shard_map.91), channel_id=1, source_target_pairs={{6,7},{14,15},{22,23},{5,4}} | collective-permute-start | bytes 884744 | tf_op jit(solution)/shard_map/ppermute | solution.py:310
  25.4 1.3 %collective-permute-start.12 = (bf16[384,384]{1,0:T(8,128)(2,1)S(1)}, bf16[384,384]{1,0:T(8,128)(2,1)S(1)}, u32[]{:S(2)}, u32[]{:S(2)}) collective-permute-start(bf16[384,384]{1,0:T(8,128)(2,1)S(1)} %shard_map.88.own.f1), channel_id=1, source_target_pairs={{20,4},{29,13}} | collective-permute-start | bytes 884744 | tf_op jit(solution)/shard_map/ppermute | solution.py:310
  26.7 3.8 %collective-permute-done.11.rest_1_ = bf16[384,384]{1,0:T(8,128)(2,1)S(1)} collective-permute-done((bf16[384,384]{1,0:T(8,128)(2,1)S(1)}, bf16[384,384]{1,0:T(8,128)(2,1)S(1)}, u32[]{:S(2)}, u32[]{:S(2)}) %collective-permute-start.11) | collective-permute-done | bytes 294944 | tf_op jit(solution)/shard_map/ppermute | solution.py:310
  30.6 1.3 %collective-permute-start.13 = (bf16[384,384]{1,0:T(8,128)(2,1)S(1)}, bf16[384,384]{1,0:T(8,128)(2,1)S(1)}, u32[]{:S(2)}, u32[]{:S(2)}) collective-permute-start(bf16[384,384]{1,0:T(8,128)(2,1)S(1)} %shard_map.93), channel_id=1, source_target_pairs={{6,7},{14,15},{22,23},{4,5}} | collective-permute-start | bytes 884744 | tf_op jit(solution)/shard_map/ppermute | solution.py:310
  31.9 1.3 %collective-permute-start.16 = (bf16[384,384]{1,0:T(8,128)(2,1)S(1)}, bf16[384,384]{1,0:T(8,128)(2,1)S(1)}, u32[]{:S(2)}, u32[]{:S(2)}) collective-permute-start(bf16[384,384]{1,0:T(8,128)(2,1)S(1)} %shard_map.90.own.f2), channel_id=1, source_target_pairs={{12,4},{21,13},{30,22}} | collective-permute-start | bytes 884744 | tf_op jit(solution)/shard_map/ppermute | solution.py:310
  33.2 2.5 %collective-permute-done.15.rest_1_ = bf16[384,384]{1,0:T(8,128)(2,1)S(1)} collective-permute-done((bf16[384,384]{1,0:T(8,128)(2,1)S(1)}, bf16[384,384]{1,0:T(8,128)(2,1)S(1)}, u32[]{:S(2)}, u32[]{:S(2)}) %collective-permute-start.15) | collective-permute-done | bytes 294944 | tf_op jit(solution)/shard_map/ppermute | solution.py:310
  36.4 1.3 %collective-permute-start.18 = (bf16[384,384]{1,0:T(8,128)(2,1)S(1)}, bf16[384,384]{1,0:T(8,128)(2,1)S(1)}, u32[]{:S(2)}, u32[]{:S(2)}) collective-permute-start(bf16[384,384]{1,0:T(8,128)(2,1)S(1)} %shard_map.96), channel_id=1, source_target_pairs={{7,6},{15,14},{23,22},{4,5}} | collective-permute-start | bytes 884744 | tf_op jit(solution)/shard_map/ppermute | solution.py:310
  37.7 2.4 %shard_map.92 = (f32[384,384]{1,0:T(8,128)S(1)}, bf16[384,384]{1,0:T(8,128)(2,1)S(1)}, bf16[384,384]{1,0:T(8,128)(2,1)S(1)}, bf16[384,384]{1,0:T(8,128)(2,1)S(1)}, bf16[384,384]{1,0:T(8,128)(2,1)S(1)}) custom-call(f32[384,384]{1,0:T(8,128)} %rhs.5, bf16[3,384,384]{2,1,0:T(8,128)(2,1)} %a_c.3, bf16[3,384,384]{2,1,0:T(8,128)(2,1)} %b_c.3, ...), custom_call_target="tpu_custom_call" | custom-call | tf_op jit(solution)/shard_map/pallas_call | solution.py:342
  40.2 0.8 %shard_map.94.s2 = f32[384,384]{1,0:T(8,128)S(1)} custom-call(f32[384,384]{1,0:T(8,128)S(1)} %get-tuple-element.27.s1, bf16[384,384]{1,0:T(8,128)(2,1)S(1)} %get-tuple-element.28.a1, bf16[384,384]{1,0:T(8,128)(2,1)S(1)} %get-tuple-element.29.b1, bf16[384,384]{1,0:T(8,128)(2,1)S(1)} %collective-permute-done.10.rest_0_, ...), custom_call_target="tpu_custom_call" | custom-call | tf_op jit(solution)/shard_map/pallas_call | solution.py:342
  41.9 1.2 %shard_map.97 = (bf16[384,384]{1,0:T(8,128)(2,1)}, f32[384,384]{1,0:T(8,128)}) custom-call(bf16[384,384]{1,0:T(8,128)(2,1)S(1)} %shard_map.86.own.f0, bf16[384,384]{1,0:T(8,128)(2,1)S(1)} %shard_map.88.own.f1, bf16[384,384]{1,0:T(8,128)(2,1)S(1)} %shard_map.90.own.f2, f32[384,384]{1,0:T(8,128)S(1)} %shard_map.95.s3, ...), custom_call_target="tpu_custom_call" | custom-call | tf_op jit(solution)/shard_map/pallas_call | solution.py:342
  (26 shorter events, 1.9 us)
Async XLA Ops:
  0.7 2.9 %collective-permute-start.1 = (bf16[384,384]{1,0:T(8,128)(2,1)S(1)}, bf16[384,384]{1,0:T(8,128)(2,1)S(1)}, u32[]{:S(2)}, u32[]{:S(2)}) collective-permute-start(bf16[384,384]{1,0:T(8,128)(2,1)S(1)} %shard_map.86.own.f0), channel_id=1, source_target_pairs={{1,2},{10,11},{19,20},{28,29}} | collective-permute-start | bytes 884744 | tf_op jit(solution)/shard_map/ppermute | solution.py:310
  1.4 2.9 %collective-permute-start = (bf16[384,384]{1,0:T(8,128)(2,1)S(1)}, bf16[384,384]{1,0:T(8,128)(2,1)S(1)}, u32[]{:S(2)}, u32[]{:S(2)}) collective-permute-start(bf16[384,384]{1,0:T(8,128)(2,1)S(1)} %shard_map.86.own.f0), channel_id=1, source_target_pairs={{10,2},{19,11},{28,20}} | collective-permute-start | bytes 884744 | tf_op jit(solution)/shard_map/ppermute | solution.py:310
  2.1 3.6 %collective-permute-start.4 = (bf16[384,384]{1,0:T(8,128)(2,1)S(1)}, bf16[384,384]{1,0:T(8,128)(2,1)S(1)}, u32[]{:S(2)}, u32[]{:S(2)}) collective-permute-start(bf16[384,384]{1,0:T(8,128)(2,1)S(1)} %shard_map.86.own.f0), channel_id=1, source_target_pairs={{19,3},{28,12}} | collective-permute-start | bytes 884744 | tf_op jit(solution)/shard_map/ppermute | solution.py:310
  2.8 3.6 %collective-permute-start.5 = (bf16[384,384]{1,0:T(8,128)(2,1)S(1)}, bf16[384,384]{1,0:T(8,128)(2,1)S(1)}, u32[]{:S(2)}, u32[]{:S(2)}) collective-permute-start(bf16[384,384]{1,0:T(8,128)(2,1)S(1)} %shard_map.86.own.f0), channel_id=1, source_target_pairs={{10,12},{28,30}} | collective-permute-start | bytes 884744 | tf_op jit(solution)/shard_map/ppermute | solution.py:310
  3.6 4.1 %collective-permute-start.6 = (bf16[384,384]{1,0:T(8,128)(2,1)S(1)}, bf16[384,384]{1,0:T(8,128)(2,1)S(1)}, u32[]{:S(2)}, u32[]{:S(2)}) collective-permute-start(bf16[384,384]{1,0:T(8,128)(2,1)S(1)} %collective-permute-done.1.left), channel_id=1, source_target_pairs={{2,3},{20,21}} | collective-permute-start | bytes 884744 | tf_op jit(solution)/shard_map/ppermute | solution.py:310
  4.3 4.1 %collective-permute-start.2 = (bf16[384,384]{1,0:T(8,128)(2,1)S(1)}, bf16[384,384]{1,0:T(8,128)(2,1)S(1)}, u32[]{:S(2)}, u32[]{:S(2)}) collective-permute-start(bf16[384,384]{1,0:T(8,128)(2,1)S(1)} %shard_map.88.own.f1), channel_id=1, source_target_pairs={{11,3},{20,12},{29,21}} | collective-permute-start | bytes 884744 | tf_op jit(solution)/shard_map/ppermute | solution.py:310
  5.0 4.7 %collective-permute-start.3 = (bf16[384,384]{1,0:T(8,128)(2,1)S(1)}, bf16[384,384]{1,0:T(8,128)(2,1)S(1)}, u32[]{:S(2)}, u32[]{:S(2)}) collective-permute-start(bf16[384,384]{1,0:T(8,128)(2,1)S(1)} %shard_map.88.own.f1), channel_id=1, source_target_pairs={{2,3},{11,12},{20,21},{29,30}} | collective-permute-start | bytes 884744 | tf_op jit(solution)/shard_map/ppermute | solution.py:310
  5.7 4.8 %collective-permute-start.7 = (bf16[384,384]{1,0:T(8,128)(2,1)S(1)}, bf16[384,384]{1,0:T(8,128)(2,1)S(1)}, u32[]{:S(2)}, u32[]{:S(2)}) collective-permute-start(bf16[384,384]{1,0:T(8,128)(2,1)S(1)} %shard_map.86.own.f0), channel_id=1, source_target_pairs={{1,6},{10,14},{19,22},{28,31}} | collective-permute-start | bytes 884744 | tf_op jit(solution)/shard_map/ppermute | solution.py:310
  6.4 17.7 %collective-permute-start.8 = (bf16[384,384]{1,0:T(8,128)(2,1)S(1)}, bf16[384,384]{1,0:T(8,128)(2,1)S(1)}, u32[]{:S(2)}, u32[]{:S(2)}) collective-permute-start(bf16[384,384]{1,0:T(8,128)(2,1)S(1)} %shard_map.86.own.f0), channel_id=1, source_target_pairs={{1,5},{10,13},{28,4}} | collective-permute-start | bytes 884744 | tf_op jit(solution)/shard_map/ppermute | solution.py:310
  7.7 17.7 %collective-permute-start.10 = (bf16[384,384]{1,0:T(8,128)(2,1)S(1)}, bf16[384,384]{1,0:T(8,128)(2,1)S(1)}, u32[]{:S(2)}, u32[]{:S(2)}) collective-permute-start(bf16[384,384]{1,0:T(8,128)(2,1)S(1)} %shard_map.88.own.f1), channel_id=1, source_target_pairs={{2,6},{11,14},{20,22},{29,31}} | collective-permute-start | bytes 884744 | tf_op jit(solution)/shard_map/ppermute | solution.py:310
  8.4 22.1 %collective-permute-start.11 = (bf16[384,384]{1,0:T(8,128)(2,1)S(1)}, bf16[384,384]{1,0:T(8,128)(2,1)S(1)}, u32[]{:S(2)}, u32[]{:S(2)}) collective-permute-start(bf16[384,384]{1,0:T(8,128)(2,1)S(1)} %shard_map.88.own.f1), channel_id=1, source_target_pairs={{2,4},{11,13},{29,5}} | collective-permute-start | bytes 884744 | tf_op jit(solution)/shard_map/ppermute | solution.py:310
  9.8 22.2 %collective-permute-start.14 = (bf16[384,384]{1,0:T(8,128)(2,1)S(1)}, bf16[384,384]{1,0:T(8,128)(2,1)S(1)}, u32[]{:S(2)}, u32[]{:S(2)}) collective-permute-start(bf16[384,384]{1,0:T(8,128)(2,1)S(1)} %shard_map.90.own.f2), channel_id=1, source_target_pairs={{3,7},{12,15},{21,23},{30,6}} | collective-permute-start | bytes 884744 | tf_op jit(solution)/shard_map/ppermute | solution.py:310
  10.5 25.2 %collective-permute-start.15 = (bf16[384,384]{1,0:T(8,128)(2,1)S(1)}, bf16[384,384]{1,0:T(8,128)(2,1)S(1)}, u32[]{:S(2)}, u32[]{:S(2)}) collective-permute-start(bf16[384,384]{1,0:T(8,128)(2,1)S(1)} %shard_map.90.own.f2), channel_id=1, source_target_pairs={{3,4},{21,5},{30,14},{12,13}} | collective-permute-start | bytes 884744 | tf_op jit(solution)/shard_map/ppermute | solution.py:310
  24.1 12.3 %collective-permute-start.9 = (bf16[384,384]{1,0:T(8,128)(2,1)S(1)}, bf16[384,384]{1,0:T(8,128)(2,1)S(1)}, u32[]{:S(2)}, u32[]{:S(2)}) collective-permute-start(bf16[384,384]{1,0:T(8,128)(2,1)S(1)} %shard_map.91), channel_id=1, source_target_pairs={{6,7},{14,15},{22,23},{5,4}} | collective-permute-start | bytes 884744 | tf_op jit(solution)/shard_map/ppermute | solution.py:310
  25.4 14.8 %collective-permute-start.12 = (bf16[384,384]{1,0:T(8,128)(2,1)S(1)}, bf16[384,384]{1,0:T(8,128)(2,1)S(1)}, u32[]{:S(2)}, u32[]{:S(2)}) collective-permute-start(bf16[384,384]{1,0:T(8,128)(2,1)S(1)} %shard_map.88.own.f1), channel_id=1, source_target_pairs={{20,4},{29,13}} | collective-permute-start | bytes 884744 | tf_op jit(solution)/shard_map/ppermute | solution.py:310
  30.6 9.6 %collective-permute-start.13 = (bf16[384,384]{1,0:T(8,128)(2,1)S(1)}, bf16[384,384]{1,0:T(8,128)(2,1)S(1)}, u32[]{:S(2)}, u32[]{:S(2)}) collective-permute-start(bf16[384,384]{1,0:T(8,128)(2,1)S(1)} %shard_map.93), channel_id=1, source_target_pairs={{6,7},{14,15},{22,23},{4,5}} | collective-permute-start | bytes 884744 | tf_op jit(solution)/shard_map/ppermute | solution.py:310
  31.9 9.5 %collective-permute-start.16 = (bf16[384,384]{1,0:T(8,128)(2,1)S(1)}, bf16[384,384]{1,0:T(8,128)(2,1)S(1)}, u32[]{:S(2)}, u32[]{:S(2)}) collective-permute-start(bf16[384,384]{1,0:T(8,128)(2,1)S(1)} %shard_map.90.own.f2), channel_id=1, source_target_pairs={{12,4},{21,13},{30,22}} | collective-permute-start | bytes 884744 | tf_op jit(solution)/shard_map/ppermute | solution.py:310
  35.7 6.2 %collective-permute-start.17 = (bf16[384,384]{1,0:T(8,128)(2,1)S(1)}, bf16[384,384]{1,0:T(8,128)(2,1)S(1)}, u32[]{:S(2)}, u32[]{:S(2)}) collective-permute-start(bf16[384,384]{1,0:T(8,128)(2,1)S(1)} %shard_map.90.own.f2), channel_id=1, source_target_pairs={{30,31}} | collective-permute-start | bytes 884744 | tf_op jit(solution)/shard_map/ppermute | solution.py:310
  36.4 5.5 %collective-permute-start.18 = (bf16[384,384]{1,0:T(8,128)(2,1)S(1)}, bf16[384,384]{1,0:T(8,128)(2,1)S(1)}, u32[]{:S(2)}, u32[]{:S(2)}) collective-permute-start(bf16[384,384]{1,0:T(8,128)(2,1)S(1)} %shard_map.96), channel_id=1, source_target_pairs={{7,6},{15,14},{23,22},{4,5}} | collective-permute-start | bytes 884744 | tf_op jit(solution)/shard_map/ppermute | solution.py:310

commit v2 on v1

--- a/solution.py
+++ b/solution.py
@@ -166,13 +166,10 @@
         f1[...] = solve(state, uk, utk, vk, vl, inverse, lhs, mid)
 
 
-def third_early(rows_n, first, down, direct, on_chip, s, a0, b0, s1):
-    even = lax.rem(lax.axis_index("col"), 2) == 0
-
+def third_early(rows_n, first, down, left, s, a0, b0, s1):
     @pl.when(level_of(rows_n) == first + 2)
     def _():
-        left = jnp.where(even, direct[...], on_chip[...])
-        s1[...] = s[...] - (dot(a0[...], down[...]) + dot(left, b0[...]))
+        s1[...] = s[...] - (dot(a0[...], down[...]) + dot(left[...], b0[...]))
 
 
 def third(rows_n, first, down, left, uk, utk, vk, vl, inverse, s1, a1, b1, f2, lhs, mid):
@@ -360,12 +357,7 @@
         down = move(f0, up(0, 1))
         left = move(f0, right(0, 1))
         down_far = move(f0, up(0, 2))
-        direct, on_chip = [], []
-        for i, j in owners(0):
-            if j + 2 < cols_n:
-                source, target = (j, direct) if j % 2 == 0 else (j + 1, on_chip)
-                target.append((i * cols_n + source, i * cols_n + j + 2))
-        left_far = [move(f0, direct), move(left, on_chip)]
+        left_far = move(f0, right(0, 2))
         far0 = spread(ops0, cols_n, f0, "a", call)
         *basis, s, a0, b0, a1, b1 = call(
             functools.partial(prepare, rows_n, first),
@@ -388,7 +380,7 @@
         (s1,) = call(
             functools.partial(third_early, rows_n, first),
             [],
-            [down_far, *left_far, s, a0, b0],
+            [down_far, left_far, s, a0, b0],
             [state],
             [],
             "third_early",

time: 43.4 us -> 42.1 us (0.970)
  waiting for transfers between devices: 19.1 us -> 17.4 us
  starting transfers between devices: 17.8 us -> 18.3 us
    ppermute x19 -> x18, waiting for transfers between devices: 19.1 us -> 17.4 us  [move(): return lax.ppermute(value, AXES, pairs)]
    ppermute x19 -> x18, starting transfers between devices: 17.8 us -> 18.3 us  [move(): return lax.ppermute(value, AXES, pairs)]
  transfers between devices with their start and end apart: 19 -> 18, of which waited for: 4 -> 3; matrix products, arithmetic and copies ran while one was open for 0% -> 0% of each run, Pallas kernels for 9% -> 9%
where the time goes in v2:
time: 42.1 us; the launch traced here: 41.8 us
  starting transfers between devices  18.3 us (43%)
  waiting for transfers between devices  17.4 us (41%)
  Pallas kernels  5.15 us (12%)
  between operations  0.97 us (2%)
    ppermute x18, starting transfers between devices, move(): return lax.ppermute(value, AXES, pairs)  18.3 us
    ppermute x18, waiting for transfers between devices, move(): return lax.ppermute(value, AXES, pairs)  17.4 us
    pallas_call x12, Pallas kernels, call(): pl.pallas_call(kernel, out_shape=outs, in_specs=[FAR_SPEC] * len(far) + [...  5.15 us
  transfers between devices with their start and end apart: 18, of which 3 were waited for; matrix products, arithmetic and copies ran while one was open for 0% of the time, Pallas kernels for 9%

profile of v2, /device:TPU:16, one launch (start us, length us, event | category | flops | bytes accessed | tf_op | source)
XLA Modules:
  0.0 41.8 jit_solution(3020671800856897931)
XLA Ops:
  0.7 0.7 %collective-permute-start = (bf16[384,384]{1,0:T(8,128)(2,1)S(1)}, bf16[384,384]{1,0:T(8,128)(2,1)S(1)}, u32[]{:S(2)}, u32[]{:S(2)}) collective-permute-start(bf16[384,384]{1,0:T(8,128)(2,1)S(1)} %shard_map.86.own.f0), channel_id=1, source_target_pairs={{10,2},{19,11},{28,20}} | collective-permute-start | bytes 884744 | tf_op jit(solution)/shard_map/ppermute | solution.py:307
  1.4 0.7 %collective-permute-start.1 = (bf16[384,384]{1,0:T(8,128)(2,1)S(1)}, bf16[384,384]{1,0:T(8,128)(2,1)S(1)}, u32[]{:S(2)}, u32[]{:S(2)}) collective-permute-start(bf16[384,384]{1,0:T(8,128)(2,1)S(1)} %shard_map.86.own.f0), channel_id=1, source_target_pairs={{1,2},{10,11},{19,20},{28,29}} | collective-permute-start | bytes 884744 | tf_op jit(solution)/shard_map/ppermute | solution.py:307
  2.1 0.7 %collective-permute-start.4 = (bf16[384,384]{1,0:T(8,128)(2,1)S(1)}, bf16[384,384]{1,0:T(8,128)(2,1)S(1)}, u32[]{:S(2)}, u32[]{:S(2)}) collective-permute-start(bf16[384,384]{1,0:T(8,128)(2,1)S(1)} %shard_map.86.own.f0), channel_id=1, source_target_pairs={{19,3},{28,12}} | collective-permute-start | bytes 884744 | tf_op jit(solution)/shard_map/ppermute | solution.py:307
  2.8 0.7 %collective-permute-start.5 = (bf16[384,384]{1,0:T(8,128)(2,1)S(1)}, bf16[384,384]{1,0:T(8,128)(2,1)S(1)}, u32[]{:S(2)}, u32[]{:S(2)}) collective-permute-start(bf16[384,384]{1,0:T(8,128)(2,1)S(1)} %shard_map.86.own.f0), channel_id=1, source_target_pairs={{1,3},{10,12},{19,21},{28,30}} | collective-permute-start | bytes 884744 | tf_op jit(solution)/shard_map/ppermute | solution.py:307
  3.6 0.7 %collective-permute-start.2 = (bf16[384,384]{1,0:T(8,128)(2,1)S(1)}, bf16[384,384]{1,0:T(8,128)(2,1)S(1)}, u32[]{:S(2)}, u32[]{:S(2)}) collective-permute-start(bf16[384,384]{1,0:T(8,128)(2,1)S(1)} %shard_map.88.own.f1), channel_id=1, source_target_pairs={{11,3},{20,12},{29,21}} | collective-permute-start | bytes 884744 | tf_op jit(solution)/shard_map/ppermute | solution.py:307
  4.3 0.7 %collective-permute-start.3 = (bf16[384,384]{1,0:T(8,128)(2,1)S(1)}, bf16[384,384]{1,0:T(8,128)(2,1)S(1)}, u32[]{:S(2)}, u32[]{:S(2)}) collective-permute-start(bf16[384,384]{1,0:T(8,128)(2,1)S(1)} %shard_map.88.own.f1), channel_id=1, source_target_pairs={{2,3},{11,12},{20,21},{29,30}} | collective-permute-start | bytes 884744 | tf_op jit(solution)/shard_map/ppermute | solution.py:307
  5.0 0.7 %collective-permute-start.6 = (bf16[384,384]{1,0:T(8,128)(2,1)S(1)}, bf16[384,384]{1,0:T(8,128)(2,1)S(1)}, u32[]{:S(2)}, u32[]{:S(2)}) collective-permute-start(bf16[384,384]{1,0:T(8,128)(2,1)S(1)} %shard_map.86.own.f0), channel_id=1, source_target_pairs={{1,6},{10,14},{19,22},{28,31}} | collective-permute-start | bytes 884744 | tf_op jit(solution)/shard_map/ppermute | solution.py:307
  5.7 1.3 %collective-permute-start.7 = (bf16[384,384]{1,0:T(8,128)(2,1)S(1)}, bf16[384,384]{1,0:T(8,128)(2,1)S(1)}, u32[]{:S(2)}, u32[]{:S(2)}) collective-permute-start(bf16[384,384]{1,0:T(8,128)(2,1)S(1)} %shard_map.86.own.f0), channel_id=1, source_target_pairs={{1,5},{10,13},{28,4}} | collective-permute-start | bytes 884744 | tf_op jit(solution)/shard_map/ppermute | solution.py:307
  7.0 1.3 %collective-permute-start.10 = (bf16[384,384]{1,0:T(8,128)(2,1)S(1)}, bf16[384,384]{1,0:T(8,128)(2,1)S(1)}, u32[]{:S(2)}, u32[]{:S(2)}) collective-permute-start(bf16[384,384]{1,0:T(8,128)(2,1)S(1)} %shard_map.88.own.f1), channel_id=1, source_target_pairs={{2,4},{11,13},{29,5}} | collective-permute-start | bytes 884744 | tf_op jit(solution)/shard_map/ppermute | solution.py:307
  8.3 0.7 %collective-permute-start.9 = (bf16[384,384]{1,0:T(8,128)(2,1)S(1)}, bf16[384,384]{1,0:T(8,128)(2,1)S(1)}, u32[]{:S(2)}, u32[]{:S(2)}) collective-permute-start(bf16[384,384]{1,0:T(8,128)(2,1)S(1)} %shard_map.88.own.f1), channel_id=1, source_target_pairs={{2,6},{11,14},{20,22},{29,31}} | collective-permute-start | bytes 884744 | tf_op jit(solution)/shard_map/ppermute | solution.py:307
  9.1 0.7 %collective-permute-start.13 = (bf16[384,384]{1,0:T(8,128)(2,1)S(1)}, bf16[384,384]{1,0:T(8,128)(2,1)S(1)}, u32[]{:S(2)}, u32[]{:S(2)}) collective-permute-start(bf16[384,384]{1,0:T(8,128)(2,1)S(1)} %shard_map.90.own.f2), channel_id=1, source_target_pairs={{3,7},{12,15},{21,23},{30,6}} | collective-permute-start | bytes 884744 | tf_op jit(solution)/shard_map/ppermute | solution.py:307
  9.8 1.3 %collective-permute-start.14 = (bf16[384,384]{1,0:T(8,128)(2,1)S(1)}, bf16[384,384]{1,0:T(8,128)(2,1)S(1)}, u32[]{:S(2)}, u32[]{:S(2)}) collective-permute-start(bf16[384,384]{1,0:T(8,128)(2,1)S(1)} %shard_map.90.own.f2), channel_id=1, source_target_pairs={{3,4},{21,5},{30,14},{12,13}} | collective-permute-start | bytes 884744 | tf_op jit(solution)/shard_map/ppermute | solution.py:307
  11.1 13.4 %collective-permute-done.7.rest_1_ = bf16[384,384]{1,0:T(8,128)(2,1)S(1)} collective-permute-done((bf16[384,384]{1,0:T(8,128)(2,1)S(1)}, bf16[384,384]{1,0:T(8,128)(2,1)S(1)}, u32[]{:S(2)}, u32[]{:S(2)}) %collective-permute-start.7) | collective-permute-done | bytes 294944 | tf_op jit(solution)/shard_map/ppermute | solution.py:307
  24.5 1.3 %collective-permute-start.8 = (bf16[384,384]{1,0:T(8,128)(2,1)S(1)}, bf16[384,384]{1,0:T(8,128)(2,1)S(1)}, u32[]{:S(2)}, u32[]{:S(2)}) collective-permute-start(bf16[384,384]{1,0:T(8,128)(2,1)S(1)} %shard_map.91), channel_id=1, source_target_pairs={{6,7},{14,15},{22,23},{5,4}} | collective-permute-start | bytes 884744 | tf_op jit(solution)/shard_map/ppermute | solution.py:307
  25.8 1.3 %collective-permute-start.11 = (bf16[384,384]{1,0:T(8,128)(2,1)S(1)}, bf16[384,384]{1,0:T(8,128)(2,1)S(1)}, u32[]{:S(2)}, u32[]{:S(2)}) collective-permute-start(bf16[384,384]{1,0:T(8,128)(2,1)S(1)} %shard_map.88.own.f1), channel_id=1, source_target_pairs={{20,4},{29,13}} | collective-permute-start | bytes 884744 | tf_op jit(solution)/shard_map/ppermute | solution.py:307
  27.1 2.5 %collective-permute-start.12 = (bf16[384,384]{1,0:T(8,128)(2,1)S(1)}, bf16[384,384]{1,0:T(8,128)(2,1)S(1)}, u32[]{:S(2)}, u32[]{:S(2)}) collective-permute-start(bf16[384,384]{1,0:T(8,128)(2,1)S(1)} %shard_map.93), channel_id=1, source_target_pairs={{6,7},{14,15},{22,23},{4,5}} | collective-permute-start | bytes 884744 | tf_op jit(solution)/shard_map/ppermute | solution.py:307
  29.6 1.3 %collective-permute-start.15 = (bf16[384,384]{1,0:T(8,128)(2,1)S(1)}, bf16[384,384]{1,0:T(8,128)(2,1)S(1)}, u32[]{:S(2)}, u32[]{:S(2)}) collective-permute-start(bf16[384,384]{1,0:T(8,128)(2,1)S(1)} %shard_map.90.own.f2), channel_id=1, source_target_pairs={{12,4},{21,13},{30,22}} | collective-permute-start | bytes 884744 | tf_op jit(solution)/shard_map/ppermute | solution.py:307
  30.9 3.4 %collective-permute-done.14.rest_1_ = bf16[384,384]{1,0:T(8,128)(2,1)S(1)} collective-permute-done((bf16[384,384]{1,0:T(8,128)(2,1)S(1)}, bf16[384,384]{1,0:T(8,128)(2,1)S(1)}, u32[]{:S(2)}, u32[]{:S(2)}) %collective-permute-start.14) | collective-permute-done | bytes 294944 | tf_op jit(solution)/shard_map/ppermute | solution.py:307
  34.4 0.7 %collective-permute-start.16 = (bf16[384,384]{1,0:T(8,128)(2,1)S(1)}, bf16[384,384]{1,0:T(8,128)(2,1)S(1)}, u32[]{:S(2)}, u32[]{:S(2)}) collective-permute-start(bf16[384,384]{1,0:T(8,128)(2,1)S(1)} %shard_map.90.own.f2), channel_id=1, source_target_pairs={{30,31}} | collective-permute-start | bytes 884744 | tf_op jit(solution)/shard_map/ppermute | solution.py:307
  35.1 1.3 %collective-permute-start.17 = (bf16[384,384]{1,0:T(8,128)(2,1)S(1)}, bf16[384,384]{1,0:T(8,128)(2,1)S(1)}, u32[]{:S(2)}, u32[]{:S(2)}) collective-permute-start(bf16[384,384]{1,0:T(8,128)(2,1)S(1)} %shard_map.96), channel_id=1, source_target_pairs={{7,6},{15,14},{23,22},{4,5}} | collective-permute-start | bytes 884744 | tf_op jit(solution)/shard_map/ppermute | solution.py:307
  36.4 2.4 %shard_map.92 = (f32[384,384]{1,0:T(8,128)S(1)}, bf16[384,384]{1,0:T(8,128)(2,1)S(1)}, bf16[384,384]{1,0:T(8,128)(2,1)S(1)}, bf16[384,384]{1,0:T(8,128)(2,1)S(1)}, bf16[384,384]{1,0:T(8,128)(2,1)S(1)}) custom-call(f32[384,384]{1,0:T(8,128)} %rhs.5, bf16[3,384,384]{2,1,0:T(8,128)(2,1)} %a_c.3, bf16[3,384,384]{2,1,0:T(8,128)(2,1)} %b_c.3, ...), custom_call_target="tpu_custom_call" | custom-call | tf_op jit(solution)/shard_map/pallas_call | solution.py:339
  38.9 0.8 %shard_map.94.s2 = f32[384,384]{1,0:T(8,128)S(1)} custom-call(f32[384,384]{1,0:T(8,128)S(1)} %get-tuple-element.27.s1, bf16[384,384]{1,0:T(8,128)(2,1)S(1)} %get-tuple-element.28.a1, bf16[384,384]{1,0:T(8,128)(2,1)S(1)} %get-tuple-element.29.b1, bf16[384,384]{1,0:T(8,128)(2,1)S(1)} %collective-permute-done.9.rest_0_, ...), custom_call_target="tpu_custom_call" | custom-call | tf_op jit(solution)/shard_map/pallas_call | solution.py:339
  39.7 0.5 %collective-permute-done.15.rest_2_ = bf16[384,384]{1,0:T(8,128)(2,1)S(1)} collective-permute-done((bf16[384,384]{1,0:T(8,128)(2,1)S(1)}, bf16[384,384]{1,0:T(8,128)(2,1)S(1)}, u32[]{:S(2)}, u32[]{:S(2)}) %collective-permute-start.15) | collective-permute-done | bytes 294944 | tf_op jit(solution)/shard_map/ppermute | solution.py:307
  40.6 1.2 %shard_map.97 = (bf16[384,384]{1,0:T(8,128)(2,1)}, f32[384,384]{1,0:T(8,128)}) custom-call(bf16[384,384]{1,0:T(8,128)(2,1)S(1)} %shard_map.86.own.f0, bf16[384,384]{1,0:T(8,128)(2,1)S(1)} %shard_map.88.own.f1, bf16[384,384]{1,0:T(8,128)(2,1)S(1)} %shard_map.90.own.f2, f32[384,384]{1,0:T(8,128)S(1)} %shard_map.95.s3, ...), custom_call_target="tpu_custom_call" | custom-call | tf_op jit(solution)/shard_map/pallas_call | solution.py:339
  (24 shorter events, 0.8 us)
Async XLA Ops:
  0.7 2.9 %collective-permute-start = (bf16[384,384]{1,0:T(8,128)(2,1)S(1)}, bf16[384,384]{1,0:T(8,128)(2,1)S(1)}, u32[]{:S(2)}, u32[]{:S(2)}) collective-permute-start(bf16[384,384]{1,0:T(8,128)(2,1)S(1)} %shard_map.86.own.f0), channel_id=1, source_target_pairs={{10,2},{19,11},{28,20}} | collective-permute-start | bytes 884744 | tf_op jit(solution)/shard_map/ppermute | solution.py:307
  1.4 2.2 %collective-permute-start.1 = (bf16[384,384]{1,0:T(8,128)(2,1)S(1)}, bf16[384,384]{1,0:T(8,128)(2,1)S(1)}, u32[]{:S(2)}, u32[]{:S(2)}) collective-permute-start(bf16[384,384]{1,0:T(8,128)(2,1)S(1)} %shard_map.86.own.f0), channel_id=1, source_target_pairs={{1,2},{10,11},{19,20},{28,29}} | collective-permute-start | bytes 884744 | tf_op jit(solution)/shard_map/ppermute | solution.py:307
  2.1 3.6 %collective-permute-start.4 = (bf16[384,384]{1,0:T(8,128)(2,1)S(1)}, bf16[384,384]{1,0:T(8,128)(2,1)S(1)}, u32[]{:S(2)}, u32[]{:S(2)}) collective-permute-start(bf16[384,384]{1,0:T(8,128)(2,1)S(1)} %shard_map.86.own.f0), channel_id=1, source_target_pairs={{19,3},{28,12}} | collective-permute-start | bytes 884744 | tf_op jit(solution)/shard_map/ppermute | solution.py:307
  2.8 4.2 %collective-permute-start.5 = (bf16[384,384]{1,0:T(8,128)(2,1)S(1)}, bf16[384,384]{1,0:T(8,128)(2,1)S(1)}, u32[]{:S(2)}, u32[]{:S(2)}) collective-permute-start(bf16[384,384]{1,0:T(8,128)(2,1)S(1)} %shard_map.86.own.f0), channel_id=1, source_target_pairs={{1,3},{10,12},{19,21},{28,30}} | collective-permute-start | bytes 884744 | tf_op jit(solution)/shard_map/ppermute | solution.py:307
  3.6 4.7 %collective-permute-start.2 = (bf16[384,384]{1,0:T(8,128)(2,1)S(1)}, bf16[384,384]{1,0:T(8,128)(2,1)S(1)}, u32[]{:S(2)}, u32[]{:S(2)}) collective-permute-start(bf16[384,384]{1,0:T(8,128)(2,1)S(1)} %shard_map.88.own.f1), channel_id=1, source_target_pairs={{11,3},{20,12},{29,21}} | collective-permute-start | bytes 884744 | tf_op jit(solution)/shard_map/ppermute | solution.py:307
  4.3 4.7 %collective-permute-start.3 = (bf16[384,384]{1,0:T(8,128)(2,1)S(1)}, bf16[384,384]{1,0:T(8,128)(2,1)S(1)}, u32[]{:S(2)}, u32[]{:S(2)}) collective-permute-start(bf16[384,384]{1,0:T(8,128)(2,1)S(1)} %shard_map.88.own.f1), channel_id=1, source_target_pairs={{2,3},{11,12},{20,21},{29,30}} | collective-permute-start | bytes 884744 | tf_op jit(solution)/shard_map/ppermute | solution.py:307
  5.0 4.8 %collective-permute-start.6 = (bf16[384,384]{1,0:T(8,128)(2,1)S(1)}, bf16[384,384]{1,0:T(8,128)(2,1)S(1)}, u32[]{:S(2)}, u32[]{:S(2)}) collective-permute-start(bf16[384,384]{1,0:T(8,128)(2,1)S(1)} %shard_map.86.own.f0), channel_id=1, source_target_pairs={{1,6},{10,14},{19,22},{28,31}} | collective-permute-start | bytes 884744 | tf_op jit(solution)/shard_map/ppermute | solution.py:307
  5.7 18.7 %collective-permute-start.7 = (bf16[384,384]{1,0:T(8,128)(2,1)S(1)}, bf16[384,384]{1,0:T(8,128)(2,1)S(1)}, u32[]{:S(2)}, u32[]{:S(2)}) collective-permute-start(bf16[384,384]{1,0:T(8,128)(2,1)S(1)} %shard_map.86.own.f0), channel_id=1, source_target_pairs={{1,5},{10,13},{28,4}} | collective-permute-start | bytes 884744 | tf_op jit(solution)/shard_map/ppermute | solution.py:307
  7.0 18.8 %collective-permute-start.10 = (bf16[384,384]{1,0:T(8,128)(2,1)S(1)}, bf16[384,384]{1,0:T(8,128)(2,1)S(1)}, u32[]{:S(2)}, u32[]{:S(2)}) collective-permute-start(bf16[384,384]{1,0:T(8,128)(2,1)S(1)} %shard_map.88.own.f1), channel_id=1, source_target_pairs={{2,4},{11,13},{29,5}} | collective-permute-start | bytes 884744 | tf_op jit(solution)/shard_map/ppermute | solution.py:307
  8.3 18.7 %collective-permute-start.9 = (bf16[384,384]{1,0:T(8,128)(2,1)S(1)}, bf16[384,384]{1,0:T(8,128)(2,1)S(1)}, u32[]{:S(2)}, u32[]{:S(2)}) collective-permute-start(bf16[384,384]{1,0:T(8,128)(2,1)S(1)} %shard_map.88.own.f1), channel_id=1, source_target_pairs={{2,6},{11,14},{20,22},{29,31}} | collective-permute-start | bytes 884744 | tf_op jit(solution)/shard_map/ppermute | solution.py:307
  9.1 20.5 %collective-permute-start.13 = (bf16[384,384]{1,0:T(8,128)(2,1)S(1)}, bf16[384,384]{1,0:T(8,128)(2,1)S(1)}, u32[]{:S(2)}, u32[]{:S(2)}) collective-permute-start(bf16[384,384]{1,0:T(8,128)(2,1)S(1)} %shard_map.90.own.f2), channel_id=1, source_target_pairs={{3,7},{12,15},{21,23},{30,6}} | collective-permute-start | bytes 884744 | tf_op jit(solution)/shard_map/ppermute | solution.py:307
  9.8 24.6 %collective-permute-start.14 = (bf16[384,384]{1,0:T(8,128)(2,1)S(1)}, bf16[384,384]{1,0:T(8,128)(2,1)S(1)}, u32[]{:S(2)}, u32[]{:S(2)}) collective-permute-start(bf16[384,384]{1,0:T(8,128)(2,1)S(1)} %shard_map.90.own.f2), channel_id=1, source_target_pairs={{3,4},{21,5},{30,14},{12,13}} | collective-permute-start | bytes 884744 | tf_op jit(solution)/shard_map/ppermute | solution.py:307
  24.5 10.6 %collective-permute-start.8 = (bf16[384,384]{1,0:T(8,128)(2,1)S(1)}, bf16[384,384]{1,0:T(8,128)(2,1)S(1)}, u32[]{:S(2)}, u32[]{:S(2)}) collective-permute-start(bf16[384,384]{1,0:T(8,128)(2,1)S(1)} %shard_map.91), channel_id=1, source_target_pairs={{6,7},{14,15},{22,23},{5,4}} | collective-permute-start | bytes 884744 | tf_op jit(solution)/shard_map/ppermute | solution.py:307
  25.8 13.1 %collective-permute-start.11 = (bf16[384,384]{1,0:T(8,128)(2,1)S(1)}, bf16[384,384]{1,0:T(8,128)(2,1)S(1)}, u32[]{:S(2)}, u32[]{:S(2)}) collective-permute-start(bf16[384,384]{1,0:T(8,128)(2,1)S(1)} %shard_map.88.own.f1), channel_id=1, source_target_pairs={{20,4},{29,13}} | collective-permute-start | bytes 884744 | tf_op jit(solution)/shard_map/ppermute | solution.py:307
  27.1 11.7 %collective-permute-start.12 = (bf16[384,384]{1,0:T(8,128)(2,1)S(1)}, bf16[384,384]{1,0:T(8,128)(2,1)S(1)}, u32[]{:S(2)}, u32[]{:S(2)}) collective-permute-start(bf16[384,384]{1,0:T(8,128)(2,1)S(1)} %shard_map.93), channel_id=1, source_target_pairs={{6,7},{14,15},{22,23},{4,5}} | collective-permute-start | bytes 884744 | tf_op jit(solution)/shard_map/ppermute | solution.py:307
  29.6 10.6 %collective-permute-start.15 = (bf16[384,384]{1,0:T(8,128)(2,1)S(1)}, bf16[384,384]{1,0:T(8,128)(2,1)S(1)}, u32[]{:S(2)}, u32[]{:S(2)}) collective-permute-start(bf16[384,384]{1,0:T(8,128)(2,1)S(1)} %shard_map.90.own.f2), channel_id=1, source_target_pairs={{12,4},{21,13},{30,22}} | collective-permute-start | bytes 884744 | tf_op jit(solution)/shard_map/ppermute | solution.py:307
  34.4 6.2 %collective-permute-start.16 = (bf16[384,384]{1,0:T(8,128)(2,1)S(1)}, bf16[384,384]{1,0:T(8,128)(2,1)S(1)}, u32[]{:S(2)}, u32[]{:S(2)}) collective-permute-start(bf16[384,384]{1,0:T(8,128)(2,1)S(1)} %shard_map.90.own.f2), channel_id=1, source_target_pairs={{30,31}} | collective-permute-start | bytes 884744 | tf_op jit(solution)/shard_map/ppermute | solution.py:307
  35.1 5.5 %collective-permute-start.17 = (bf16[384,384]{1,0:T(8,128)(2,1)S(1)}, bf16[384,384]{1,0:T(8,128)(2,1)S(1)}, u32[]{:S(2)}, u32[]{:S(2)}) collective-permute-start(bf16[384,384]{1,0:T(8,128)(2,1)S(1)} %shard_map.96), channel_id=1, source_target_pairs={{7,6},{15,14},{23,22},{4,5}} | collective-permute-start | bytes 884744 | tf_op jit(solution)/shard_map/ppermute | solution.py:307

commit v3 on v2

--- a/solution.py
+++ b/solution.py
@@ -142,12 +142,13 @@
         f0[...] = solve(s[...], uk, utk, vk, vl, inverse, lhs, mid)
 
 
-def prepare(rows_n, first, rhs, a_c, b_c, u_far, v_far, a_vals, b_vals, uk, utk, vk, vl, inverse, s, a0, b0, a1, b1, u, v, av, bv, sem):
+def prepare(rows_n, first, rhs, a_c, b_c, u_far, v_far, a_vals, b_vals, uk, utk, vk, vl, inverse, s, a0, b0, a1, b1, a2, b2, u, v, av, bv, sem):
     level = level_of(rows_n)
+    terms = ((rhs, s), (a_c.at[0], a0), (b_c.at[0], b0), (a_c.at[1], a1), (b_c.at[1], b1))
 
     @pl.when((level > first) & (level <= first + 2))
     def _():
-        moves = copies(((v_far, v), (u_far, u), (a_vals, av), (b_vals, bv), (rhs, s), (a_c.at[0], a0), (b_c.at[0], b0), (a_c.at[1], a1), (b_c.at[1], b1)), sem)
+        moves = copies(((v_far, v), (u_far, u), (a_vals, av), (b_vals, bv), *terms), sem)
         moves[0].wait()
         set_right_basis(v, vk, vl)
         moves[1].wait()
@@ -158,11 +159,22 @@
         for move in moves[4:]:
             move.wait()
 
-
-def second(rows_n, first, down, left, uk, utk, vk, vl, inverse, s, ca, cb, f1, lhs, mid):
-    @pl.when(level_of(rows_n) == first + 1)
-    def _():
-        state = s[...] - (dot(ca[...], down[...]) + dot(left[...], cb[...]))
+    @pl.when(level > first + 2)
+    def _():
+        for move in copies((*terms, (a_c.at[2], a2), (b_c.at[2], b2)), sem):
+            move.wait()
+
+
+def take_left(rows_n, level, left, s, coup_b, out):
+    @pl.when(level_of(rows_n) == level)
+    def _():
+        out[...] = s[...] - dot(left[...], coup_b[...])
+
+
+def second(rows_n, level, down, uk, utk, vk, vl, inverse, s, coup_a, f1, lhs, mid):
+    @pl.when(level_of(rows_n) == level)
+    def _():
+        state = s[...] - dot(coup_a[...], down[...])
         f1[...] = solve(state, uk, utk, vk, vl, inverse, lhs, mid)
 
 
@@ -170,13 +182,6 @@
     @pl.when(level_of(rows_n) == first + 2)
     def _():
         s1[...] = s[...] - (dot(a0[...], down[...]) + dot(left[...], b0[...]))
-
-
-def third(rows_n, first, down, left, uk, utk, vk, vl, inverse, s1, a1, b1, f2, lhs, mid):
-    @pl.when(level_of(rows_n) == first + 2)
-    def _():
-        state = s1[...] - (dot(a1[...], down[...]) + dot(left[...], b1[...]))
-        f2[...] = solve(state, uk, utk, vk, vl, inverse, lhs, mid)
 
 
 def subtract(cols_n, ops, arrived, got, state, coup_a, coup_b, out, kinds=("down", "left")):
@@ -189,18 +194,7 @@
             out[...] -= dot(got[...], coup_b[...]) if kind == "left" else dot(coup_a[...], got[...])
 
 
-def middle(rows_n, cols_n, first, ops, rhs, a_c, b_c, *rest):
-    arrived, (s1, a1, b1, a2, b2, s, a0, b0, got, sem) = rest[: len(ops)], rest[len(ops) :]
-
-    @pl.when(level_of(rows_n) > first + 2)
-    def _():
-        pairs = ((rhs, s), (a_c.at[0], a0), (b_c.at[0], b0), (a_c.at[1], a1), (b_c.at[1], b1), (a_c.at[2], a2), (b_c.at[2], b2))
-        for move in copies(pairs, sem):
-            move.wait()
-        subtract(cols_n, ops, arrived, got, s, a0, b0, s1)
-
-
-def middle_late(rows_n, cols_n, first, ops, s1, a1, b1, *rest):
+def middle(rows_n, cols_n, first, ops, s1, a1, b1, *rest):
     arrived, (s2, got) = rest[: len(ops)], rest[len(ops) :]
 
     @pl.when(level_of(rows_n) > first + 2)
@@ -354,27 +348,39 @@
             loads + basis_work + work + [pltpu.SemaphoreType.DMA((5,))],
             "begin",
         )
+
+        def advance(t, down, left, state_in, coup_a, coup_b):
+            (part,) = call(
+                functools.partial(take_left, rows_n, first + t + 1),
+                [],
+                [left, state_in, coup_b],
+                [state],
+                [],
+                f"left{t}",
+            )
+            return call(
+                functools.partial(second, rows_n, first + t + 1),
+                [],
+                [down, *basis, part, coup_a],
+                [square],
+                work,
+                f"solve{t}",
+            )
+
         down = move(f0, up(0, 1))
         left = move(f0, right(0, 1))
         down_far = move(f0, up(0, 2))
         left_far = move(f0, right(0, 2))
         far0 = spread(ops0, cols_n, f0, "a", call)
-        *basis, s, a0, b0, a1, b1 = call(
+        *basis, s, a0, b0, a1, b1, a2, b2 = call(
             functools.partial(prepare, rows_n, first),
             [rhs, a_c, b_c, u, v, a_vals, b_vals],
             [],
-            basis_shapes + [state] + [square] * 4,
+            basis_shapes + [state] + [square] * 6,
             loads[1:] + [pltpu.SemaphoreType.DMA((9,))],
             "prepare",
         )
-        (f1,) = call(
-            functools.partial(second, rows_n, first),
-            [],
-            [down, left, *basis, s, a0, b0],
-            [square],
-            work,
-            "second",
-        )
+        (f1,) = advance(0, down, left, s, a0, b0)
         down = move(f1, up(1, 1))
         left = move(f1, right(1, 1))
         (s1,) = call(
@@ -386,36 +392,22 @@
             "third_early",
         )
         far1 = spread(ops1, cols_n, f1, "b", call)
-        (f2,) = call(
-            functools.partial(third, rows_n, first),
-            [],
-            [down, left, *basis, s1, a1, b1],
-            [square],
-            work,
-            "third",
-        )
-        s1, a1, b1, a2, b2 = call(
-            functools.partial(middle, rows_n, cols_n, first, ops0),
-            [rhs, a_c, b_c],
-            far0,
-            [state] + [square] * 4,
-            [pltpu.VMEM((n, n), full)] + [pltpu.VMEM((n, n), half)] * 3 + [pltpu.SemaphoreType.DMA((7,))],
-            "middle",
-        )
-        (s2,) = call(
-            functools.partial(middle_late, rows_n, cols_n, first, ops1),
-            [],
-            [s1, a1, b1, *far1],
-            [state],
-            [pltpu.VMEM((n, n), half)],
-            "middle_late",
-        )
+        (f2,) = advance(1, down, left, s1, a1, b1)
+        for k, (ops, far, a, b) in enumerate(((ops0, far0, a0, b0), (ops1, far1, a1, b1))):
+            (s,) = call(
+                functools.partial(middle, rows_n, cols_n, first, ops),
+                [],
+                [s, a, b, *far],
+                [state],
+                [pltpu.VMEM((n, n), half)],
+                f"middle{k}",
+            )
         lasts = spread(ops2, cols_n, f2, "c", call)
         sent = [k for k, op in enumerate(ops2) if any(kind == "down" for _, _, kind, _ in op)]
         (s3,) = call(
             functools.partial(downs, cols_n, first, rows_n, [ops2[k] for k in sent]),
             [],
-            [s2, a2, *[lasts[k] for k in sent]],
+            [s, a2, *[lasts[k] for k in sent]],
             [state],
             [pltpu.VMEM((n, n), half)],
             "downs",

time: 42.1 us -> 43.4 us (1.031)
  waiting for transfers between devices: 17.4 us -> 18.7 us
    ppermute x18, waiting for transfers between devices: 17.4 us -> 18.7 us  [move(): return lax.ppermute(value, AXES, pairs)]
    pallas_call x12 -> x14, Pallas kernels: 5.15 us -> 5.12 us  [call(): pl.pallas_call(kernel, out_shape=outs, in_specs=[FAR_SPEC] * len(far) + [...]
where the time goes in v3:
time: 43.4 us; the launch traced here: 43.1 us
  waiting for transfers between devices  18.7 us (43%)
  starting transfers between devices  18.3 us (42%)
  Pallas kernels  5.12 us (12%)
  between operations  0.99 us (2%)
    ppermute x18, waiting for transfers between devices, move(): return lax.ppermute(value, AXES, pairs)  18.7 us
    ppermute x18, starting transfers between devices, move(): return lax.ppermute(value, AXES, pairs)  18.3 us
    pallas_call x14, Pallas kernels, call(): pl.pallas_call(kernel, out_shape=outs, in_specs=[FAR_SPEC] * len(far) + [...  5.12 us
  transfers between devices with their start and end apart: 18, of which 3 were waited for; matrix products, arithmetic and copies ran while one was open for 0% of the time, Pallas kernels for 9%

profile of v3, /device:TPU:16, one launch (start us, length us, event | category | flops | bytes accessed | tf_op | source)
XLA Modules:
  0.0 43.1 jit_solution(3624099260623365096)
XLA Ops:
  0.7 0.7 %collective-permute-start.1 = (bf16[384,384]{1,0:T(8,128)(2,1)S(1)}, bf16[384,384]{1,0:T(8,128)(2,1)S(1)}, u32[]{:S(2)}, u32[]{:S(2)}) collective-permute-start(bf16[384,384]{1,0:T(8,128)(2,1)S(1)} %shard_map.86.own.f0), channel_id=1, source_target_pairs={{1,2},{10,11},{19,20},{28,29}} | collective-permute-start | bytes 884744 | tf_op jit(solution)/shard_map/ppermute | solution.py:301
  1.4 0.7 %collective-permute-start = (bf16[384,384]{1,0:T(8,128)(2,1)S(1)}, bf16[384,384]{1,0:T(8,128)(2,1)S(1)}, u32[]{:S(2)}, u32[]{:S(2)}) collective-permute-start(bf16[384,384]{1,0:T(8,128)(2,1)S(1)} %shard_map.86.own.f0), channel_id=1, source_target_pairs={{10,2},{19,11},{28,20}} | collective-permute-start | bytes 884744 | tf_op jit(solution)/shard_map/ppermute | solution.py:301
  2.1 0.7 %collective-permute-start.4 = (bf16[384,384]{1,0:T(8,128)(2,1)S(1)}, bf16[384,384]{1,0:T(8,128)(2,1)S(1)}, u32[]{:S(2)}, u32[]{:S(2)}) collective-permute-start(bf16[384,384]{1,0:T(8,128)(2,1)S(1)} %shard_map.86.own.f0), channel_id=1, source_target_pairs={{19,3},{28,12}} | collective-permute-start | bytes 884744 | tf_op jit(solution)/shard_map/ppermute | solution.py:301
  2.8 0.7 %collective-permute-start.5 = (bf16[384,384]{1,0:T(8,128)(2,1)S(1)}, bf16[384,384]{1,0:T(8,128)(2,1)S(1)}, u32[]{:S(2)}, u32[]{:S(2)}) collective-permute-start(bf16[384,384]{1,0:T(8,128)(2,1)S(1)} %shard_map.86.own.f0), channel_id=1, source_target_pairs={{1,3},{10,12},{19,21},{28,30}} | collective-permute-start | bytes 884744 | tf_op jit(solution)/shard_map/ppermute | solution.py:301
  3.4 1.7 %shard_map.87 = (bf16[384,1152]{1,0:T(8,128)(2,1)S(1)}, bf16[384,1152]{1,0:T(8,128)(2,1)S(1)}, bf16[1152,384]{1,0:T(8,128)(2,1)S(1)}, bf16[384,1152]{1,0:T(8,128...) custom-call(f32[384,384]{1,0:T(8,128)} %rhs.3, ...), custom_call_target="tpu_custom_call" | custom-call | tf_op jit(solution)/shard_map/pallas_call | solution.py:333
  5.2 0.7 %collective-permute-start.3 = (bf16[384,384]{1,0:T(8,128)(2,1)S(1)}, bf16[384,384]{1,0:T(8,128)(2,1)S(1)}, u32[]{:S(2)}, u32[]{:S(2)}) collective-permute-start(bf16[384,384]{1,0:T(8,128)(2,1)S(1)} %shard_map.89.own.f1), channel_id=1, source_target_pairs={{2,3},{11,12},{20,21},{29,30}} | collective-permute-start | bytes 884744 | tf_op jit(solution)/shard_map/ppermute | solution.py:301
  5.9 0.7 %collective-permute-start.2 = (bf16[384,384]{1,0:T(8,128)(2,1)S(1)}, bf16[384,384]{1,0:T(8,128)(2,1)S(1)}, u32[]{:S(2)}, u32[]{:S(2)}) collective-permute-start(bf16[384,384]{1,0:T(8,128)(2,1)S(1)} %shard_map.89.own.f1), channel_id=1, source_target_pairs={{11,3},{20,12},{29,21}} | collective-permute-start | bytes 884744 | tf_op jit(solution)/shard_map/ppermute | solution.py:301
  6.6 0.7 %collective-permute-start.6 = (bf16[384,384]{1,0:T(8,128)(2,1)S(1)}, bf16[384,384]{1,0:T(8,128)(2,1)S(1)}, u32[]{:S(2)}, u32[]{:S(2)}) collective-permute-start(bf16[384,384]{1,0:T(8,128)(2,1)S(1)} %shard_map.86.own.f0), channel_id=1, source_target_pairs={{1,6},{10,14},{19,22},{28,31}} | collective-permute-start | bytes 884744 | tf_op jit(solution)/shard_map/ppermute | solution.py:301
  7.3 1.3 %collective-permute-start.7 = (bf16[384,384]{1,0:T(8,128)(2,1)S(1)}, bf16[384,384]{1,0:T(8,128)(2,1)S(1)}, u32[]{:S(2)}, u32[]{:S(2)}) collective-permute-start(bf16[384,384]{1,0:T(8,128)(2,1)S(1)} %shard_map.86.own.f0), channel_id=1, source_target_pairs={{1,5},{10,13},{28,4}} | collective-permute-start | bytes 884744 | tf_op jit(solution)/shard_map/ppermute | solution.py:301
  8.6 1.3 %collective-permute-start.10 = (bf16[384,384]{1,0:T(8,128)(2,1)S(1)}, bf16[384,384]{1,0:T(8,128)(2,1)S(1)}, u32[]{:S(2)}, u32[]{:S(2)}) collective-permute-start(bf16[384,384]{1,0:T(8,128)(2,1)S(1)} %shard_map.89.own.f1), channel_id=1, source_target_pairs={{2,4},{11,13},{29,5}} | collective-permute-start | bytes 884744 | tf_op jit(solution)/shard_map/ppermute | solution.py:301
  9.9 0.7 %collective-permute-start.9 = (bf16[384,384]{1,0:T(8,128)(2,1)S(1)}, bf16[384,384]{1,0:T(8,128)(2,1)S(1)}, u32[]{:S(2)}, u32[]{:S(2)}) collective-permute-start(bf16[384,384]{1,0:T(8,128)(2,1)S(1)} %shard_map.89.own.f1), channel_id=1, source_target_pairs={{2,6},{11,14},{20,22},{29,31}} | collective-permute-start | bytes 884744 | tf_op jit(solution)/shard_map/ppermute | solution.py:301
  10.7 0.7 %collective-permute-start.13 = (bf16[384,384]{1,0:T(8,128)(2,1)S(1)}, bf16[384,384]{1,0:T(8,128)(2,1)S(1)}, u32[]{:S(2)}, u32[]{:S(2)}) collective-permute-start(bf16[384,384]{1,0:T(8,128)(2,1)S(1)} %shard_map.92.own.f2), channel_id=1, source_target_pairs={{3,7},{12,15},{21,23},{30,6}} | collective-permute-start | bytes 884744 | tf_op jit(solution)/shard_map/ppermute | solution.py:301
  11.4 1.3 %collective-permute-start.14 = (bf16[384,384]{1,0:T(8,128)(2,1)S(1)}, bf16[384,384]{1,0:T(8,128)(2,1)S(1)}, u32[]{:S(2)}, u32[]{:S(2)}) collective-permute-start(bf16[384,384]{1,0:T(8,128)(2,1)S(1)} %shard_map.92.own.f2), channel_id=1, source_target_pairs={{3,4},{21,5},{30,14},{12,13}} | collective-permute-start | bytes 884744 | tf_op jit(solution)/shard_map/ppermute | solution.py:301
  12.7 13.1 %collective-permute-done.7.rest_1_ = bf16[384,384]{1,0:T(8,128)(2,1)S(1)} collective-permute-done((bf16[384,384]{1,0:T(8,128)(2,1)S(1)}, bf16[384,384]{1,0:T(8,128)(2,1)S(1)}, u32[]{:S(2)}, u32[]{:S(2)}) %collective-permute-start.7) | collective-permute-done | bytes 294944 | tf_op jit(solution)/shard_map/ppermute | solution.py:301
  25.8 1.3 %collective-permute-start.8 = (bf16[384,384]{1,0:T(8,128)(2,1)S(1)}, bf16[384,384]{1,0:T(8,128)(2,1)S(1)}, u32[]{:S(2)}, u32[]{:S(2)}) collective-permute-start(bf16[384,384]{1,0:T(8,128)(2,1)S(1)} %shard_map.93), channel_id=1, source_target_pairs={{6,7},{14,15},{22,23},{5,4}} | collective-permute-start | bytes 884744 | tf_op jit(solution)/shard_map/ppermute | solution.py:301
  27.1 1.3 %collective-permute-start.11 = (bf16[384,384]{1,0:T(8,128)(2,1)S(1)}, bf16[384,384]{1,0:T(8,128)(2,1)S(1)}, u32[]{:S(2)}, u32[]{:S(2)}) collective-permute-start(bf16[384,384]{1,0:T(8,128)(2,1)S(1)} %shard_map.89.own.f1), channel_id=1, source_target_pairs={{20,4},{29,13}} | collective-permute-start | bytes 884744 | tf_op jit(solution)/shard_map/ppermute | solution.py:301
  28.4 2.5 %collective-permute-start.12 = (bf16[384,384]{1,0:T(8,128)(2,1)S(1)}, bf16[384,384]{1,0:T(8,128)(2,1)S(1)}, u32[]{:S(2)}, u32[]{:S(2)}) collective-permute-start(bf16[384,384]{1,0:T(8,128)(2,1)S(1)} %shard_map.95), channel_id=1, source_target_pairs={{6,7},{14,15},{22,23},{4,5}} | collective-permute-start | bytes 884744 | tf_op jit(solution)/shard_map/ppermute | solution.py:301
  30.9 1.3 %collective-permute-start.15 = (bf16[384,384]{1,0:T(8,128)(2,1)S(1)}, bf16[384,384]{1,0:T(8,128)(2,1)S(1)}, u32[]{:S(2)}, u32[]{:S(2)}) collective-permute-start(bf16[384,384]{1,0:T(8,128)(2,1)S(1)} %shard_map.92.own.f2), channel_id=1, source_target_pairs={{12,4},{21,13},{30,22}} | collective-permute-start | bytes 884744 | tf_op jit(solution)/shard_map/ppermute | solution.py:301
  32.2 3.2 %collective-permute-done.14.rest_1_ = bf16[384,384]{1,0:T(8,128)(2,1)S(1)} collective-permute-done((bf16[384,384]{1,0:T(8,128)(2,1)S(1)}, bf16[384,384]{1,0:T(8,128)(2,1)S(1)}, u32[]{:S(2)}, u32[]{:S(2)}) %collective-permute-start.14) | collective-permute-done | bytes 294944 | tf_op jit(solution)/shard_map/ppermute | solution.py:301
  36.2 1.3 %collective-permute-start.17 = (bf16[384,384]{1,0:T(8,128)(2,1)S(1)}, bf16[384,384]{1,0:T(8,128)(2,1)S(1)}, u32[]{:S(2)}, u32[]{:S(2)}) collective-permute-start(bf16[384,384]{1,0:T(8,128)(2,1)S(1)} %shard_map.98), channel_id=1, source_target_pairs={{7,6},{15,14},{23,22},{4,5}} | collective-permute-start | bytes 884744 | tf_op jit(solution)/shard_map/ppermute | solution.py:301
  37.5 0.8 %shard_map.94.s1 = f32[384,384]{1,0:T(8,128)S(1)} custom-call(f32[384,384]{1,0:T(8,128)S(1)} %get-tuple-element.19.s.s1, bf16[384,384]{1,0:T(8,128)(2,1)S(1)} %get-tuple-element.21.coup_a.a0.a1, bf16[384,384]{1,0:T(8,128)(2,1)S(1)} %get-tuple-element.20.coup_b.b0.b1, bf16[384,384]{1,0:T(8,128)(2,1)S(1)} %collective-permute-done.6.rest_0_, ...), custom_call_target="tpu_custom_call" | custom-call | tf_op jit(solution)/shard_map/pallas_call | solution.py:333
  38.3 0.8 %shard_map.96.s2 = f32[384,384]{1,0:T(8,128)S(1)} custom-call(f32[384,384]{1,0:T(8,128)S(1)} %shard_map.94.s1, bf16[384,384]{1,0:T(8,128)(2,1)S(1)} %get-tuple-element.23.coup_a.a1, bf16[384,384]{1,0:T(8,128)(2,1)S(1)} %get-tuple-element.22.coup_b.b1, bf16[384,384]{1,0:T(8,128)(2,1)S(1)} %collective-permute-done.9.rest_0_, ...), custom_call_target="tpu_custom_call" | custom-call | tf_op jit(solution)/shard_map/pallas_call | solution.py:333
  39.1 2.4 %collective-permute-done.15.rest_2_ = bf16[384,384]{1,0:T(8,128)(2,1)S(1)} collective-permute-done((bf16[384,384]{1,0:T(8,128)(2,1)S(1)}, bf16[384,384]{1,0:T(8,128)(2,1)S(1)}, u32[]{:S(2)}, u32[]{:S(2)}) %collective-permute-start.15) | collective-permute-done | bytes 294944 | tf_op jit(solution)/shard_map/ppermute | solution.py:301
  41.9 1.2 %shard_map.99 = (bf16[384,384]{1,0:T(8,128)(2,1)}, f32[384,384]{1,0:T(8,128)}) custom-call(bf16[384,384]{1,0:T(8,128)(2,1)S(1)} %shard_map.86.own.f0, bf16[384,384]{1,0:T(8,128)(2,1)S(1)} %shard_map.89.own.f1, bf16[384,384]{1,0:T(8,128)(2,1)S(1)} %shard_map.92.own.f2, f32[384,384]{1,0:T(8,128)S(1)} %shard_map.97.s3, ...), custom_call_target="tpu_custom_call" | custom-call | tf_op jit(solution)/shard_map/pallas_call | solution.py:333
  (26 shorter events, 1.4 us)
Async XLA Ops:
  0.7 4.4 %collective-permute-start.1 = (bf16[384,384]{1,0:T(8,128)(2,1)S(1)}, bf16[384,384]{1,0:T(8,128)(2,1)S(1)}, u32[]{:S(2)}, u32[]{:S(2)}) collective-permute-start(bf16[384,384]{1,0:T(8,128)(2,1)S(1)} %shard_map.86.own.f0), channel_id=1, source_target_pairs={{1,2},{10,11},{19,20},{28,29}} | collective-permute-start | bytes 884744 | tf_op jit(solution)/shard_map/ppermute | solution.py:301
  1.4 3.8 %collective-permute-start = (bf16[384,384]{1,0:T(8,128)(2,1)S(1)}, bf16[384,384]{1,0:T(8,128)(2,1)S(1)}, u32[]{:S(2)}, u32[]{:S(2)}) collective-permute-start(bf16[384,384]{1,0:T(8,128)(2,1)S(1)} %shard_map.86.own.f0), channel_id=1, source_target_pairs={{10,2},{19,11},{28,20}} | collective-permute-start | bytes 884744 | tf_op jit(solution)/shard_map/ppermute | solution.py:301
  2.1 5.2 %collective-permute-start.4 = (bf16[384,384]{1,0:T(8,128)(2,1)S(1)}, bf16[384,384]{1,0:T(8,128)(2,1)S(1)}, u32[]{:S(2)}, u32[]{:S(2)}) collective-permute-start(bf16[384,384]{1,0:T(8,128)(2,1)S(1)} %shard_map.86.own.f0), channel_id=1, source_target_pairs={{19,3},{28,12}} | collective-permute-start | bytes 884744 | tf_op jit(solution)/shard_map/ppermute | solution.py:301
  2.8 5.8 %collective-permute-start.5 = (bf16[384,384]{1,0:T(8,128)(2,1)S(1)}, bf16[384,384]{1,0:T(8,128)(2,1)S(1)}, u32[]{:S(2)}, u32[]{:S(2)}) collective-permute-start(bf16[384,384]{1,0:T(8,128)(2,1)S(1)} %shard_map.86.own.f0), channel_id=1, source_target_pairs={{1,3},{10,12},{19,21},{28,30}} | collective-permute-start | bytes 884744 | tf_op jit(solution)/shard_map/ppermute | solution.py:301
  5.2 4.7 %collective-permute-start.3 = (bf16[384,384]{1,0:T(8,128)(2,1)S(1)}, bf16[384,384]{1,0:T(8,128)(2,1)S(1)}, u32[]{:S(2)}, u32[]{:S(2)}) collective-permute-start(bf16[384,384]{1,0:T(8,128)(2,1)S(1)} %shard_map.89.own.f1), channel_id=1, source_target_pairs={{2,3},{11,12},{20,21},{29,30}} | collective-permute-start | bytes 884744 | tf_op jit(solution)/shard_map/ppermute | solution.py:301
  5.9 4.7 %collective-permute-start.2 = (bf16[384,384]{1,0:T(8,128)(2,1)S(1)}, bf16[384,384]{1,0:T(8,128)(2,1)S(1)}, u32[]{:S(2)}, u32[]{:S(2)}) collective-permute-start(bf16[384,384]{1,0:T(8,128)(2,1)S(1)} %shard_map.89.own.f1), channel_id=1, source_target_pairs={{11,3},{20,12},{29,21}} | collective-permute-start | bytes 884744 | tf_op jit(solution)/shard_map/ppermute | solution.py:301
  6.6 4.8 %collective-permute-start.6 = (bf16[384,384]{1,0:T(8,128)(2,1)S(1)}, bf16[384,384]{1,0:T(8,128)(2,1)S(1)}, u32[]{:S(2)}, u32[]{:S(2)}) collective-permute-start(bf16[384,384]{1,0:T(8,128)(2,1)S(1)} %shard_map.86.own.f0), channel_id=1, source_target_pairs={{1,6},{10,14},{19,22},{28,31}} | collective-permute-start | bytes 884744 | tf_op jit(solution)/shard_map/ppermute | solution.py:301
  7.3 18.4 %collective-permute-start.7 = (bf16[384,384]{1,0:T(8,128)(2,1)S(1)}, bf16[384,384]{1,0:T(8,128)(2,1)S(1)}, u32[]{:S(2)}, u32[]{:S(2)}) collective-permute-start(bf16[384,384]{1,0:T(8,128)(2,1)S(1)} %shard_map.86.own.f0), channel_id=1, source_target_pairs={{1,5},{10,13},{28,4}} | collective-permute-start | bytes 884744 | tf_op jit(solution)/shard_map/ppermute | solution.py:301
  8.6 18.5 %collective-permute-start.10 = (bf16[384,384]{1,0:T(8,128)(2,1)S(1)}, bf16[384,384]{1,0:T(8,128)(2,1)S(1)}, u32[]{:S(2)}, u32[]{:S(2)}) collective-permute-start(bf16[384,384]{1,0:T(8,128)(2,1)S(1)} %shard_map.89.own.f1), channel_id=1, source_target_pairs={{2,4},{11,13},{29,5}} | collective-permute-start | bytes 884744 | tf_op jit(solution)/shard_map/ppermute | solution.py:301
  9.9 18.4 %collective-permute-start.9 = (bf16[384,384]{1,0:T(8,128)(2,1)S(1)}, bf16[384,384]{1,0:T(8,128)(2,1)S(1)}, u32[]{:S(2)}, u32[]{:S(2)}) collective-permute-start(bf16[384,384]{1,0:T(8,128)(2,1)S(1)} %shard_map.89.own.f1), channel_id=1, source_target_pairs={{2,6},{11,14},{20,22},{29,31}} | collective-permute-start | bytes 884744 | tf_op jit(solution)/shard_map/ppermute | solution.py:301
  10.7 20.2 %collective-permute-start.13 = (bf16[384,384]{1,0:T(8,128)(2,1)S(1)}, bf16[384,384]{1,0:T(8,128)(2,1)S(1)}, u32[]{:S(2)}, u32[]{:S(2)}) collective-permute-start(bf16[384,384]{1,0:T(8,128)(2,1)S(1)} %shard_map.92.own.f2), channel_id=1, source_target_pairs={{3,7},{12,15},{21,23},{30,6}} | collective-permute-start | bytes 884744 | tf_op jit(solution)/shard_map/ppermute | solution.py:301
  11.4 24.1 %collective-permute-start.14 = (bf16[384,384]{1,0:T(8,128)(2,1)S(1)}, bf16[384,384]{1,0:T(8,128)(2,1)S(1)}, u32[]{:S(2)}, u32[]{:S(2)}) collective-permute-start(bf16[384,384]{1,0:T(8,128)(2,1)S(1)} %shard_map.92.own.f2), channel_id=1, source_target_pairs={{3,4},{21,5},{30,14},{12,13}} | collective-permute-start | bytes 884744 | tf_op jit(solution)/shard_map/ppermute | solution.py:301
  25.8 10.4 %collective-permute-start.8 = (bf16[384,384]{1,0:T(8,128)(2,1)S(1)}, bf16[384,384]{1,0:T(8,128)(2,1)S(1)}, u32[]{:S(2)}, u32[]{:S(2)}) collective-permute-start(bf16[384,384]{1,0:T(8,128)(2,1)S(1)} %shard_map.93), channel_id=1, source_target_pairs={{6,7},{14,15},{22,23},{5,4}} | collective-permute-start | bytes 884744 | tf_op jit(solution)/shard_map/ppermute | solution.py:301
  27.1 11.2 %collective-permute-start.11 = (bf16[384,384]{1,0:T(8,128)(2,1)S(1)}, bf16[384,384]{1,0:T(8,128)(2,1)S(1)}, u32[]{:S(2)}, u32[]{:S(2)}) collective-permute-start(bf16[384,384]{1,0:T(8,128)(2,1)S(1)} %shard_map.89.own.f1), channel_id=1, source_target_pairs={{20,4},{29,13}} | collective-permute-start | bytes 884744 | tf_op jit(solution)/shard_map/ppermute | solution.py:301
  28.4 9.9 %collective-permute-start.12 = (bf16[384,384]{1,0:T(8,128)(2,1)S(1)}, bf16[384,384]{1,0:T(8,128)(2,1)S(1)}, u32[]{:S(2)}, u32[]{:S(2)}) collective-permute-start(bf16[384,384]{1,0:T(8,128)(2,1)S(1)} %shard_map.95), channel_id=1, source_target_pairs={{6,7},{14,15},{22,23},{4,5}} | collective-permute-start | bytes 884744 | tf_op jit(solution)/shard_map/ppermute | solution.py:301
  30.9 10.6 %collective-permute-start.15 = (bf16[384,384]{1,0:T(8,128)(2,1)S(1)}, bf16[384,384]{1,0:T(8,128)(2,1)S(1)}, u32[]{:S(2)}, u32[]{:S(2)}) collective-permute-start(bf16[384,384]{1,0:T(8,128)(2,1)S(1)} %shard_map.92.own.f2), channel_id=1, source_target_pairs={{12,4},{21,13},{30,22}} | collective-permute-start | bytes 884744 | tf_op jit(solution)/shard_map/ppermute | solution.py:301
  35.5 6.4 %collective-permute-start.16 = (bf16[384,384]{1,0:T(8,128)(2,1)S(1)}, bf16[384,384]{1,0:T(8,128)(2,1)S(1)}, u32[]{:S(2)}, u32[]{:S(2)}) collective-permute-start(bf16[384,384]{1,0:T(8,128)(2,1)S(1)} %shard_map.92.own.f2), channel_id=1, source_target_pairs={{30,31}} | collective-permute-start | bytes 884744 | tf_op jit(solution)/shard_map/ppermute | solution.py:301
  36.2 5.7 %collective-permute-start.17 = (bf16[384,384]{1,0:T(8,128)(2,1)S(1)}, bf16[384,384]{1,0:T(8,128)(2,1)S(1)}, u32[]{:S(2)}, u32[]{:S(2)}) collective-permute-start(bf16[384,384]{1,0:T(8,128)(2,1)S(1)} %shard_map.98), channel_id=1, source_target_pairs={{7,6},{15,14},{23,22},{4,5}} | collective-permute-start | bytes 884744 | tf_op jit(solution)/shard_map/ppermute | solution.py:301

commit v4 on v3

--- a/solution.py
+++ b/solution.py
@@ -27,10 +27,11 @@
     ops, forwards = [], []
     while todo:
         used_from, used_to, op = set(), set(), []
-        waiting = {targets[0] for _, targets, kind in todo if kind == "down"}
+        busy = [source for source, _, _ in todo]
+        waiting = {targets[0]: busy.count(source) for source, targets, kind in todo if kind == "down"}
         for item in list(todo):
             source, targets, kind = item
-            for target in sorted(targets, key=lambda t: t in waiting):
+            for target in sorted(targets, key=lambda t: (waiting.get(t, 0), -t[1])):
                 if source not in used_from and target not in used_to:
                     used_from.add(source)
                     used_to.add(target)
@@ -42,6 +43,18 @@
     return ops + [forwards] if forwards else ops
 
 
+def with_near(ops, near):
+    far = {source[0]: target[1] // 2 != source[1] // 2 for source, target in near}
+    mixed = [[], []]
+    for source, target in near:
+        mixed[0 if far[source[0]] else 1].append((source, target, "near", None))
+    for edge in ops[0]:
+        mixed[1 if far.get(edge[0][0], False) else 0].append(edge)
+    ops = mixed + ops[1:]
+    came = {target: k for k, op in enumerate(ops) for _, target, kind, handed in op if kind == "left" and handed is None}
+    return [[edge if edge[3] is None else (*edge[:3], came[edge[0]]) for edge in op] for op in ops]
+
+
 def one_of(me, ids):
     hit = me < 0
     for each in sorted(ids):
@@ -84,11 +97,14 @@
     return lax.dot_general(a, b, (((1,), (1,)), ((), ())), preferred_element_type=jnp.float32)
 
 
-def solve(state, uk, utk, vk, vl, inverse, lhs, mid):
+def spectral(state, utk, vk, lhs, mid):
     put_left(lhs, split(state))
     part = dot(lhs[...], vk[...])
     put_right(mid, split(part))
-    part = dot(utk[...], mid[...]) * inverse[...]
+    return dot(utk[...], mid[...])
+
+
+def back(part, uk, vl, lhs, mid):
     put_left(lhs, split(part))
     part = dot_t(lhs[...], vl[...])
     put_right(mid, split(part))
@@ -139,10 +155,11 @@
             move.wait()
         set_left_basis(u, uk, utk)
         set_inverse(inverse, av, bv)
-        f0[...] = solve(s[...], uk, utk, vk, vl, inverse, lhs, mid)
-
-
-def prepare(rows_n, first, rhs, a_c, b_c, u_far, v_far, a_vals, b_vals, uk, utk, vk, vl, inverse, s, a0, b0, a1, b1, a2, b2, u, v, av, bv, sem):
+        part = spectral(s[...], utk, vk, lhs, mid) * inverse[...]
+        f0[...] = back(part, uk, vl, lhs, mid)
+
+
+def prepare(rows_n, first, rhs, a_c, b_c, u_far, v_far, a_vals, b_vals, uk, utk, vk, vl, inverse, coup, s, a0, b0, a1, b1, a2, b2, u, v, av, bv, both, sem):
     level = level_of(rows_n)
     terms = ((rhs, s), (a_c.at[0], a0), (b_c.at[0], b0), (a_c.at[1], a1), (b_c.at[1], b1))
 
@@ -158,6 +175,15 @@
         set_inverse(inverse, av, bv)
         for move in moves[4:]:
             move.wait()
+        n = u.shape[0]
+        for t, a in enumerate((a0, a1)):
+
+            @pl.when(level == first + 1 + t)
+            def _():
+                both[0:n] = a[...]
+                both[n:] = a[...]
+
+        put_left(coup, split(dot(utk[:, n:], both[...])))
 
     @pl.when(level > first + 2)
     def _():
@@ -165,17 +191,25 @@
             move.wait()
 
 
-def take_left(rows_n, level, left, s, coup_b, out):
+def take_left(rows_n, level, near, far, s, coup_b, utk, vk, out, lhs, mid):
+    even = lax.rem(lax.axis_index("col"), 2) == 0
+
     @pl.when(level_of(rows_n) == level)
     def _():
-        out[...] = s[...] - dot(left[...], coup_b[...])
-
-
-def second(rows_n, level, down, uk, utk, vk, vl, inverse, s, coup_a, f1, lhs, mid):
+        left = jnp.where(even, far[...], near[...])
+        out[...] = spectral(s[...] - dot(left, coup_b[...]), utk, vk, lhs, mid)
+
+
+def finish_solve(rows_n, level, down, y, coup, uk, vk, vl, inverse, f, lhs, mid):
     @pl.when(level_of(rows_n) == level)
     def _():
-        state = s[...] - dot(coup_a[...], down[...])
-        f1[...] = solve(state, uk, utk, vk, vl, inverse, lhs, mid)
+        n = y.shape[0]
+        lhs[:, 0:n] = down[...]
+        lhs[:, n : 2 * n] = down[...]
+        part = dot(lhs[:, 0 : 2 * n], vk[0 : 2 * n])
+        put_right(mid, split(part))
+        part = (y[...] - dot(coup[...], mid[...])) * inverse[...]
+        f[...] = back(part, uk, vl, lhs, mid)
 
 
 def third_early(rows_n, first, down, left, s, a0, b0, s1):
@@ -224,22 +258,27 @@
         subtract(cols_n, ops, arrived, got, s2, a2, None, s3, ("down",))
 
 
-def finish(rows_n, cols_n, first, ops, f0, f1, f2, s3, b2, *rest):
-    arrived, (out, nxt, got, mine, zeros, sem) = rest[: len(ops)], rest[len(ops) :]
+def publish(rows_n, first, f0, f1, f2, out, zeros, sem):
     level = level_of(rows_n)
+    for t, block in enumerate((f0, f1, f2)):
+
+        @pl.when(level == first + t)
+        def _():
+            pltpu.make_async_copy(block, out, sem).start()
+
+    @pl.when((level < first) | (level > first + 2))
+    def _():
+        zeros[...] = jnp.zeros(zeros.shape, zeros.dtype)
+        pltpu.make_async_copy(zeros, out, sem).start()
+
+    pltpu.make_async_copy(zeros, out, sem).wait()
+
+
+def finish(rows_n, cols_n, first, ops, s3, b2, *rest):
+    arrived, (nxt, got, mine, sem) = rest[: len(ops)], rest[len(ops) :]
     n = s3.shape[0]
     step = n // 3
-    active = level > first + 2
-    for t, block in enumerate((f0, f1, f2)):
-
-        @pl.when(level == first + t)
-        def _():
-            pltpu.make_async_copy(block, out, sem.at[3]).start()
-
-    @pl.when((level < first) | active)
-    def _():
-        zeros[...] = jnp.zeros(zeros.shape, zeros.dtype)
-        pltpu.make_async_copy(zeros, out, sem.at[3]).start()
+    active = level_of(rows_n) > first + 2
 
     @pl.when(jnp.logical_not(active))
     def _():
@@ -257,7 +296,6 @@
 
     for k in range(3):
         pltpu.make_async_copy(mine.at[pl.ds(k * step, step)], nxt.at[pl.ds(k * step, step)], sem.at[k]).wait()
-    pltpu.make_async_copy(zeros, out, sem.at[3]).wait()
 
 
 def relay(cols_n, choices, own, *rest):
@@ -306,11 +344,13 @@
     first = (rows_n + cols_n) // 2 - 2
     offset = first - rows_n + 1
     ops0 = plan(rows_n, cols_n, offset, 3, 3)
-    ops1 = plan(rows_n, cols_n, offset + 1, 2, 2)
     ops2 = plan(rows_n, cols_n, offset + 2, 1, 1)
 
     def owners(t):
         return [(i, i + offset + t) for i in range(rows_n) if 0 <= i + offset + t < cols_n]
+
+    near = [((i, j), (i, j + 1)) for i, j in owners(1) if j + 1 < cols_n]
+    ops1 = with_near(plan(rows_n, cols_n, offset + 1, 2, 2), near)
 
     def up(t, far):
         return [(i * cols_n + j, (i - far) * cols_n + j) for i, j in owners(t) if i >= far]
@@ -334,7 +374,7 @@
                 kernel,
                 out_shape=outs,
                 in_specs=[FAR_SPEC] * len(far) + [VMEM_SPEC] * len(near),
-                out_specs=[FAR_SPEC if name == "finish" else VMEM_SPEC] * len(outs),
+                out_specs=[FAR_SPEC if name in ("finish", "publish") else VMEM_SPEC] * len(outs),
                 scratch_shapes=scratch,
                 compiler_params=pltpu.CompilerParams(vmem_limit_bytes=24 << 20),
             )(*ins)
@@ -349,19 +389,20 @@
             "begin",
         )
 
-        def advance(t, down, left, state_in, coup_a, coup_b):
-            (part,) = call(
+        def advance(t, down, near, far, state_in, coup_b):
+            uk, utk, vk, vl, inverse = basis
+            (y,) = call(
                 functools.partial(take_left, rows_n, first + t + 1),
                 [],
-                [left, state_in, coup_b],
+                [near, far, state_in, coup_b, utk, vk],
                 [state],
-                [],
+                work,
                 f"left{t}",
             )
             return call(
-                functools.partial(second, rows_n, first + t + 1),
+                functools.partial(finish_solve, rows_n, first + t + 1),
                 [],
-                [down, *basis, part, coup_a],
+                [down, y, coup, uk, vk, vl, inverse],
                 [square],
                 work,
                 f"solve{t}",
@@ -372,17 +413,16 @@
         down_far = move(f0, up(0, 2))
         left_far = move(f0, right(0, 2))
         far0 = spread(ops0, cols_n, f0, "a", call)
-        *basis, s, a0, b0, a1, b1, a2, b2 = call(
+        *basis, coup, s, a0, b0, a1, b1, a2, b2 = call(
             functools.partial(prepare, rows_n, first),
             [rhs, a_c, b_c, u, v, a_vals, b_vals],
             [],
-            basis_shapes + [state] + [square] * 6,
-            loads[1:] + [pltpu.SemaphoreType.DMA((9,))],
+            basis_shapes + [wide, state] + [square] * 6,
+            loads[1:] + [pltpu.VMEM((2 * n, n), half), pltpu.SemaphoreType.DMA((9,))],
             "prepare",
         )
-        (f1,) = advance(0, down, left, s, a0, b0)
+        (f1,) = advance(0, down, left, left, s, b0)
         down = move(f1, up(1, 1))
-        left = move(f1, right(1, 1))
         (s1,) = call(
             functools.partial(third_early, rows_n, first),
             [],
@@ -392,7 +432,7 @@
             "third_early",
         )
         far1 = spread(ops1, cols_n, f1, "b", call)
-        (f2,) = advance(1, down, left, s1, a1, b1)
+        (f2,) = advance(1, down, far1[1], far1[0], s1, b1)
         for k, (ops, far, a, b) in enumerate(((ops0, far0, a0, b0), (ops1, far1, a1, b1))):
             (s,) = call(
                 functools.partial(middle, rows_n, cols_n, first, ops),
@@ -412,14 +452,23 @@
             [pltpu.VMEM((n, n), half)],
             "downs",
         )
-        return call(
+        (out,) = call(
+            functools.partial(publish, rows_n, first),
+            [],
+            [f0, f1, f2],
+            [square],
+            [pltpu.VMEM((n, n), half), pltpu.SemaphoreType.DMA],
+            "publish",
+        )
+        (nxt,) = call(
             functools.partial(finish, rows_n, cols_n, first, ops2),
             [],
-            [f0, f1, f2, s3, b2, *lasts],
-            [square, state],
-            [pltpu.VMEM((n, n), half), pltpu.VMEM((n, n), full), pltpu.VMEM((n, n), half), pltpu.SemaphoreType.DMA((4,))],
+            [s3, b2, *lasts],
+            [state],
+            [pltpu.VMEM((n, n), half), pltpu.VMEM((n, n), full), pltpu.SemaphoreType.DMA((3,))],
             "finish",
         )
+        return out, nxt
 
     placed = (
         P("row", "col"),

time: 43.4 us -> 49.5 us (1.14)
  the two profiles are of different devices: /device:TPU:16 before, /device:TPU:17 now
where the time goes in v4:
time: 49.5 us; the launch traced here: 49.1 us
  starting transfers between devices  31.7 us (64%)
  waiting for transfers between devices  10.9 us (22%)
  Pallas kernels  5.53 us (11%)
  between operations  1.01 us (2%)
    ppermute x18, starting transfers between devices, move(): return lax.ppermute(value, AXES, pairs)  31.7 us
    ppermute x18, waiting for transfers between devices, move(): return lax.ppermute(value, AXES, pairs)  10.9 us
    pallas_call x15, Pallas kernels, call(): pl.pallas_call(kernel, out_shape=outs, in_specs=[FAR_SPEC] * len(far) + [...  5.53 us
  transfers between devices with their start and end apart: 18, of which 2 were waited for; matrix products, arithmetic and copies ran while one was open for 0% of the time, Pallas kernels for 9%

profile of v4, /device:TPU:17, one launch (start us, length us, event | category | flops | bytes accessed | tf_op | source)
XLA Modules:
  0.0 49.1 jit_solution(12579320348475820859)
XLA Ops:
  0.7 0.7 %collective-permute-start.1 = (bf16[384,384]{1,0:T(8,128)(2,1)S(1)}, bf16[384,384]{1,0:T(8,128)(2,1)S(1)}, u32[]{:S(2)}, u32[]{:S(2)}) collective-permute-start(bf16[384,384]{1,0:T(8,128)(2,1)S(1)} %shard_map.86.f0.own), channel_id=1, source_target_pairs={{1,2},{10,11},{19,20},{28,29}} | collective-permute-start | bytes 884744 | tf_op jit(solution)/shard_map/ppermute | solution.py:339
  1.4 0.7 %collective-permute-start = (bf16[384,384]{1,0:T(8,128)(2,1)S(1)}, bf16[384,384]{1,0:T(8,128)(2,1)S(1)}, u32[]{:S(2)}, u32[]{:S(2)}) collective-permute-start(bf16[384,384]{1,0:T(8,128)(2,1)S(1)} %shard_map.86.f0.own), channel_id=1, source_target_pairs={{10,2},{19,11},{28,20}} | collective-permute-start | bytes 884744 | tf_op jit(solution)/shard_map/ppermute | solution.py:339
  2.1 0.7 %collective-permute-start.5 = (bf16[384,384]{1,0:T(8,128)(2,1)S(1)}, bf16[384,384]{1,0:T(8,128)(2,1)S(1)}, u32[]{:S(2)}, u32[]{:S(2)}) collective-permute-start(bf16[384,384]{1,0:T(8,128)(2,1)S(1)} %shard_map.86.f0.own), channel_id=1, source_target_pairs={{19,3},{28,12}} | collective-permute-start | bytes 884744 | tf_op jit(solution)/shard_map/ppermute | solution.py:339
  2.8 0.7 %collective-permute-start.6 = (bf16[384,384]{1,0:T(8,128)(2,1)S(1)}, bf16[384,384]{1,0:T(8,128)(2,1)S(1)}, u32[]{:S(2)}, u32[]{:S(2)}) collective-permute-start(bf16[384,384]{1,0:T(8,128)(2,1)S(1)} %shard_map.86.f0.own), channel_id=1, source_target_pairs={{1,3},{10,12},{19,21},{28,30}} | collective-permute-start | bytes 884744 | tf_op jit(solution)/shard_map/ppermute | solution.py:339
  3.4 1.7 %shard_map.87 = (bf16[384,1152]{1,0:T(8,128)(2,1)S(1)}, bf16[384,1152]{1,0:T(8,128)(2,1)S(1)}, bf16[1152,384]{1,0:T(8,128)(2,1)S(1)}, bf16[384,1152]{1,0:T(8,128...) custom-call(f32[384,384]{1,0:T(8,128)} %rhs.3, ...), custom_call_target="tpu_custom_call" | custom-call | tf_op jit(solution)/shard_map/pallas_call | solution.py:373
  5.2 0.7 %collective-permute-start.3 = (bf16[384,384]{1,0:T(8,128)(2,1)S(1)}, bf16[384,384]{1,0:T(8,128)(2,1)S(1)}, u32[]{:S(2)}, u32[]{:S(2)}) collective-permute-start(bf16[384,384]{1,0:T(8,128)(2,1)S(1)} %shard_map.89.f1.own), channel_id=1, source_target_pairs={{2,3},{20,21},{11,15},{29,31}} | collective-permute-start | bytes 884744 | tf_op jit(solution)/shard_map/ppermute | solution.py:339
  5.9 0.7 %collective-permute-start.4 = (bf16[384,384]{1,0:T(8,128)(2,1)S(1)}, bf16[384,384]{1,0:T(8,128)(2,1)S(1)}, u32[]{:S(2)}, u32[]{:S(2)}) collective-permute-start(bf16[384,384]{1,0:T(8,128)(2,1)S(1)} %shard_map.89.f1.own), channel_id=1, source_target_pairs={{11,12},{29,30},{2,7},{20,23}} | collective-permute-start | bytes 884744 | tf_op jit(solution)/shard_map/ppermute | solution.py:339
  6.6 0.7 %collective-permute-start.2 = (bf16[384,384]{1,0:T(8,128)(2,1)S(1)}, bf16[384,384]{1,0:T(8,128)(2,1)S(1)}, u32[]{:S(2)}, u32[]{:S(2)}) collective-permute-start(bf16[384,384]{1,0:T(8,128)(2,1)S(1)} %shard_map.89.f1.own), channel_id=1, source_target_pairs={{11,3},{20,12},{29,21}} | collective-permute-start | bytes 884744 | tf_op jit(solution)/shard_map/ppermute | solution.py:339
  7.3 0.7 %collective-permute-start.7 = (bf16[384,384]{1,0:T(8,128)(2,1)S(1)}, bf16[384,384]{1,0:T(8,128)(2,1)S(1)}, u32[]{:S(2)}, u32[]{:S(2)}) collective-permute-start(bf16[384,384]{1,0:T(8,128)(2,1)S(1)} %shard_map.86.f0.own), channel_id=1, source_target_pairs={{1,7},{10,15},{19,23},{28,31}} | collective-permute-start | bytes 884744 | tf_op jit(solution)/shard_map/ppermute | solution.py:339
  8.0 1.3 %collective-permute-start.8 = (bf16[384,384]{1,0:T(8,128)(2,1)S(1)}, bf16[384,384]{1,0:T(8,128)(2,1)S(1)}, u32[]{:S(2)}, u32[]{:S(2)}) collective-permute-start(bf16[384,384]{1,0:T(8,128)(2,1)S(1)} %shard_map.86.f0.own), channel_id=1, source_target_pairs={{1,5},{10,13},{28,4}} | collective-permute-start | bytes 884744 | tf_op jit(solution)/shard_map/ppermute | solution.py:339
  9.3 1.3 %collective-permute-start.10 = (bf16[384,384]{1,0:T(8,128)(2,1)S(1)}, bf16[384,384]{1,0:T(8,128)(2,1)S(1)}, u32[]{:S(2)}, u32[]{:S(2)}) collective-permute-start(bf16[384,384]{1,0:T(8,128)(2,1)S(1)} %shard_map.89.f1.own), channel_id=1, source_target_pairs={{2,4},{11,13},{29,5}} | collective-permute-start | bytes 884744 | tf_op jit(solution)/shard_map/ppermute | solution.py:339
  10.7 0.7 %collective-permute-start.13 = (bf16[384,384]{1,0:T(8,128)(2,1)S(1)}, bf16[384,384]{1,0:T(8,128)(2,1)S(1)}, u32[]{:S(2)}, u32[]{:S(2)}) collective-permute-start(bf16[384,384]{1,0:T(8,128)(2,1)S(1)} %shard_map.92.f2.own), channel_id=1, source_target_pairs={{3,7},{12,15},{21,23},{30,6}} | collective-permute-start | bytes 884744 | tf_op jit(solution)/shard_map/ppermute | solution.py:339
  11.4 1.3 %collective-permute-start.14 = (bf16[384,384]{1,0:T(8,128)(2,1)S(1)}, bf16[384,384]{1,0:T(8,128)(2,1)S(1)}, u32[]{:S(2)}, u32[]{:S(2)}) collective-permute-start(bf16[384,384]{1,0:T(8,128)(2,1)S(1)} %shard_map.92.f2.own), channel_id=1, source_target_pairs={{3,5},{12,4},{21,13},{30,14}} | collective-permute-start | bytes 884744 | tf_op jit(solution)/shard_map/ppermute | solution.py:339
  12.7 8.0 %collective-permute-done.8.rest_1_ = bf16[384,384]{1,0:T(8,128)(2,1)S(1)} collective-permute-done((bf16[384,384]{1,0:T(8,128)(2,1)S(1)}, bf16[384,384]{1,0:T(8,128)(2,1)S(1)}, u32[]{:S(2)}, u32[]{:S(2)}) %collective-permute-start.8) | collective-permute-done | bytes 294944 | tf_op jit(solution)/shard_map/ppermute | solution.py:339
  20.8 8.4 %collective-permute-start.9 = (bf16[384,384]{1,0:T(8,128)(2,1)S(1)}, bf16[384,384]{1,0:T(8,128)(2,1)S(1)}, u32[]{:S(2)}, u32[]{:S(2)}) collective-permute-start(bf16[384,384]{1,0:T(8,128)(2,1)S(1)} %shard_map.94), channel_id=1, source_target_pairs={{7,6},{15,14},{23,22},{5,4}} | collective-permute-start | bytes 884744 | tf_op jit(solution)/shard_map/ppermute | solution.py:339
  29.2 0.7 %collective-permute-start.11 = (bf16[384,384]{1,0:T(8,128)(2,1)S(1)}, bf16[384,384]{1,0:T(8,128)(2,1)S(1)}, u32[]{:S(2)}, u32[]{:S(2)}) collective-permute-start(bf16[384,384]{1,0:T(8,128)(2,1)S(1)} %shard_map.89.f1.own), channel_id=1, source_target_pairs={{20,4},{29,13}} | collective-permute-start | bytes 884744 | tf_op jit(solution)/shard_map/ppermute | solution.py:339
  30.0 1.3 %collective-permute-start.12 = (bf16[384,384]{1,0:T(8,128)(2,1)S(1)}, bf16[384,384]{1,0:T(8,128)(2,1)S(1)}, u32[]{:S(2)}, u32[]{:S(2)}) collective-permute-start(bf16[384,384]{1,0:T(8,128)(2,1)S(1)} %shard_map.96), channel_id=1, source_target_pairs={{7,6},{15,14},{23,22},{4,5}} | collective-permute-start | bytes 884744 | tf_op jit(solution)/shard_map/ppermute | solution.py:339
  31.3 1.3 %collective-permute-start.15 = (bf16[384,384]{1,0:T(8,128)(2,1)S(1)}, bf16[384,384]{1,0:T(8,128)(2,1)S(1)}, u32[]{:S(2)}, u32[]{:S(2)}) collective-permute-start(bf16[384,384]{1,0:T(8,128)(2,1)S(1)} %shard_map.92.f2.own), channel_id=1, source_target_pairs={{21,5},{30,22},{12,13}} | collective-permute-start | bytes 884744 | tf_op jit(solution)/shard_map/ppermute | solution.py:339
  32.6 2.9 %collective-permute-done.14.rest_1_ = bf16[384,384]{1,0:T(8,128)(2,1)S(1)} collective-permute-done((bf16[384,384]{1,0:T(8,128)(2,1)S(1)}, bf16[384,384]{1,0:T(8,128)(2,1)S(1)}, u32[]{:S(2)}, u32[]{:S(2)}) %collective-permute-start.14) | collective-permute-done | bytes 294944 | tf_op jit(solution)/shard_map/ppermute | solution.py:339
  35.4 0.7 %collective-permute-start.16 = (bf16[384,384]{1,0:T(8,128)(2,1)S(1)}, bf16[384,384]{1,0:T(8,128)(2,1)S(1)}, u32[]{:S(2)}, u32[]{:S(2)}) collective-permute-start(bf16[384,384]{1,0:T(8,128)(2,1)S(1)} %shard_map.92.f2.own), channel_id=1, source_target_pairs={{30,31}} | collective-permute-start | bytes 884744 | tf_op jit(solution)/shard_map/ppermute | solution.py:339
  36.2 9.3 %collective-permute-start.17 = (bf16[384,384]{1,0:T(8,128)(2,1)S(1)}, bf16[384,384]{1,0:T(8,128)(2,1)S(1)}, u32[]{:S(2)}, u32[]{:S(2)}) collective-permute-start(bf16[384,384]{1,0:T(8,128)(2,1)S(1)} %shard_map.99), channel_id=1, source_target_pairs={{7,6},{15,14},{23,22},{5,4}} | collective-permute-start | bytes 884744 | tf_op jit(solution)/shard_map/ppermute | solution.py:339
  45.5 0.8 %shard_map.93 = bf16[384,384]{1,0:T(8,128)(2,1)} custom-call(bf16[384,384]{1,0:T(8,128)(2,1)S(1)} %shard_map.86.f0.own, bf16[384,384]{1,0:T(8,128)(2,1)S(1)} %shard_map.89.f1.own, bf16[384,384]{1,0:T(8,128)(2,1)S(1)} %shard_map.92.f2.own), custom_call_target="tpu_custom_call" | custom-call | tf_op jit(solution)/shard_map/pallas_call | solution.py:373
  46.7 0.8 %shard_map.97.s2 = f32[384,384]{1,0:T(8,128)S(1)} custom-call(f32[384,384]{1,0:T(8,128)S(1)} %shard_map.95.s1, bf16[384,384]{1,0:T(8,128)(2,1)S(1)} %get-tuple-element.25.a1, bf16[384,384]{1,0:T(8,128)(2,1)S(1)} %get-tuple-element.24.coup_b.b1, bf16[384,384]{1,0:T(8,128)(2,1)S(1)} %collective-permute-done.4.far.rest_0_, ...), custom_call_target="tpu_custom_call" | custom-call | tf_op jit(solution)/shard_map/pallas_call | solution.py:373
  48.0 1.1 %shard_map.100 = f32[384,384]{1,0:T(8,128)} custom-call(f32[384,384]{1,0:T(8,128)S(1)} %shard_map.98.s3, bf16[384,384]{1,0:T(8,128)(2,1)S(1)} %get-tuple-element.27.b2, bf16[384,384]{1,0:T(8,128)(2,1)S(1)} %collective-permute-done.13.rest_0_, bf16[384,384]{1,0:T(8,128)(2,1)S(1)} %collective-permute-done.14.rest_1_, ...), custom_call_target="tpu_custom_call" | custom-call | tf_op jit(solution)/shard_map/pallas_call | solution.py:373
  (27 shorter events, 1.2 us)
Async XLA Ops:
  0.7 4.4 %collective-permute-start.1 = (bf16[384,384]{1,0:T(8,128)(2,1)S(1)}, bf16[384,384]{1,0:T(8,128)(2,1)S(1)}, u32[]{:S(2)}, u32[]{:S(2)}) collective-permute-start(bf16[384,384]{1,0:T(8,128)(2,1)S(1)} %shard_map.86.f0.own), channel_id=1, source_target_pairs={{1,2},{10,11},{19,20},{28,29}} | collective-permute-start | bytes 884744 | tf_op jit(solution)/shard_map/ppermute | solution.py:339
  1.4 3.8 %collective-permute-start = (bf16[384,384]{1,0:T(8,128)(2,1)S(1)}, bf16[384,384]{1,0:T(8,128)(2,1)S(1)}, u32[]{:S(2)}, u32[]{:S(2)}) collective-permute-start(bf16[384,384]{1,0:T(8,128)(2,1)S(1)} %shard_map.86.f0.own), channel_id=1, source_target_pairs={{10,2},{19,11},{28,20}} | collective-permute-start | bytes 884744 | tf_op jit(solution)/shard_map/ppermute | solution.py:339
  2.1 5.2 %collective-permute-start.5 = (bf16[384,384]{1,0:T(8,128)(2,1)S(1)}, bf16[384,384]{1,0:T(8,128)(2,1)S(1)}, u32[]{:S(2)}, u32[]{:S(2)}) collective-permute-start(bf16[384,384]{1,0:T(8,128)(2,1)S(1)} %shard_map.86.f0.own), channel_id=1, source_target_pairs={{19,3},{28,12}} | collective-permute-start | bytes 884744 | tf_op jit(solution)/shard_map/ppermute | solution.py:339
  2.8 5.2 %collective-permute-start.6 = (bf16[384,384]{1,0:T(8,128)(2,1)S(1)}, bf16[384,384]{1,0:T(8,128)(2,1)S(1)}, u32[]{:S(2)}, u32[]{:S(2)}) collective-permute-start(bf16[384,384]{1,0:T(8,128)(2,1)S(1)} %shard_map.86.f0.own), channel_id=1, source_target_pairs={{1,3},{10,12},{19,21},{28,30}} | collective-permute-start | bytes 884744 | tf_op jit(solution)/shard_map/ppermute | solution.py:339
  5.2 4.1 %collective-permute-start.3 = (bf16[384,384]{1,0:T(8,128)(2,1)S(1)}, bf16[384,384]{1,0:T(8,128)(2,1)S(1)}, u32[]{:S(2)}, u32[]{:S(2)}) collective-permute-start(bf16[384,384]{1,0:T(8,128)(2,1)S(1)} %shard_map.89.f1.own), channel_id=1, source_target_pairs={{2,3},{20,21},{11,15},{29,31}} | collective-permute-start | bytes 884744 | tf_op jit(solution)/shard_map/ppermute | solution.py:339
  5.9 4.7 %collective-permute-start.4 = (bf16[384,384]{1,0:T(8,128)(2,1)S(1)}, bf16[384,384]{1,0:T(8,128)(2,1)S(1)}, u32[]{:S(2)}, u32[]{:S(2)}) collective-permute-start(bf16[384,384]{1,0:T(8,128)(2,1)S(1)} %shard_map.89.f1.own), channel_id=1, source_target_pairs={{11,12},{29,30},{2,7},{20,23}} | collective-permute-start | bytes 884744 | tf_op jit(solution)/shard_map/ppermute | solution.py:339
  6.6 4.1 %collective-permute-start.2 = (bf16[384,384]{1,0:T(8,128)(2,1)S(1)}, bf16[384,384]{1,0:T(8,128)(2,1)S(1)}, u32[]{:S(2)}, u32[]{:S(2)}) collective-permute-start(bf16[384,384]{1,0:T(8,128)(2,1)S(1)} %shard_map.89.f1.own), channel_id=1, source_target_pairs={{11,3},{20,12},{29,21}} | collective-permute-start | bytes 884744 | tf_op jit(solution)/shard_map/ppermute | solution.py:339
  7.3 5.4 %collective-permute-start.7 = (bf16[384,384]{1,0:T(8,128)(2,1)S(1)}, bf16[384,384]{1,0:T(8,128)(2,1)S(1)}, u32[]{:S(2)}, u32[]{:S(2)}) collective-permute-start(bf16[384,384]{1,0:T(8,128)(2,1)S(1)} %shard_map.86.f0.own), channel_id=1, source_target_pairs={{1,7},{10,15},{19,23},{28,31}} | collective-permute-start | bytes 884744 | tf_op jit(solution)/shard_map/ppermute | solution.py:339
  8.0 12.7 %collective-permute-start.8 = (bf16[384,384]{1,0:T(8,128)(2,1)S(1)}, bf16[384,384]{1,0:T(8,128)(2,1)S(1)}, u32[]{:S(2)}, u32[]{:S(2)}) collective-permute-start(bf16[384,384]{1,0:T(8,128)(2,1)S(1)} %shard_map.86.f0.own), channel_id=1, source_target_pairs={{1,5},{10,13},{28,4}} | collective-permute-start | bytes 884744 | tf_op jit(solution)/shard_map/ppermute | solution.py:339
  9.3 20.6 %collective-permute-start.10 = (bf16[384,384]{1,0:T(8,128)(2,1)S(1)}, bf16[384,384]{1,0:T(8,128)(2,1)S(1)}, u32[]{:S(2)}, u32[]{:S(2)}) collective-permute-start(bf16[384,384]{1,0:T(8,128)(2,1)S(1)} %shard_map.89.f1.own), channel_id=1, source_target_pairs={{2,4},{11,13},{29,5}} | collective-permute-start | bytes 884744 | tf_op jit(solution)/shard_map/ppermute | solution.py:339
  10.7 20.6 %collective-permute-start.13 = (bf16[384,384]{1,0:T(8,128)(2,1)S(1)}, bf16[384,384]{1,0:T(8,128)(2,1)S(1)}, u32[]{:S(2)}, u32[]{:S(2)}) collective-permute-start(bf16[384,384]{1,0:T(8,128)(2,1)S(1)} %shard_map.92.f2.own), channel_id=1, source_target_pairs={{3,7},{12,15},{21,23},{30,6}} | collective-permute-start | bytes 884744 | tf_op jit(solution)/shard_map/ppermute | solution.py:339
  11.4 24.0 %collective-permute-start.14 = (bf16[384,384]{1,0:T(8,128)(2,1)S(1)}, bf16[384,384]{1,0:T(8,128)(2,1)S(1)}, u32[]{:S(2)}, u32[]{:S(2)}) collective-permute-start(bf16[384,384]{1,0:T(8,128)(2,1)S(1)} %shard_map.92.f2.own), channel_id=1, source_target_pairs={{3,5},{12,4},{21,13},{30,14}} | collective-permute-start | bytes 884744 | tf_op jit(solution)/shard_map/ppermute | solution.py:339
  20.8 15.4 %collective-permute-start.9 = (bf16[384,384]{1,0:T(8,128)(2,1)S(1)}, bf16[384,384]{1,0:T(8,128)(2,1)S(1)}, u32[]{:S(2)}, u32[]{:S(2)}) collective-permute-start(bf16[384,384]{1,0:T(8,128)(2,1)S(1)} %shard_map.94), channel_id=1, source_target_pairs={{7,6},{15,14},{23,22},{5,4}} | collective-permute-start | bytes 884744 | tf_op jit(solution)/shard_map/ppermute | solution.py:339
  29.2 17.5 %collective-permute-start.11 = (bf16[384,384]{1,0:T(8,128)(2,1)S(1)}, bf16[384,384]{1,0:T(8,128)(2,1)S(1)}, u32[]{:S(2)}, u32[]{:S(2)}) collective-permute-start(bf16[384,384]{1,0:T(8,128)(2,1)S(1)} %shard_map.89.f1.own), channel_id=1, source_target_pairs={{20,4},{29,13}} | collective-permute-start | bytes 884744 | tf_op jit(solution)/shard_map/ppermute | solution.py:339
  30.0 16.7 %collective-permute-start.12 = (bf16[384,384]{1,0:T(8,128)(2,1)S(1)}, bf16[384,384]{1,0:T(8,128)(2,1)S(1)}, u32[]{:S(2)}, u32[]{:S(2)}) collective-permute-start(bf16[384,384]{1,0:T(8,128)(2,1)S(1)} %shard_map.96), channel_id=1, source_target_pairs={{7,6},{15,14},{23,22},{4,5}} | collective-permute-start | bytes 884744 | tf_op jit(solution)/shard_map/ppermute | solution.py:339
  31.3 16.3 %collective-permute-start.15 = (bf16[384,384]{1,0:T(8,128)(2,1)S(1)}, bf16[384,384]{1,0:T(8,128)(2,1)S(1)}, u32[]{:S(2)}, u32[]{:S(2)}) collective-permute-start(bf16[384,384]{1,0:T(8,128)(2,1)S(1)} %shard_map.92.f2.own), channel_id=1, source_target_pairs={{21,5},{30,22},{12,13}} | collective-permute-start | bytes 884744 | tf_op jit(solution)/shard_map/ppermute | solution.py:339
  35.4 12.5 %collective-permute-start.16 = (bf16[384,384]{1,0:T(8,128)(2,1)S(1)}, bf16[384,384]{1,0:T(8,128)(2,1)S(1)}, u32[]{:S(2)}, u32[]{:S(2)}) collective-permute-start(bf16[384,384]{1,0:T(8,128)(2,1)S(1)} %shard_map.92.f2.own), channel_id=1, source_target_pairs={{30,31}} | collective-permute-start | bytes 884744 | tf_op jit(solution)/shard_map/ppermute | solution.py:339
  36.2 11.8 %collective-permute-start.17 = (bf16[384,384]{1,0:T(8,128)(2,1)S(1)}, bf16[384,384]{1,0:T(8,128)(2,1)S(1)}, u32[]{:S(2)}, u32[]{:S(2)}) collective-permute-start(bf16[384,384]{1,0:T(8,128)(2,1)S(1)} %shard_map.99), channel_id=1, source_target_pairs={{7,6},{15,14},{23,22},{5,4}} | collective-permute-start | bytes 884744 | tf_op jit(solution)/shard_map/ppermute | solution.py:339

commit v5 on v4

--- a/solution.py
+++ b/solution.py
@@ -43,18 +43,6 @@
     return ops + [forwards] if forwards else ops
 
 
-def with_near(ops, near):
-    far = {source[0]: target[1] // 2 != source[1] // 2 for source, target in near}
-    mixed = [[], []]
-    for source, target in near:
-        mixed[0 if far[source[0]] else 1].append((source, target, "near", None))
-    for edge in ops[0]:
-        mixed[1 if far.get(edge[0][0], False) else 0].append(edge)
-    ops = mixed + ops[1:]
-    came = {target: k for k, op in enumerate(ops) for _, target, kind, handed in op if kind == "left" and handed is None}
-    return [[edge if edge[3] is None else (*edge[:3], came[edge[0]]) for edge in op] for op in ops]
-
-
 def one_of(me, ids):
     hit = me < 0
     for each in sorted(ids):
@@ -191,13 +179,10 @@
             move.wait()
 
 
-def take_left(rows_n, level, near, far, s, coup_b, utk, vk, out, lhs, mid):
-    even = lax.rem(lax.axis_index("col"), 2) == 0
-
+def take_left(rows_n, level, left, s, coup_b, utk, vk, out, lhs, mid):
     @pl.when(level_of(rows_n) == level)
     def _():
-        left = jnp.where(even, far[...], near[...])
-        out[...] = spectral(s[...] - dot(left, coup_b[...]), utk, vk, lhs, mid)
+        out[...] = spectral(s[...] - dot(left[...], coup_b[...]), utk, vk, lhs, mid)
 
 
 def finish_solve(rows_n, level, down, y, coup, uk, vk, vl, inverse, f, lhs, mid):
@@ -344,13 +329,11 @@
     first = (rows_n + cols_n) // 2 - 2
     offset = first - rows_n + 1
     ops0 = plan(rows_n, cols_n, offset, 3, 3)
+    ops1 = plan(rows_n, cols_n, offset + 1, 2, 2)
     ops2 = plan(rows_n, cols_n, offset + 2, 1, 1)
 
     def owners(t):
         return [(i, i + offset + t) for i in range(rows_n) if 0 <= i + offset + t < cols_n]
-
-    near = [((i, j), (i, j + 1)) for i, j in owners(1) if j + 1 < cols_n]
-    ops1 = with_near(plan(rows_n, cols_n, offset + 1, 2, 2), near)
 
     def up(t, far):
         return [(i * cols_n + j, (i - far) * cols_n + j) for i, j in owners(t) if i >= far]
@@ -389,12 +372,12 @@
             "begin",
         )
 
-        def advance(t, down, near, far, state_in, coup_b):
+        def advance(t, down, left, state_in, coup_b):
             uk, utk, vk, vl, inverse = basis
             (y,) = call(
                 functools.partial(take_left, rows_n, first + t + 1),
                 [],
-                [near, far, state_in, coup_b, utk, vk],
+                [left, state_in, coup_b, utk, vk],
                 [state],
                 work,
                 f"left{t}",
@@ -421,8 +404,9 @@
             loads[1:] + [pltpu.VMEM((2 * n, n), half), pltpu.SemaphoreType.DMA((9,))],
             "prepare",
         )
-        (f1,) = advance(0, down, left, left, s, b0)
+        (f1,) = advance(0, down, left, s, b0)
         down = move(f1, up(1, 1))
+        left = move(f1, right(1, 1))
         (s1,) = call(
             functools.partial(third_early, rows_n, first),
             [],
@@ -432,7 +416,7 @@
             "third_early",
         )
         far1 = spread(ops1, cols_n, f1, "b", call)
-        (f2,) = advance(1, down, far1[1], far1[0], s1, b1)
+        (f2,) = advance(1, down, left, s1, b1)
         for k, (ops, far, a, b) in enumerate(((ops0, far0, a0, b0), (ops1, far1, a1, b1))):
             (s,) = call(
                 functools.partial(middle, rows_n, cols_n, first, ops),

time: 49.5 us -> 44.3 us (0.89)
  starting transfers between devices: 31.7 us -> 27.4 us
  waiting for transfers between devices: 10.9 us -> 10.1 us
    ppermute x18, starting transfers between devices: 31.7 us -> 27.4 us  [move(): return lax.ppermute(value, AXES, pairs)]
    ppermute x18, waiting for transfers between devices: 10.9 us -> 10.1 us  [move(): return lax.ppermute(value, AXES, pairs)]
  transfers between devices with their start and end apart: 18 -> 18, of which waited for: 2 -> 2; matrix products, arithmetic and copies ran while one was open for 0% -> 0% of each run, Pallas kernels for 9% -> 10%
where the time goes in v5:
time: 44.3 us; the launch traced here: 44 us
  starting transfers between devices  27.4 us (62%)
  waiting for transfers between devices  10.1 us (23%)
  Pallas kernels  5.51 us (12%)
  between operations  1.01 us (2%)
    ppermute x18, starting transfers between devices, move(): return lax.ppermute(value, AXES, pairs)  27.4 us
    ppermute x18, waiting for transfers between devices, move(): return lax.ppermute(value, AXES, pairs)  10.1 us
    pallas_call x15, Pallas kernels, call(): pl.pallas_call(kernel, out_shape=outs, in_specs=[FAR_SPEC] * len(far) + [...  5.51 us
  transfers between devices with their start and end apart: 18, of which 2 were waited for; matrix products, arithmetic and copies ran while one was open for 0% of the time, Pallas kernels for 10%

profile of v5, /device:TPU:17, one launch (start us, length us, event | category | flops | bytes accessed | tf_op | source)
XLA Modules:
  0.0 44.0 jit_solution(15128762420838228003)
XLA Ops:
  0.7 0.7 %collective-permute-start.1 = (bf16[384,384]{1,0:T(8,128)(2,1)S(1)}, bf16[384,384]{1,0:T(8,128)(2,1)S(1)}, u32[]{:S(2)}, u32[]{:S(2)}) collective-permute-start(bf16[384,384]{1,0:T(8,128)(2,1)S(1)} %shard_map.86.f0.own), channel_id=1, source_target_pairs={{1,2},{10,11},{19,20},{28,29}} | collective-permute-start | bytes 884744 | tf_op jit(solution)/shard_map/ppermute | solution.py:324
  1.4 0.7 %collective-permute-start = (bf16[384,384]{1,0:T(8,128)(2,1)S(1)}, bf16[384,384]{1,0:T(8,128)(2,1)S(1)}, u32[]{:S(2)}, u32[]{:S(2)}) collective-permute-start(bf16[384,384]{1,0:T(8,128)(2,1)S(1)} %shard_map.86.f0.own), channel_id=1, source_target_pairs={{10,2},{19,11},{28,20}} | collective-permute-start | bytes 884744 | tf_op jit(solution)/shard_map/ppermute | solution.py:324
  2.1 0.7 %collective-permute-start.4 = (bf16[384,384]{1,0:T(8,128)(2,1)S(1)}, bf16[384,384]{1,0:T(8,128)(2,1)S(1)}, u32[]{:S(2)}, u32[]{:S(2)}) collective-permute-start(bf16[384,384]{1,0:T(8,128)(2,1)S(1)} %shard_map.86.f0.own), channel_id=1, source_target_pairs={{19,3},{28,12}} | collective-permute-start | bytes 884744 | tf_op jit(solution)/shard_map/ppermute | solution.py:324
  2.8 0.7 %collective-permute-start.5 = (bf16[384,384]{1,0:T(8,128)(2,1)S(1)}, bf16[384,384]{1,0:T(8,128)(2,1)S(1)}, u32[]{:S(2)}, u32[]{:S(2)}) collective-permute-start(bf16[384,384]{1,0:T(8,128)(2,1)S(1)} %shard_map.86.f0.own), channel_id=1, source_target_pairs={{1,3},{10,12},{19,21},{28,30}} | collective-permute-start | bytes 884744 | tf_op jit(solution)/shard_map/ppermute | solution.py:324
  3.4 1.7 %shard_map.87 = (bf16[384,1152]{1,0:T(8,128)(2,1)S(1)}, bf16[384,1152]{1,0:T(8,128)(2,1)S(1)}, bf16[1152,384]{1,0:T(8,128)(2,1)S(1)}, bf16[384,1152]{1,0:T(8,128...) custom-call(f32[384,384]{1,0:T(8,128)} %rhs.3, ...), custom_call_target="tpu_custom_call" | custom-call | tf_op jit(solution)/shard_map/pallas_call | solution.py:356
  5.2 0.7 %collective-permute-start.3 = (bf16[384,384]{1,0:T(8,128)(2,1)S(1)}, bf16[384,384]{1,0:T(8,128)(2,1)S(1)}, u32[]{:S(2)}, u32[]{:S(2)}) collective-permute-start(bf16[384,384]{1,0:T(8,128)(2,1)S(1)} %shard_map.89.f1.own), channel_id=1, source_target_pairs={{2,3},{11,12},{20,21},{29,30}} | collective-permute-start | bytes 884744 | tf_op jit(solution)/shard_map/ppermute | solution.py:324
  5.9 0.7 %collective-permute-start.2 = (bf16[384,384]{1,0:T(8,128)(2,1)S(1)}, bf16[384,384]{1,0:T(8,128)(2,1)S(1)}, u32[]{:S(2)}, u32[]{:S(2)}) collective-permute-start(bf16[384,384]{1,0:T(8,128)(2,1)S(1)} %shard_map.89.f1.own), channel_id=1, source_target_pairs={{11,3},{20,12},{29,21}} | collective-permute-start | bytes 884744 | tf_op jit(solution)/shard_map/ppermute | solution.py:324
  6.6 0.7 %collective-permute-start.6 = (bf16[384,384]{1,0:T(8,128)(2,1)S(1)}, bf16[384,384]{1,0:T(8,128)(2,1)S(1)}, u32[]{:S(2)}, u32[]{:S(2)}) collective-permute-start(bf16[384,384]{1,0:T(8,128)(2,1)S(1)} %shard_map.86.f0.own), channel_id=1, source_target_pairs={{1,7},{10,15},{19,23},{28,31}} | collective-permute-start | bytes 884744 | tf_op jit(solution)/shard_map/ppermute | solution.py:324
  7.3 1.3 %collective-permute-start.7 = (bf16[384,384]{1,0:T(8,128)(2,1)S(1)}, bf16[384,384]{1,0:T(8,128)(2,1)S(1)}, u32[]{:S(2)}, u32[]{:S(2)}) collective-permute-start(bf16[384,384]{1,0:T(8,128)(2,1)S(1)} %shard_map.86.f0.own), channel_id=1, source_target_pairs={{1,5},{10,13},{28,4}} | collective-permute-start | bytes 884744 | tf_op jit(solution)/shard_map/ppermute | solution.py:324
  8.6 1.3 %collective-permute-start.10 = (bf16[384,384]{1,0:T(8,128)(2,1)S(1)}, bf16[384,384]{1,0:T(8,128)(2,1)S(1)}, u32[]{:S(2)}, u32[]{:S(2)}) collective-permute-start(bf16[384,384]{1,0:T(8,128)(2,1)S(1)} %shard_map.89.f1.own), channel_id=1, source_target_pairs={{2,4},{11,13},{29,5}} | collective-permute-start | bytes 884744 | tf_op jit(solution)/shard_map/ppermute | solution.py:324
  9.9 0.7 %collective-permute-start.9 = (bf16[384,384]{1,0:T(8,128)(2,1)S(1)}, bf16[384,384]{1,0:T(8,128)(2,1)S(1)}, u32[]{:S(2)}, u32[]{:S(2)}) collective-permute-start(bf16[384,384]{1,0:T(8,128)(2,1)S(1)} %shard_map.89.f1.own), channel_id=1, source_target_pairs={{2,7},{11,15},{20,23},{29,31}} | collective-permute-start | bytes 884744 | tf_op jit(solution)/shard_map/ppermute | solution.py:324
  10.7 0.7 %collective-permute-start.13 = (bf16[384,384]{1,0:T(8,128)(2,1)S(1)}, bf16[384,384]{1,0:T(8,128)(2,1)S(1)}, u32[]{:S(2)}, u32[]{:S(2)}) collective-permute-start(bf16[384,384]{1,0:T(8,128)(2,1)S(1)} %shard_map.92.f2.own), channel_id=1, source_target_pairs={{3,7},{12,15},{21,23},{30,6}} | collective-permute-start | bytes 884744 | tf_op jit(solution)/shard_map/ppermute | solution.py:324
  11.4 1.3 %collective-permute-start.14 = (bf16[384,384]{1,0:T(8,128)(2,1)S(1)}, bf16[384,384]{1,0:T(8,128)(2,1)S(1)}, u32[]{:S(2)}, u32[]{:S(2)}) collective-permute-start(bf16[384,384]{1,0:T(8,128)(2,1)S(1)} %shard_map.92.f2.own), channel_id=1, source_target_pairs={{3,5},{12,4},{21,13},{30,14}} | collective-permute-start | bytes 884744 | tf_op jit(solution)/shard_map/ppermute | solution.py:324
  12.7 6.4 %collective-permute-done.7.rest_1_ = bf16[384,384]{1,0:T(8,128)(2,1)S(1)} collective-permute-done((bf16[384,384]{1,0:T(8,128)(2,1)S(1)}, bf16[384,384]{1,0:T(8,128)(2,1)S(1)}, u32[]{:S(2)}, u32[]{:S(2)}) %collective-permute-start.7) | collective-permute-done | bytes 294944 | tf_op jit(solution)/shard_map/ppermute | solution.py:324
  19.2 9.2 %collective-permute-start.8 = (bf16[384,384]{1,0:T(8,128)(2,1)S(1)}, bf16[384,384]{1,0:T(8,128)(2,1)S(1)}, u32[]{:S(2)}, u32[]{:S(2)}) collective-permute-start(bf16[384,384]{1,0:T(8,128)(2,1)S(1)} %shard_map.94), channel_id=1, source_target_pairs={{7,6},{15,14},{23,22},{5,4}} | collective-permute-start | bytes 884744 | tf_op jit(solution)/shard_map/ppermute | solution.py:324
  28.4 0.7 %collective-permute-start.11 = (bf16[384,384]{1,0:T(8,128)(2,1)S(1)}, bf16[384,384]{1,0:T(8,128)(2,1)S(1)}, u32[]{:S(2)}, u32[]{:S(2)}) collective-permute-start(bf16[384,384]{1,0:T(8,128)(2,1)S(1)} %shard_map.89.f1.own), channel_id=1, source_target_pairs={{20,4},{29,13}} | collective-permute-start | bytes 884744 | tf_op jit(solution)/shard_map/ppermute | solution.py:324
  29.1 1.3 %collective-permute-start.12 = (bf16[384,384]{1,0:T(8,128)(2,1)S(1)}, bf16[384,384]{1,0:T(8,128)(2,1)S(1)}, u32[]{:S(2)}, u32[]{:S(2)}) collective-permute-start(bf16[384,384]{1,0:T(8,128)(2,1)S(1)} %shard_map.96), channel_id=1, source_target_pairs={{7,6},{15,14},{23,22},{4,5}} | collective-permute-start | bytes 884744 | tf_op jit(solution)/shard_map/ppermute | solution.py:324
  30.5 1.3 %collective-permute-start.15 = (bf16[384,384]{1,0:T(8,128)(2,1)S(1)}, bf16[384,384]{1,0:T(8,128)(2,1)S(1)}, u32[]{:S(2)}, u32[]{:S(2)}) collective-permute-start(bf16[384,384]{1,0:T(8,128)(2,1)S(1)} %shard_map.92.f2.own), channel_id=1, source_target_pairs={{21,5},{30,22},{12,13}} | collective-permute-start | bytes 884744 | tf_op jit(solution)/shard_map/ppermute | solution.py:324
  31.8 3.6 %collective-permute-done.14.rest_1_ = bf16[384,384]{1,0:T(8,128)(2,1)S(1)} collective-permute-done((bf16[384,384]{1,0:T(8,128)(2,1)S(1)}, bf16[384,384]{1,0:T(8,128)(2,1)S(1)}, u32[]{:S(2)}, u32[]{:S(2)}) %collective-permute-start.14) | collective-permute-done | bytes 294944 | tf_op jit(solution)/shard_map/ppermute | solution.py:324
  35.3 0.7 %collective-permute-start.16 = (bf16[384,384]{1,0:T(8,128)(2,1)S(1)}, bf16[384,384]{1,0:T(8,128)(2,1)S(1)}, u32[]{:S(2)}, u32[]{:S(2)}) collective-permute-start(bf16[384,384]{1,0:T(8,128)(2,1)S(1)} %shard_map.92.f2.own), channel_id=1, source_target_pairs={{30,31}} | collective-permute-start | bytes 884744 | tf_op jit(solution)/shard_map/ppermute | solution.py:324
  36.1 4.3 %collective-permute-start.17 = (bf16[384,384]{1,0:T(8,128)(2,1)S(1)}, bf16[384,384]{1,0:T(8,128)(2,1)S(1)}, u32[]{:S(2)}, u32[]{:S(2)}) collective-permute-start(bf16[384,384]{1,0:T(8,128)(2,1)S(1)} %shard_map.99), channel_id=1, source_target_pairs={{7,6},{15,14},{23,22},{5,4}} | collective-permute-start | bytes 884744 | tf_op jit(solution)/shard_map/ppermute | solution.py:324
  40.4 0.8 %shard_map.93 = bf16[384,384]{1,0:T(8,128)(2,1)} custom-call(bf16[384,384]{1,0:T(8,128)(2,1)S(1)} %shard_map.86.f0.own, bf16[384,384]{1,0:T(8,128)(2,1)S(1)} %shard_map.89.f1.own, bf16[384,384]{1,0:T(8,128)(2,1)S(1)} %shard_map.92.f2.own), custom_call_target="tpu_custom_call" | custom-call | tf_op jit(solution)/shard_map/pallas_call | solution.py:356
  41.6 0.8 %shard_map.97.s2 = f32[384,384]{1,0:T(8,128)S(1)} custom-call(f32[384,384]{1,0:T(8,128)S(1)} %shard_map.95.s1, bf16[384,384]{1,0:T(8,128)(2,1)S(1)} %get-tuple-element.25.a1, bf16[384,384]{1,0:T(8,128)(2,1)S(1)} %get-tuple-element.24.coup_b.b1, bf16[384,384]{1,0:T(8,128)(2,1)S(1)} %collective-permute-done.9.rest_0_, ...), custom_call_target="tpu_custom_call" | custom-call | tf_op jit(solution)/shard_map/pallas_call | solution.py:356
  42.8 1.1 %shard_map.100 = f32[384,384]{1,0:T(8,128)} custom-call(f32[384,384]{1,0:T(8,128)S(1)} %shard_map.98.s3, bf16[384,384]{1,0:T(8,128)(2,1)S(1)} %get-tuple-element.27.b2, bf16[384,384]{1,0:T(8,128)(2,1)S(1)} %collective-permute-done.13.rest_0_, bf16[384,384]{1,0:T(8,128)(2,1)S(1)} %collective-permute-done.14.rest_1_, ...), custom_call_target="tpu_custom_call" | custom-call | tf_op jit(solution)/shard_map/pallas_call | solution.py:356
  (27 shorter events, 1.2 us)
Async XLA Ops:
  0.7 4.4 %collective-permute-start.1 = (bf16[384,384]{1,0:T(8,128)(2,1)S(1)}, bf16[384,384]{1,0:T(8,128)(2,1)S(1)}, u32[]{:S(2)}, u32[]{:S(2)}) collective-permute-start(bf16[384,384]{1,0:T(8,128)(2,1)S(1)} %shard_map.86.f0.own), channel_id=1, source_target_pairs={{1,2},{10,11},{19,20},{28,29}} | collective-permute-start | bytes 884744 | tf_op jit(solution)/shard_map/ppermute | solution.py:324
  1.4 3.8 %collective-permute-start = (bf16[384,384]{1,0:T(8,128)(2,1)S(1)}, bf16[384,384]{1,0:T(8,128)(2,1)S(1)}, u32[]{:S(2)}, u32[]{:S(2)}) collective-permute-start(bf16[384,384]{1,0:T(8,128)(2,1)S(1)} %shard_map.86.f0.own), channel_id=1, source_target_pairs={{10,2},{19,11},{28,20}} | collective-permute-start | bytes 884744 | tf_op jit(solution)/shard_map/ppermute | solution.py:324
  2.1 5.2 %collective-permute-start.4 = (bf16[384,384]{1,0:T(8,128)(2,1)S(1)}, bf16[384,384]{1,0:T(8,128)(2,1)S(1)}, u32[]{:S(2)}, u32[]{:S(2)}) collective-permute-start(bf16[384,384]{1,0:T(8,128)(2,1)S(1)} %shard_map.86.f0.own), channel_id=1, source_target_pairs={{19,3},{28,12}} | collective-permute-start | bytes 884744 | tf_op jit(solution)/shard_map/ppermute | solution.py:324
  2.8 5.8 %collective-permute-start.5 = (bf16[384,384]{1,0:T(8,128)(2,1)S(1)}, bf16[384,384]{1,0:T(8,128)(2,1)S(1)}, u32[]{:S(2)}, u32[]{:S(2)}) collective-permute-start(bf16[384,384]{1,0:T(8,128)(2,1)S(1)} %shard_map.86.f0.own), channel_id=1, source_target_pairs={{1,3},{10,12},{19,21},{28,30}} | collective-permute-start | bytes 884744 | tf_op jit(solution)/shard_map/ppermute | solution.py:324
  5.2 4.7 %collective-permute-start.3 = (bf16[384,384]{1,0:T(8,128)(2,1)S(1)}, bf16[384,384]{1,0:T(8,128)(2,1)S(1)}, u32[]{:S(2)}, u32[]{:S(2)}) collective-permute-start(bf16[384,384]{1,0:T(8,128)(2,1)S(1)} %shard_map.89.f1.own), channel_id=1, source_target_pairs={{2,3},{11,12},{20,21},{29,30}} | collective-permute-start | bytes 884744 | tf_op jit(solution)/shard_map/ppermute | solution.py:324
  5.9 4.7 %collective-permute-start.2 = (bf16[384,384]{1,0:T(8,128)(2,1)S(1)}, bf16[384,384]{1,0:T(8,128)(2,1)S(1)}, u32[]{:S(2)}, u32[]{:S(2)}) collective-permute-start(bf16[384,384]{1,0:T(8,128)(2,1)S(1)} %shard_map.89.f1.own), channel_id=1, source_target_pairs={{11,3},{20,12},{29,21}} | collective-permute-start | bytes 884744 | tf_op jit(solution)/shard_map/ppermute | solution.py:324
  6.6 4.8 %collective-permute-start.6 = (bf16[384,384]{1,0:T(8,128)(2,1)S(1)}, bf16[384,384]{1,0:T(8,128)(2,1)S(1)}, u32[]{:S(2)}, u32[]{:S(2)}) collective-permute-start(bf16[384,384]{1,0:T(8,128)(2,1)S(1)} %shard_map.86.f0.own), channel_id=1, source_target_pairs={{1,7},{10,15},{19,23},{28,31}} | collective-permute-start | bytes 884744 | tf_op jit(solution)/shard_map/ppermute | solution.py:324
  7.3 11.8 %collective-permute-start.7 = (bf16[384,384]{1,0:T(8,128)(2,1)S(1)}, bf16[384,384]{1,0:T(8,128)(2,1)S(1)}, u32[]{:S(2)}, u32[]{:S(2)}) collective-permute-start(bf16[384,384]{1,0:T(8,128)(2,1)S(1)} %shard_map.86.f0.own), channel_id=1, source_target_pairs={{1,5},{10,13},{28,4}} | collective-permute-start | bytes 884744 | tf_op jit(solution)/shard_map/ppermute | solution.py:324
  8.6 19.8 %collective-permute-start.10 = (bf16[384,384]{1,0:T(8,128)(2,1)S(1)}, bf16[384,384]{1,0:T(8,128)(2,1)S(1)}, u32[]{:S(2)}, u32[]{:S(2)}) collective-permute-start(bf16[384,384]{1,0:T(8,128)(2,1)S(1)} %shard_map.89.f1.own), channel_id=1, source_target_pairs={{2,4},{11,13},{29,5}} | collective-permute-start | bytes 884744 | tf_op jit(solution)/shard_map/ppermute | solution.py:324
  9.9 19.1 %collective-permute-start.9 = (bf16[384,384]{1,0:T(8,128)(2,1)S(1)}, bf16[384,384]{1,0:T(8,128)(2,1)S(1)}, u32[]{:S(2)}, u32[]{:S(2)}) collective-permute-start(bf16[384,384]{1,0:T(8,128)(2,1)S(1)} %shard_map.89.f1.own), channel_id=1, source_target_pairs={{2,7},{11,15},{20,23},{29,31}} | collective-permute-start | bytes 884744 | tf_op jit(solution)/shard_map/ppermute | solution.py:324
  10.7 19.8 %collective-permute-start.13 = (bf16[384,384]{1,0:T(8,128)(2,1)S(1)}, bf16[384,384]{1,0:T(8,128)(2,1)S(1)}, u32[]{:S(2)}, u32[]{:S(2)}) collective-permute-start(bf16[384,384]{1,0:T(8,128)(2,1)S(1)} %shard_map.92.f2.own), channel_id=1, source_target_pairs={{3,7},{12,15},{21,23},{30,6}} | collective-permute-start | bytes 884744 | tf_op jit(solution)/shard_map/ppermute | solution.py:324
  11.4 23.9 %collective-permute-start.14 = (bf16[384,384]{1,0:T(8,128)(2,1)S(1)}, bf16[384,384]{1,0:T(8,128)(2,1)S(1)}, u32[]{:S(2)}, u32[]{:S(2)}) collective-permute-start(bf16[384,384]{1,0:T(8,128)(2,1)S(1)} %shard_map.92.f2.own), channel_id=1, source_target_pairs={{3,5},{12,4},{21,13},{30,14}} | collective-permute-start | bytes 884744 | tf_op jit(solution)/shard_map/ppermute | solution.py:324
  19.2 16.9 %collective-permute-start.8 = (bf16[384,384]{1,0:T(8,128)(2,1)S(1)}, bf16[384,384]{1,0:T(8,128)(2,1)S(1)}, u32[]{:S(2)}, u32[]{:S(2)}) collective-permute-start(bf16[384,384]{1,0:T(8,128)(2,1)S(1)} %shard_map.94), channel_id=1, source_target_pairs={{7,6},{15,14},{23,22},{5,4}} | collective-permute-start | bytes 884744 | tf_op jit(solution)/shard_map/ppermute | solution.py:324
  28.4 13.2 %collective-permute-start.11 = (bf16[384,384]{1,0:T(8,128)(2,1)S(1)}, bf16[384,384]{1,0:T(8,128)(2,1)S(1)}, u32[]{:S(2)}, u32[]{:S(2)}) collective-permute-start(bf16[384,384]{1,0:T(8,128)(2,1)S(1)} %shard_map.89.f1.own), channel_id=1, source_target_pairs={{20,4},{29,13}} | collective-permute-start | bytes 884744 | tf_op jit(solution)/shard_map/ppermute | solution.py:324
  29.1 12.4 %collective-permute-start.12 = (bf16[384,384]{1,0:T(8,128)(2,1)S(1)}, bf16[384,384]{1,0:T(8,128)(2,1)S(1)}, u32[]{:S(2)}, u32[]{:S(2)}) collective-permute-start(bf16[384,384]{1,0:T(8,128)(2,1)S(1)} %shard_map.96), channel_id=1, source_target_pairs={{7,6},{15,14},{23,22},{4,5}} | collective-permute-start | bytes 884744 | tf_op jit(solution)/shard_map/ppermute | solution.py:324
  30.5 11.9 %collective-permute-start.15 = (bf16[384,384]{1,0:T(8,128)(2,1)S(1)}, bf16[384,384]{1,0:T(8,128)(2,1)S(1)}, u32[]{:S(2)}, u32[]{:S(2)}) collective-permute-start(bf16[384,384]{1,0:T(8,128)(2,1)S(1)} %shard_map.92.f2.own), channel_id=1, source_target_pairs={{21,5},{30,22},{12,13}} | collective-permute-start | bytes 884744 | tf_op jit(solution)/shard_map/ppermute | solution.py:324
  35.3 7.5 %collective-permute-start.16 = (bf16[384,384]{1,0:T(8,128)(2,1)S(1)}, bf16[384,384]{1,0:T(8,128)(2,1)S(1)}, u32[]{:S(2)}, u32[]{:S(2)}) collective-permute-start(bf16[384,384]{1,0:T(8,128)(2,1)S(1)} %shard_map.92.f2.own), channel_id=1, source_target_pairs={{30,31}} | collective-permute-start | bytes 884744 | tf_op jit(solution)/shard_map/ppermute | solution.py:324
  36.1 6.8 %collective-permute-start.17 = (bf16[384,384]{1,0:T(8,128)(2,1)S(1)}, bf16[384,384]{1,0:T(8,128)(2,1)S(1)}, u32[]{:S(2)}, u32[]{:S(2)}) collective-permute-start(bf16[384,384]{1,0:T(8,128)(2,1)S(1)} %shard_map.99), channel_id=1, source_target_pairs={{7,6},{15,14},{23,22},{5,4}} | collective-permute-start | bytes 884744 | tf_op jit(solution)/shard_map/ppermute | solution.py:324

commit v6 on v5

--- a/solution.py
+++ b/solution.py
@@ -13,7 +13,7 @@
 FAR_SPEC = pl.BlockSpec(memory_space=pltpu.HBM)
 
 
-def plan(rows_n, cols_n, offset, gap, up_gap):
+def plan(rows_n, cols_n, offset, gap, up_gap, apart=False):
     rights, ups, last = [], [], []
     for i in range(rows_n):
         m = i + offset
@@ -27,10 +27,16 @@
     ops, forwards = [], []
     while todo:
         used_from, used_to, op = set(), set(), []
+        allowed = {"left", "down"}
+        if apart:
+            turn = {kind for _, _, kind in todo}
+            allowed = turn if len(turn) == 1 else {"left" if len(ops) % 2 == 0 else "down"}
         busy = [source for source, _, _ in todo]
         waiting = {targets[0]: busy.count(source) for source, targets, kind in todo if kind == "down"}
         for item in list(todo):
             source, targets, kind = item
+            if kind not in allowed:
+                continue
             for target in sorted(targets, key=lambda t: (waiting.get(t, 0), -t[1])):
                 if source not in used_from and target not in used_to:
                     used_from.add(source)
@@ -179,22 +185,40 @@
             move.wait()
 
 
-def take_left(rows_n, level, left, s, coup_b, utk, vk, out, lhs, mid):
-    @pl.when(level_of(rows_n) == level)
-    def _():
-        out[...] = spectral(s[...] - dot(left[...], coup_b[...]), utk, vk, lhs, mid)
-
-
-def finish_solve(rows_n, level, down, y, coup, uk, vk, vl, inverse, f, lhs, mid):
-    @pl.when(level_of(rows_n) == level)
+def late(t):
+    return (lax.rem(lax.axis_index("col"), 2) == 0) & (t == 1)
+
+
+def take_left(rows_n, first, t, left, s, coup_b, utk, vk, out, lhs, mid):
+    mine = level_of(rows_n) == first + t + 1
+
+    @pl.when(mine)
+    def _():
+        out[...] = s[...] - dot(left[...], coup_b[...])
+
+    @pl.when(mine & jnp.logical_not(late(t)))
+    def _():
+        out[...] = spectral(out[...], utk, vk, lhs, mid)
+
+
+def finish_solve(rows_n, first, t, down, y, coup, coup_a, uk, utk, vk, vl, inverse, f, lhs, mid, part):
+    mine = level_of(rows_n) == first + t + 1
+
+    @pl.when(mine & late(t))
+    def _():
+        part[...] = spectral(y[...] - dot(coup_a[...], down[...]), utk, vk, lhs, mid) * inverse[...]
+
+    @pl.when(mine & jnp.logical_not(late(t)))
     def _():
         n = y.shape[0]
         lhs[:, 0:n] = down[...]
         lhs[:, n : 2 * n] = down[...]
-        part = dot(lhs[:, 0 : 2 * n], vk[0 : 2 * n])
-        put_right(mid, split(part))
-        part = (y[...] - dot(coup[...], mid[...])) * inverse[...]
-        f[...] = back(part, uk, vl, lhs, mid)
+        put_right(mid, split(dot(lhs[:, 0 : 2 * n], vk[0 : 2 * n])))
+        part[...] = (y[...] - dot(coup[...], mid[...])) * inverse[...]
+
+    @pl.when(mine)
+    def _():
+        f[...] = back(part[...], uk, vl, lhs, mid)
 
 
 def third_early(rows_n, first, down, left, s, a0, b0, s1):
@@ -330,7 +354,7 @@
     offset = first - rows_n + 1
     ops0 = plan(rows_n, cols_n, offset, 3, 3)
     ops1 = plan(rows_n, cols_n, offset + 1, 2, 2)
-    ops2 = plan(rows_n, cols_n, offset + 2, 1, 1)
+    ops2 = plan(rows_n, cols_n, offset + 2, 1, 1, True)
 
     def owners(t):
         return [(i, i + offset + t) for i in range(rows_n) if 0 <= i + offset + t < cols_n]
@@ -372,10 +396,10 @@
             "begin",
         )
 
-        def advance(t, down, left, state_in, coup_b):
-            uk, utk, vk, vl, inverse = basis
+        def advance(t, down, left, state_in, coup_a, coup_b):
+            _, utk, vk, _, _ = basis
             (y,) = call(
-                functools.partial(take_left, rows_n, first + t + 1),
+                functools.partial(take_left, rows_n, first, t),
                 [],
                 [left, state_in, coup_b, utk, vk],
                 [state],
@@ -383,11 +407,11 @@
                 f"left{t}",
             )
             return call(
-                functools.partial(finish_solve, rows_n, first + t + 1),
+                functools.partial(finish_solve, rows_n, first, t),
                 [],
-                [down, y, coup, uk, vk, vl, inverse],
+                [down, y, coup, coup_a, *basis],
                 [square],
-                work,
+                work + [pltpu.VMEM((n, n), full)],
                 f"solve{t}",
             )
 
@@ -404,7 +428,7 @@
             loads[1:] + [pltpu.VMEM((2 * n, n), half), pltpu.SemaphoreType.DMA((9,))],
             "prepare",
         )
-        (f1,) = advance(0, down, left, s, b0)
+        (f1,) = advance(0, down, left, s, a0, b0)
         down = move(f1, up(1, 1))
         left = move(f1, right(1, 1))
         (s1,) = call(
@@ -416,7 +440,7 @@
             "third_early",
         )
         far1 = spread(ops1, cols_n, f1, "b", call)
-        (f2,) = advance(1, down, left, s1, b1)
+        (f2,) = advance(1, down, left, s1, a1, b1)
         for k, (ops, far, a, b) in enumerate(((ops0, far0, a0, b0), (ops1, far1, a1, b1))):
             (s,) = call(
                 functools.partial(middle, rows_n, cols_n, first, ops),

time: 44.3 us -> 42.4 us (0.957)
  starting transfers between devices: 27.4 us -> 20.6 us
  waiting for transfers between devices: 10.1 us -> 14.7 us
    ppermute x18 -> x19, starting transfers between devices: 27.4 us -> 20.6 us  [move(): return lax.ppermute(value, AXES, pairs)]
    ppermute x18 -> x19, waiting for transfers between devices: 10.1 us -> 14.7 us  [move(): return lax.ppermute(value, AXES, pairs)]
  transfers between devices with their start and end apart: 18 -> 19, of which waited for: 2 -> 2; matrix products, arithmetic and copies ran while one was open for 0% -> 0% of each run, Pallas kernels for 10% -> 10%
where the time goes in v6:
time: 42.4 us; the launch traced here: 42 us
  starting transfers between devices  20.6 us (49%)
  waiting for transfers between devices  14.7 us (35%)
  Pallas kernels  5.56 us (13%)
  between operations  1.18 us (3%)
    ppermute x19, starting transfers between devices, move(): return lax.ppermute(value, AXES, pairs)  20.6 us
    ppermute x19, waiting for transfers between devices, move(): return lax.ppermute(value, AXES, pairs)  14.7 us
    pallas_call x15, Pallas kernels, call(): pl.pallas_call(kernel, out_shape=outs, in_specs=[FAR_SPEC] * len(far) + [...  5.56 us
  transfers between devices with their start and end apart: 19, of which 2 were waited for; matrix products, arithmetic and copies ran while one was open for 0% of the time, Pallas kernels for 10%

profile of v6, /device:TPU:17, one launch (start us, length us, event | category | flops | bytes accessed | tf_op | source)
XLA Modules:
  0.0 42.0 jit_solution(8380673593782872252)
XLA Ops:
  0.7 0.7 %collective-permute-start.1 = (bf16[384,384]{1,0:T(8,128)(2,1)S(1)}, bf16[384,384]{1,0:T(8,128)(2,1)S(1)}, u32[]{:S(2)}, u32[]{:S(2)}) collective-permute-start(bf16[384,384]{1,0:T(8,128)(2,1)S(1)} %shard_map.86.f0.own), channel_id=1, source_target_pairs={{1,2},{10,11},{19,20},{28,29}} | collective-permute-start | bytes 884744 | tf_op jit(solution)/shard_map/ppermute | solution.py:348
  1.4 0.7 %collective-permute-start = (bf16[384,384]{1,0:T(8,128)(2,1)S(1)}, bf16[384,384]{1,0:T(8,128)(2,1)S(1)}, u32[]{:S(2)}, u32[]{:S(2)}) collective-permute-start(bf16[384,384]{1,0:T(8,128)(2,1)S(1)} %shard_map.86.f0.own), channel_id=1, source_target_pairs={{10,2},{19,11},{28,20}} | collective-permute-start | bytes 884744 | tf_op jit(solution)/shard_map/ppermute | solution.py:348
  2.1 0.7 %collective-permute-start.6 = (bf16[384,384]{1,0:T(8,128)(2,1)S(1)}, bf16[384,384]{1,0:T(8,128)(2,1)S(1)}, u32[]{:S(2)}, u32[]{:S(2)}) collective-permute-start(bf16[384,384]{1,0:T(8,128)(2,1)S(1)} %shard_map.86.f0.own), channel_id=1, source_target_pairs={{1,7},{10,15},{19,23},{28,31}} | collective-permute-start | bytes 884744 | tf_op jit(solution)/shard_map/ppermute | solution.py:348
  2.8 1.3 %collective-permute-start.7 = (bf16[384,384]{1,0:T(8,128)(2,1)S(1)}, bf16[384,384]{1,0:T(8,128)(2,1)S(1)}, u32[]{:S(2)}, u32[]{:S(2)}) collective-permute-start(bf16[384,384]{1,0:T(8,128)(2,1)S(1)} %shard_map.86.f0.own), channel_id=1, source_target_pairs={{1,5},{10,13},{28,4}} | collective-permute-start | bytes 884744 | tf_op jit(solution)/shard_map/ppermute | solution.py:348
  4.1 0.7 %collective-permute-start.4 = (bf16[384,384]{1,0:T(8,128)(2,1)S(1)}, bf16[384,384]{1,0:T(8,128)(2,1)S(1)}, u32[]{:S(2)}, u32[]{:S(2)}) collective-permute-start(bf16[384,384]{1,0:T(8,128)(2,1)S(1)} %shard_map.86.f0.own), channel_id=1, source_target_pairs={{19,3},{28,12}} | collective-permute-start | bytes 884744 | tf_op jit(solution)/shard_map/ppermute | solution.py:348
  4.7 1.7 %shard_map.87 = (bf16[384,1152]{1,0:T(8,128)(2,1)S(1)}, bf16[384,1152]{1,0:T(8,128)(2,1)S(1)}, bf16[1152,384]{1,0:T(8,128)(2,1)S(1)}, bf16[384,1152]{1,0:T(8,128...) custom-call(f32[384,384]{1,0:T(8,128)} %rhs.3, ...), custom_call_target="tpu_custom_call" | custom-call | tf_op jit(solution)/shard_map/pallas_call | solution.py:380
  6.5 0.7 %collective-permute-start.5 = (bf16[384,384]{1,0:T(8,128)(2,1)S(1)}, bf16[384,384]{1,0:T(8,128)(2,1)S(1)}, u32[]{:S(2)}, u32[]{:S(2)}) collective-permute-start(bf16[384,384]{1,0:T(8,128)(2,1)S(1)} %shard_map.86.f0.own), channel_id=1, source_target_pairs={{1,3},{10,12},{19,21},{28,30}} | collective-permute-start | bytes 884744 | tf_op jit(solution)/shard_map/ppermute | solution.py:348
  7.2 0.7 %collective-permute-start.3 = (bf16[384,384]{1,0:T(8,128)(2,1)S(1)}, bf16[384,384]{1,0:T(8,128)(2,1)S(1)}, u32[]{:S(2)}, u32[]{:S(2)}) collective-permute-start(bf16[384,384]{1,0:T(8,128)(2,1)S(1)} %shard_map.89.f1.own), channel_id=1, source_target_pairs={{2,3},{11,12},{20,21},{29,30}} | collective-permute-start | bytes 884744 | tf_op jit(solution)/shard_map/ppermute | solution.py:348
  7.9 0.7 %collective-permute-start.2 = (bf16[384,384]{1,0:T(8,128)(2,1)S(1)}, bf16[384,384]{1,0:T(8,128)(2,1)S(1)}, u32[]{:S(2)}, u32[]{:S(2)}) collective-permute-start(bf16[384,384]{1,0:T(8,128)(2,1)S(1)} %shard_map.89.f1.own), channel_id=1, source_target_pairs={{11,3},{20,12},{29,21}} | collective-permute-start | bytes 884744 | tf_op jit(solution)/shard_map/ppermute | solution.py:348
  8.6 7.3 %collective-permute-done.7.rest_1_ = bf16[384,384]{1,0:T(8,128)(2,1)S(1)} collective-permute-done((bf16[384,384]{1,0:T(8,128)(2,1)S(1)}, bf16[384,384]{1,0:T(8,128)(2,1)S(1)}, u32[]{:S(2)}, u32[]{:S(2)}) %collective-permute-start.7) | collective-permute-done | bytes 294944 | tf_op jit(solution)/shard_map/ppermute | solution.py:348
  15.9 1.3 %collective-permute-start.10 = (bf16[384,384]{1,0:T(8,128)(2,1)S(1)}, bf16[384,384]{1,0:T(8,128)(2,1)S(1)}, u32[]{:S(2)}, u32[]{:S(2)}) collective-permute-start(bf16[384,384]{1,0:T(8,128)(2,1)S(1)} %shard_map.89.f1.own), channel_id=1, source_target_pairs={{2,4},{11,13},{29,5}} | collective-permute-start | bytes 884744 | tf_op jit(solution)/shard_map/ppermute | solution.py:348
  17.2 0.7 %collective-permute-start.9 = (bf16[384,384]{1,0:T(8,128)(2,1)S(1)}, bf16[384,384]{1,0:T(8,128)(2,1)S(1)}, u32[]{:S(2)}, u32[]{:S(2)}) collective-permute-start(bf16[384,384]{1,0:T(8,128)(2,1)S(1)} %shard_map.89.f1.own), channel_id=1, source_target_pairs={{2,7},{11,15},{20,23},{29,31}} | collective-permute-start | bytes 884744 | tf_op jit(solution)/shard_map/ppermute | solution.py:348
  17.9 4.3 %collective-permute-start.8 = (bf16[384,384]{1,0:T(8,128)(2,1)S(1)}, bf16[384,384]{1,0:T(8,128)(2,1)S(1)}, u32[]{:S(2)}, u32[]{:S(2)}) collective-permute-start(bf16[384,384]{1,0:T(8,128)(2,1)S(1)} %shard_map.94), channel_id=1, source_target_pairs={{7,6},{15,14},{23,22},{5,4}} | collective-permute-start | bytes 884744 | tf_op jit(solution)/shard_map/ppermute | solution.py:348
  22.3 0.7 %collective-permute-start.16 = (bf16[384,384]{1,0:T(8,128)(2,1)S(1)}, bf16[384,384]{1,0:T(8,128)(2,1)S(1)}, u32[]{:S(2)}, u32[]{:S(2)}) collective-permute-start(bf16[384,384]{1,0:T(8,128)(2,1)S(1)} %shard_map.92.f2.own), channel_id=1, source_target_pairs={{3,7},{12,15},{21,23},{30,31}} | collective-permute-start | bytes 884744 | tf_op jit(solution)/shard_map/ppermute | solution.py:348
  23.0 1.3 %collective-permute-start.17 = (bf16[384,384]{1,0:T(8,128)(2,1)S(1)}, bf16[384,384]{1,0:T(8,128)(2,1)S(1)}, u32[]{:S(2)}, u32[]{:S(2)}) collective-permute-start(bf16[384,384]{1,0:T(8,128)(2,1)S(1)} %shard_map.92.f2.own), channel_id=1, source_target_pairs={{3,5},{12,13}} | collective-permute-start | bytes 884744 | tf_op jit(solution)/shard_map/ppermute | solution.py:348
  24.3 0.7 %collective-permute-start.11 = (bf16[384,384]{1,0:T(8,128)(2,1)S(1)}, bf16[384,384]{1,0:T(8,128)(2,1)S(1)}, u32[]{:S(2)}, u32[]{:S(2)}) collective-permute-start(bf16[384,384]{1,0:T(8,128)(2,1)S(1)} %shard_map.89.f1.own), channel_id=1, source_target_pairs={{20,4},{29,13}} | collective-permute-start | bytes 884744 | tf_op jit(solution)/shard_map/ppermute | solution.py:348
  25.0 1.5 %collective-permute-start.13 = (bf16[384,384]{1,0:T(8,128)(2,1)S(1)}, bf16[384,384]{1,0:T(8,128)(2,1)S(1)}, u32[]{:S(2)}, u32[]{:S(2)}) collective-permute-start(bf16[384,384]{1,0:T(8,128)(2,1)S(1)} %shard_map.92.f2.own), channel_id=1, source_target_pairs={{12,4},{21,5},{30,6}} | collective-permute-start | bytes 884744 | tf_op jit(solution)/shard_map/ppermute | solution.py:348
  26.6 1.3 %collective-permute-start.12 = (bf16[384,384]{1,0:T(8,128)(2,1)S(1)}, bf16[384,384]{1,0:T(8,128)(2,1)S(1)}, u32[]{:S(2)}, u32[]{:S(2)}) collective-permute-start(bf16[384,384]{1,0:T(8,128)(2,1)S(1)} %shard_map.96), channel_id=1, source_target_pairs={{7,6},{15,14},{23,22},{4,5}} | collective-permute-start | bytes 884744 | tf_op jit(solution)/shard_map/ppermute | solution.py:348
  27.9 0.7 %collective-permute-start.14 = (bf16[384,384]{1,0:T(8,128)(2,1)S(1)}, bf16[384,384]{1,0:T(8,128)(2,1)S(1)}, u32[]{:S(2)}, u32[]{:S(2)}) collective-permute-start(bf16[384,384]{1,0:T(8,128)(2,1)S(1)} %shard_map.92.f2.own), channel_id=1, source_target_pairs={{21,13},{30,14}} | collective-permute-start | bytes 884744 | tf_op jit(solution)/shard_map/ppermute | solution.py:348
  28.6 7.3 %collective-permute-done.17.rest_1_.rest_2_ = bf16[384,384]{1,0:T(8,128)(2,1)S(1)} collective-permute-done((bf16[384,384]{1,0:T(8,128)(2,1)S(1)}, bf16[384,384]{1,0:T(8,128)(2,1)S(1)}, u32[]{:S(2)}, u32[]{:S(2)}) %collective-permute-start.17) | collective-permute-done | bytes 294944 | tf_op jit(solution)/shard_map/ppermute | solution.py:348
  36.6 1.6 %collective-permute-start.18 = (bf16[384,384]{1,0:T(8,128)(2,1)S(1)}, bf16[384,384]{1,0:T(8,128)(2,1)S(1)}, u32[]{:S(2)}, u32[]{:S(2)}) collective-permute-start(bf16[384,384]{1,0:T(8,128)(2,1)S(1)} %shard_map.99), channel_id=1, source_target_pairs={{7,6},{15,14},{23,22},{5,4}} | collective-permute-start | bytes 884744 | tf_op jit(solution)/shard_map/ppermute | solution.py:348
  38.2 0.8 %shard_map.93 = bf16[384,384]{1,0:T(8,128)(2,1)} custom-call(bf16[384,384]{1,0:T(8,128)(2,1)S(1)} %shard_map.86.f0.own, bf16[384,384]{1,0:T(8,128)(2,1)S(1)} %shard_map.89.f1.own, bf16[384,384]{1,0:T(8,128)(2,1)S(1)} %shard_map.92.f2.own), custom_call_target="tpu_custom_call" | custom-call | tf_op jit(solution)/shard_map/pallas_call | solution.py:380
  39.5 0.8 %shard_map.97.s2 = f32[384,384]{1,0:T(8,128)S(1)} custom-call(f32[384,384]{1,0:T(8,128)S(1)} %shard_map.95.s1, bf16[384,384]{1,0:T(8,128)(2,1)S(1)} %get-tuple-element.25.coup_a.a1, bf16[384,384]{1,0:T(8,128)(2,1)S(1)} %get-tuple-element.24.coup_b.b1, bf16[384,384]{1,0:T(8,128)(2,1)S(1)} %collective-permute-done.9.rest_0_, ...), custom_call_target="tpu_custom_call" | custom-call | tf_op jit(solution)/shard_map/pallas_call | solution.py:380
  40.7 1.1 %shard_map.100 = f32[384,384]{1,0:T(8,128)} custom-call(f32[384,384]{1,0:T(8,128)S(1)} %shard_map.98.s3, bf16[384,384]{1,0:T(8,128)(2,1)S(1)} %get-tuple-element.27.b2, bf16[384,384]{1,0:T(8,128)(2,1)S(1)} %collective-permute-done.16.rest_0_, bf16[384,384]{1,0:T(8,128)(2,1)S(1)} %collective-permute-done.13.rest_0_.rest_1_, ...), custom_call_target="tpu_custom_call" | custom-call | tf_op jit(solution)/shard_map/pallas_call | solution.py:380
  (29 shorter events, 1.9 us)
Async XLA Ops:
  0.7 5.7 %collective-permute-start.1 = (bf16[384,384]{1,0:T(8,128)(2,1)S(1)}, bf16[384,384]{1,0:T(8,128)(2,1)S(1)}, u32[]{:S(2)}, u32[]{:S(2)}) collective-permute-start(bf16[384,384]{1,0:T(8,128)(2,1)S(1)} %shard_map.86.f0.own), channel_id=1, source_target_pairs={{1,2},{10,11},{19,20},{28,29}} | collective-permute-start | bytes 884744 | tf_op jit(solution)/shard_map/ppermute | solution.py:348
  1.4 5.8 %collective-permute-start = (bf16[384,384]{1,0:T(8,128)(2,1)S(1)}, bf16[384,384]{1,0:T(8,128)(2,1)S(1)}, u32[]{:S(2)}, u32[]{:S(2)}) collective-permute-start(bf16[384,384]{1,0:T(8,128)(2,1)S(1)} %shard_map.86.f0.own), channel_id=1, source_target_pairs={{10,2},{19,11},{28,20}} | collective-permute-start | bytes 884744 | tf_op jit(solution)/shard_map/ppermute | solution.py:348
  2.1 5.8 %collective-permute-start.6 = (bf16[384,384]{1,0:T(8,128)(2,1)S(1)}, bf16[384,384]{1,0:T(8,128)(2,1)S(1)}, u32[]{:S(2)}, u32[]{:S(2)}) collective-permute-start(bf16[384,384]{1,0:T(8,128)(2,1)S(1)} %shard_map.86.f0.own), channel_id=1, source_target_pairs={{1,7},{10,15},{19,23},{28,31}} | collective-permute-start | bytes 884744 | tf_op jit(solution)/shard_map/ppermute | solution.py:348
  2.8 13.1 %collective-permute-start.7 = (bf16[384,384]{1,0:T(8,128)(2,1)S(1)}, bf16[384,384]{1,0:T(8,128)(2,1)S(1)}, u32[]{:S(2)}, u32[]{:S(2)}) collective-permute-start(bf16[384,384]{1,0:T(8,128)(2,1)S(1)} %shard_map.86.f0.own), channel_id=1, source_target_pairs={{1,5},{10,13},{28,4}} | collective-permute-start | bytes 884744 | tf_op jit(solution)/shard_map/ppermute | solution.py:348
  4.1 13.2 %collective-permute-start.4 = (bf16[384,384]{1,0:T(8,128)(2,1)S(1)}, bf16[384,384]{1,0:T(8,128)(2,1)S(1)}, u32[]{:S(2)}, u32[]{:S(2)}) collective-permute-start(bf16[384,384]{1,0:T(8,128)(2,1)S(1)} %shard_map.86.f0.own), channel_id=1, source_target_pairs={{19,3},{28,12}} | collective-permute-start | bytes 884744 | tf_op jit(solution)/shard_map/ppermute | solution.py:348
  6.5 11.5 %collective-permute-start.5 = (bf16[384,384]{1,0:T(8,128)(2,1)S(1)}, bf16[384,384]{1,0:T(8,128)(2,1)S(1)}, u32[]{:S(2)}, u32[]{:S(2)}) collective-permute-start(bf16[384,384]{1,0:T(8,128)(2,1)S(1)} %shard_map.86.f0.own), channel_id=1, source_target_pairs={{1,3},{10,12},{19,21},{28,30}} | collective-permute-start | bytes 884744 | tf_op jit(solution)/shard_map/ppermute | solution.py:348
  7.2 15.0 %collective-permute-start.3 = (bf16[384,384]{1,0:T(8,128)(2,1)S(1)}, bf16[384,384]{1,0:T(8,128)(2,1)S(1)}, u32[]{:S(2)}, u32[]{:S(2)}) collective-permute-start(bf16[384,384]{1,0:T(8,128)(2,1)S(1)} %shard_map.89.f1.own), channel_id=1, source_target_pairs={{2,3},{11,12},{20,21},{29,30}} | collective-permute-start | bytes 884744 | tf_op jit(solution)/shard_map/ppermute | solution.py:348
  7.9 14.4 %collective-permute-start.2 = (bf16[384,384]{1,0:T(8,128)(2,1)S(1)}, bf16[384,384]{1,0:T(8,128)(2,1)S(1)}, u32[]{:S(2)}, u32[]{:S(2)}) collective-permute-start(bf16[384,384]{1,0:T(8,128)(2,1)S(1)} %shard_map.89.f1.own), channel_id=1, source_target_pairs={{11,3},{20,12},{29,21}} | collective-permute-start | bytes 884744 | tf_op jit(solution)/shard_map/ppermute | solution.py:348
  15.9 8.4 %collective-permute-start.10 = (bf16[384,384]{1,0:T(8,128)(2,1)S(1)}, bf16[384,384]{1,0:T(8,128)(2,1)S(1)}, u32[]{:S(2)}, u32[]{:S(2)}) collective-permute-start(bf16[384,384]{1,0:T(8,128)(2,1)S(1)} %shard_map.89.f1.own), channel_id=1, source_target_pairs={{2,4},{11,13},{29,5}} | collective-permute-start | bytes 884744 | tf_op jit(solution)/shard_map/ppermute | solution.py:348
  17.2 7.8 %collective-permute-start.9 = (bf16[384,384]{1,0:T(8,128)(2,1)S(1)}, bf16[384,384]{1,0:T(8,128)(2,1)S(1)}, u32[]{:S(2)}, u32[]{:S(2)}) collective-permute-start(bf16[384,384]{1,0:T(8,128)(2,1)S(1)} %shard_map.89.f1.own), channel_id=1, source_target_pairs={{2,7},{11,15},{20,23},{29,31}} | collective-permute-start | bytes 884744 | tf_op jit(solution)/shard_map/ppermute | solution.py:348
  17.9 8.6 %collective-permute-start.8 = (bf16[384,384]{1,0:T(8,128)(2,1)S(1)}, bf16[384,384]{1,0:T(8,128)(2,1)S(1)}, u32[]{:S(2)}, u32[]{:S(2)}) collective-permute-start(bf16[384,384]{1,0:T(8,128)(2,1)S(1)} %shard_map.94), channel_id=1, source_target_pairs={{7,6},{15,14},{23,22},{5,4}} | collective-permute-start | bytes 884744 | tf_op jit(solution)/shard_map/ppermute | solution.py:348
  22.3 5.5 %collective-permute-start.16 = (bf16[384,384]{1,0:T(8,128)(2,1)S(1)}, bf16[384,384]{1,0:T(8,128)(2,1)S(1)}, u32[]{:S(2)}, u32[]{:S(2)}) collective-permute-start(bf16[384,384]{1,0:T(8,128)(2,1)S(1)} %shard_map.92.f2.own), channel_id=1, source_target_pairs={{3,7},{12,15},{21,23},{30,31}} | collective-permute-start | bytes 884744 | tf_op jit(solution)/shard_map/ppermute | solution.py:348
  23.0 12.9 %collective-permute-start.17 = (bf16[384,384]{1,0:T(8,128)(2,1)S(1)}, bf16[384,384]{1,0:T(8,128)(2,1)S(1)}, u32[]{:S(2)}, u32[]{:S(2)}) collective-permute-start(bf16[384,384]{1,0:T(8,128)(2,1)S(1)} %shard_map.92.f2.own), channel_id=1, source_target_pairs={{3,5},{12,13}} | collective-permute-start | bytes 884744 | tf_op jit(solution)/shard_map/ppermute | solution.py:348
  24.3 12.3 %collective-permute-start.11 = (bf16[384,384]{1,0:T(8,128)(2,1)S(1)}, bf16[384,384]{1,0:T(8,128)(2,1)S(1)}, u32[]{:S(2)}, u32[]{:S(2)}) collective-permute-start(bf16[384,384]{1,0:T(8,128)(2,1)S(1)} %shard_map.89.f1.own), channel_id=1, source_target_pairs={{20,4},{29,13}} | collective-permute-start | bytes 884744 | tf_op jit(solution)/shard_map/ppermute | solution.py:348
  25.0 15.3 %collective-permute-start.13 = (bf16[384,384]{1,0:T(8,128)(2,1)S(1)}, bf16[384,384]{1,0:T(8,128)(2,1)S(1)}, u32[]{:S(2)}, u32[]{:S(2)}) collective-permute-start(bf16[384,384]{1,0:T(8,128)(2,1)S(1)} %shard_map.92.f2.own), channel_id=1, source_target_pairs={{12,4},{21,5},{30,6}} | collective-permute-start | bytes 884744 | tf_op jit(solution)/shard_map/ppermute | solution.py:348
  26.6 12.9 %collective-permute-start.12 = (bf16[384,384]{1,0:T(8,128)(2,1)S(1)}, bf16[384,384]{1,0:T(8,128)(2,1)S(1)}, u32[]{:S(2)}, u32[]{:S(2)}) collective-permute-start(bf16[384,384]{1,0:T(8,128)(2,1)S(1)} %shard_map.96), channel_id=1, source_target_pairs={{7,6},{15,14},{23,22},{4,5}} | collective-permute-start | bytes 884744 | tf_op jit(solution)/shard_map/ppermute | solution.py:348
  27.9 12.4 %collective-permute-start.14 = (bf16[384,384]{1,0:T(8,128)(2,1)S(1)}, bf16[384,384]{1,0:T(8,128)(2,1)S(1)}, u32[]{:S(2)}, u32[]{:S(2)}) collective-permute-start(bf16[384,384]{1,0:T(8,128)(2,1)S(1)} %shard_map.92.f2.own), channel_id=1, source_target_pairs={{21,13},{30,14}} | collective-permute-start | bytes 884744 | tf_op jit(solution)/shard_map/ppermute | solution.py:348
  35.9 4.4 %collective-permute-start.15 = (bf16[384,384]{1,0:T(8,128)(2,1)S(1)}, bf16[384,384]{1,0:T(8,128)(2,1)S(1)}, u32[]{:S(2)}, u32[]{:S(2)}) collective-permute-start(bf16[384,384]{1,0:T(8,128)(2,1)S(1)} %shard_map.92.f2.own), channel_id=1, source_target_pairs={{30,22}} | collective-permute-start | bytes 884744 | tf_op jit(solution)/shard_map/ppermute | solution.py:348
  36.6 4.1 %collective-permute-start.18 = (bf16[384,384]{1,0:T(8,128)(2,1)S(1)}, bf16[384,384]{1,0:T(8,128)(2,1)S(1)}, u32[]{:S(2)}, u32[]{:S(2)}) collective-permute-start(bf16[384,384]{1,0:T(8,128)(2,1)S(1)} %shard_map.99), channel_id=1, source_target_pairs={{7,6},{15,14},{23,22},{5,4}} | collective-permute-start | bytes 884744 | tf_op jit(solution)/shard_map/ppermute | solution.py:348

commit v7 on v6

--- a/solution.py
+++ b/solution.py
@@ -30,7 +30,7 @@
         allowed = {"left", "down"}
         if apart:
             turn = {kind for _, _, kind in todo}
-            allowed = turn if len(turn) == 1 else {"left" if len(ops) % 2 == 0 else "down"}
+            allowed = turn if len(turn) == 1 else {"down" if 0 < len(ops) < 4 else "left"}
         busy = [source for source, _, _ in todo]
         waiting = {targets[0]: busy.count(source) for source, targets, kind in todo if kind == "down"}
         for item in list(todo):
@@ -47,6 +47,42 @@
                     break
         ops.append(op)
     return ops + [forwards] if forwards else ops
+
+
+def chain(rows_n, cols_n, offset):
+    first, steps, ups = [], [], []
+    for i in range(rows_n):
+        m = i + offset
+        if not 0 <= m < cols_n:
+            continue
+        chips = {}
+        for j in range(m + 3, cols_n):
+            if j // 2 != (m + 2) // 2:
+                chips.setdefault(j // 2, []).append((i, j))
+        leads = [max(chips[chip]) for chip in sorted(chips)]
+        for n, lead in enumerate(leads):
+            if n == 0:
+                first.append(((i, m), lead, "left", None))
+            mates = [t for t in chips[lead[1] // 2] if t != lead]
+            onward = leads[n + 1 : n + 2]
+            for k, target in enumerate(onward + mates):
+                while len(steps) < n + k + 1:
+                    steps.append([])
+                steps[n + k].append((lead, target))
+        ups += [((i, m), (k, m), "down", None) for k in range(i - 2)]
+    ops = [first]
+    for edge in ups:
+        for op in ops + [[]]:
+            if all(edge[0] != other[0] and edge[1] != other[1] for other in op):
+                if not op:
+                    ops.append(op)
+                op.append(edge)
+                break
+    came = {target: 0 for _, target, _, _ in first}
+    for step in steps:
+        came.update({target: len(ops) for _, target in step if target not in came})
+        ops.append([(lead, target, "left", came[lead]) for lead, target in step])
+    return ops
 
 
 def one_of(me, ids):
@@ -352,12 +388,16 @@
     rows_n, cols_n = mesh.shape["row"], mesh.shape["col"]
     first = (rows_n + cols_n) // 2 - 2
     offset = first - rows_n + 1
-    ops0 = plan(rows_n, cols_n, offset, 3, 3)
+    ops0 = chain(rows_n, cols_n, offset)
     ops1 = plan(rows_n, cols_n, offset + 1, 2, 2)
     ops2 = plan(rows_n, cols_n, offset + 2, 1, 1, True)
 
     def owners(t):
         return [(i, i + offset + t) for i in range(rows_n) if 0 <= i + offset + t < cols_n]
+
+    beside = [
+        ((i, j + 2), (i, j + 3), "left", None) for i, j in owners(0) if (j + 2) % 2 == 0 and j + 3 < cols_n
+    ]
 
     def up(t, far):
         return [(i * cols_n + j, (i - far) * cols_n + j) for i, j in owners(t) if i >= far]
@@ -420,6 +460,7 @@
         down_far = move(f0, up(0, 2))
         left_far = move(f0, right(0, 2))
         far0 = spread(ops0, cols_n, f0, "a", call)
+        far0.append(move(left_far, [(a[0] * cols_n + a[1], b[0] * cols_n + b[1]) for a, b, _, _ in beside]))
         *basis, coup, s, a0, b0, a1, b1, a2, b2 = call(
             functools.partial(prepare, rows_n, first),
             [rhs, a_c, b_c, u, v, a_vals, b_vals],
@@ -441,7 +482,7 @@
         )
         far1 = spread(ops1, cols_n, f1, "b", call)
         (f2,) = advance(1, down, left, s1, a1, b1)
-        for k, (ops, far, a, b) in enumerate(((ops0, far0, a0, b0), (ops1, far1, a1, b1))):
+        for k, (ops, far, a, b) in enumerate(((ops0 + [beside], far0, a0, b0), (ops1, far1, a1, b1))):
             (s,) = call(
                 functools.partial(middle, rows_n, cols_n, first, ops),
                 [],

time: 42.4 us -> 42.1 us (level)
  the two profiles are of different devices: /device:TPU:17 before, /device:TPU:16 now
where the time goes in v7:
time: 42.1 us; the launch traced here: 41.7 us
  starting transfers between devices  19.6 us (47%)
  waiting for transfers between devices  15 us (36%)
  Pallas kernels  5.94 us (14%)
  between operations  1.18 us (3%)
    ppermute x20, starting transfers between devices, move(): return lax.ppermute(value, AXES, pairs)  19.6 us
    ppermute x20, waiting for transfers between devices, move(): return lax.ppermute(value, AXES, pairs)  15 us
    pallas_call x16, Pallas kernels, call(): pl.pallas_call(kernel, out_shape=outs, in_specs=[FAR_SPEC] * len(far) + [...  5.94 us
  transfers between devices with their start and end apart: 20, of which 3 were waited for; matrix products, arithmetic and copies ran while one was open for 0% of the time, Pallas kernels for 11%

profile of v7, /device:TPU:16, one launch (start us, length us, event | category | flops | bytes accessed | tf_op | source)
XLA Modules:
  0.0 41.7 jit_solution(8064488108582010204)
XLA Ops:
  0.7 0.7 %collective-permute-start.1 = (bf16[384,384]{1,0:T(8,128)(2,1)S(1)}, bf16[384,384]{1,0:T(8,128)(2,1)S(1)}, u32[]{:S(2)}, u32[]{:S(2)}) collective-permute-start(bf16[384,384]{1,0:T(8,128)(2,1)S(1)} %shard_map.86.f0.own), channel_id=1, source_target_pairs={{1,2},{10,11},{19,20},{28,29}} | collective-permute-start | bytes 884744 | tf_op jit(solution)/shard_map/ppermute | solution.py:384
  1.4 0.7 %collective-permute-start = (bf16[384,384]{1,0:T(8,128)(2,1)S(1)}, bf16[384,384]{1,0:T(8,128)(2,1)S(1)}, u32[]{:S(2)}, u32[]{:S(2)}) collective-permute-start(bf16[384,384]{1,0:T(8,128)(2,1)S(1)} %shard_map.86.f0.own), channel_id=1, source_target_pairs={{10,2},{19,11},{28,20}} | collective-permute-start | bytes 884744 | tf_op jit(solution)/shard_map/ppermute | solution.py:384
  2.1 1.3 %collective-permute-start.6 = (bf16[384,384]{1,0:T(8,128)(2,1)S(1)}, bf16[384,384]{1,0:T(8,128)(2,1)S(1)}, u32[]{:S(2)}, u32[]{:S(2)}) collective-permute-start(bf16[384,384]{1,0:T(8,128)(2,1)S(1)} %shard_map.86.f0.own), channel_id=1, source_target_pairs={{1,5},{10,15},{19,23},{28,4}} | collective-permute-start | bytes 884744 | tf_op jit(solution)/shard_map/ppermute | solution.py:384
  3.4 0.7 %collective-permute-start.5 = (bf16[384,384]{1,0:T(8,128)(2,1)S(1)}, bf16[384,384]{1,0:T(8,128)(2,1)S(1)}, u32[]{:S(2)}, u32[]{:S(2)}) collective-permute-start(bf16[384,384]{1,0:T(8,128)(2,1)S(1)} %shard_map.86.f0.own), channel_id=1, source_target_pairs={{1,3},{10,12},{19,21},{28,30}} | collective-permute-start | bytes 884744 | tf_op jit(solution)/shard_map/ppermute | solution.py:384
  4.1 0.7 %collective-permute-start.4 = (bf16[384,384]{1,0:T(8,128)(2,1)S(1)}, bf16[384,384]{1,0:T(8,128)(2,1)S(1)}, u32[]{:S(2)}, u32[]{:S(2)}) collective-permute-start(bf16[384,384]{1,0:T(8,128)(2,1)S(1)} %shard_map.86.f0.own), channel_id=1, source_target_pairs={{19,3},{28,12}} | collective-permute-start | bytes 884744 | tf_op jit(solution)/shard_map/ppermute | solution.py:384
  4.7 1.7 %shard_map.87 = (bf16[384,1152]{1,0:T(8,128)(2,1)S(1)}, bf16[384,1152]{1,0:T(8,128)(2,1)S(1)}, bf16[1152,384]{1,0:T(8,128)(2,1)S(1)}, bf16[384,1152]{1,0:T(8,128...) custom-call(f32[384,384]{1,0:T(8,128)} %rhs.3, ...), custom_call_target="tpu_custom_call" | custom-call | tf_op jit(solution)/shard_map/pallas_call | solution.py:420
  6.5 0.7 %collective-permute-start.3 = (bf16[384,384]{1,0:T(8,128)(2,1)S(1)}, bf16[384,384]{1,0:T(8,128)(2,1)S(1)}, u32[]{:S(2)}, u32[]{:S(2)}) collective-permute-start(bf16[384,384]{1,0:T(8,128)(2,1)S(1)} %shard_map.89.f1.own), channel_id=1, source_target_pairs={{2,3},{11,12},{20,21},{29,30}} | collective-permute-start | bytes 884744 | tf_op jit(solution)/shard_map/ppermute | solution.py:384
  7.2 0.7 %collective-permute-start.2 = (bf16[384,384]{1,0:T(8,128)(2,1)S(1)}, bf16[384,384]{1,0:T(8,128)(2,1)S(1)}, u32[]{:S(2)}, u32[]{:S(2)}) collective-permute-start(bf16[384,384]{1,0:T(8,128)(2,1)S(1)} %shard_map.89.f1.own), channel_id=1, source_target_pairs={{11,3},{20,12},{29,21}} | collective-permute-start | bytes 884744 | tf_op jit(solution)/shard_map/ppermute | solution.py:384
  7.9 9.9 %collective-permute-done.6.rest_0_ = bf16[384,384]{1,0:T(8,128)(2,1)S(1)} collective-permute-done((bf16[384,384]{1,0:T(8,128)(2,1)S(1)}, bf16[384,384]{1,0:T(8,128)(2,1)S(1)}, u32[]{:S(2)}, u32[]{:S(2)}) %collective-permute-start.6) | collective-permute-done | bytes 294944 | tf_op jit(solution)/shard_map/ppermute | solution.py:384
  18.5 0.7 %collective-permute-start.7 = (bf16[384,384]{1,0:T(8,128)(2,1)S(1)}, bf16[384,384]{1,0:T(8,128)(2,1)S(1)}, u32[]{:S(2)}, u32[]{:S(2)}) collective-permute-start(bf16[384,384]{1,0:T(8,128)(2,1)S(1)} %shard_map.94), channel_id=1, source_target_pairs={{5,7},{15,14},{23,22}} | collective-permute-start | bytes 884744 | tf_op jit(solution)/shard_map/ppermute | solution.py:384
  19.2 1.3 %collective-permute-start.11 = (bf16[384,384]{1,0:T(8,128)(2,1)S(1)}, bf16[384,384]{1,0:T(8,128)(2,1)S(1)}, u32[]{:S(2)}, u32[]{:S(2)}) collective-permute-start(bf16[384,384]{1,0:T(8,128)(2,1)S(1)} %shard_map.89.f1.own), channel_id=1, source_target_pairs={{2,4},{11,13},{29,5}} | collective-permute-start | bytes 884744 | tf_op jit(solution)/shard_map/ppermute | solution.py:384
  20.5 1.3 %collective-permute-start.12 = (bf16[384,384]{1,0:T(8,128)(2,1)S(1)}, bf16[384,384]{1,0:T(8,128)(2,1)S(1)}, u32[]{:S(2)}, u32[]{:S(2)}) collective-permute-start(bf16[384,384]{1,0:T(8,128)(2,1)S(1)} %shard_map.89.f1.own), channel_id=1, source_target_pairs={{20,4},{29,13}} | collective-permute-start | bytes 884744 | tf_op jit(solution)/shard_map/ppermute | solution.py:384
  21.9 0.7 %collective-permute-start.9 = (bf16[384,384]{1,0:T(8,128)(2,1)S(1)}, bf16[384,384]{1,0:T(8,128)(2,1)S(1)}, u32[]{:S(2)}, u32[]{:S(2)}) collective-permute-start(bf16[384,384]{1,0:T(8,128)(2,1)S(1)} %collective-permute-done.5.left), channel_id=1, source_target_pairs={{12,13},{30,31}} | collective-permute-start | bytes 884744 | tf_op jit(solution)/shard_map/ppermute | solution.py:384
  22.6 0.7 %collective-permute-start.17 = (bf16[384,384]{1,0:T(8,128)(2,1)S(1)}, bf16[384,384]{1,0:T(8,128)(2,1)S(1)}, u32[]{:S(2)}, u32[]{:S(2)}) collective-permute-start(bf16[384,384]{1,0:T(8,128)(2,1)S(1)} %shard_map.92.f2.own), channel_id=1, source_target_pairs={{3,7},{12,15},{21,23},{30,31}} | collective-permute-start | bytes 884744 | tf_op jit(solution)/shard_map/ppermute | solution.py:384
  24.1 3.8 %collective-permute-done.11.rest_1_ = bf16[384,384]{1,0:T(8,128)(2,1)S(1)} collective-permute-done((bf16[384,384]{1,0:T(8,128)(2,1)S(1)}, bf16[384,384]{1,0:T(8,128)(2,1)S(1)}, u32[]{:S(2)}, u32[]{:S(2)}) %collective-permute-start.11) | collective-permute-done | bytes 294944 | tf_op jit(solution)/shard_map/ppermute | solution.py:384
  27.8 1.5 %collective-permute-start.8 = (bf16[384,384]{1,0:T(8,128)(2,1)S(1)}, bf16[384,384]{1,0:T(8,128)(2,1)S(1)}, u32[]{:S(2)}, u32[]{:S(2)}) collective-permute-start(bf16[384,384]{1,0:T(8,128)(2,1)S(1)} %shard_map.95), channel_id=1, source_target_pairs={{5,4},{7,6}} | collective-permute-start | bytes 884744 | tf_op jit(solution)/shard_map/ppermute | solution.py:384
  29.4 1.3 %collective-permute-start.14 = (bf16[384,384]{1,0:T(8,128)(2,1)S(1)}, bf16[384,384]{1,0:T(8,128)(2,1)S(1)}, u32[]{:S(2)}, u32[]{:S(2)}) collective-permute-start(bf16[384,384]{1,0:T(8,128)(2,1)S(1)} %shard_map.92.f2.own), channel_id=1, source_target_pairs={{12,4},{21,5},{30,6}} | collective-permute-start | bytes 884744 | tf_op jit(solution)/shard_map/ppermute | solution.py:384
  30.7 2.9 %collective-permute-start.13 = (bf16[384,384]{1,0:T(8,128)(2,1)S(1)}, bf16[384,384]{1,0:T(8,128)(2,1)S(1)}, u32[]{:S(2)}, u32[]{:S(2)}) collective-permute-start(bf16[384,384]{1,0:T(8,128)(2,1)S(1)} %shard_map.97), channel_id=1, source_target_pairs={{7,6},{15,14},{23,22},{4,5}} | collective-permute-start | bytes 884744 | tf_op jit(solution)/shard_map/ppermute | solution.py:384
  35.0 1.3 %collective-permute-start.19 = (bf16[384,384]{1,0:T(8,128)(2,1)S(1)}, bf16[384,384]{1,0:T(8,128)(2,1)S(1)}, u32[]{:S(2)}, u32[]{:S(2)}) collective-permute-start(bf16[384,384]{1,0:T(8,128)(2,1)S(1)} %shard_map.100), channel_id=1, source_target_pairs={{7,6},{15,14},{23,22},{5,4}} | collective-permute-start | bytes 884744 | tf_op jit(solution)/shard_map/ppermute | solution.py:384
  36.3 0.8 %shard_map.93 = bf16[384,384]{1,0:T(8,128)(2,1)} custom-call(bf16[384,384]{1,0:T(8,128)(2,1)S(1)} %shard_map.86.f0.own, bf16[384,384]{1,0:T(8,128)(2,1)S(1)} %shard_map.89.f1.own, bf16[384,384]{1,0:T(8,128)(2,1)S(1)} %shard_map.92.f2.own), custom_call_target="tpu_custom_call" | custom-call | tf_op jit(solution)/shard_map/pallas_call | solution.py:420
  37.1 0.8 %shard_map.96.s1 = f32[384,384]{1,0:T(8,128)S(1)} custom-call(f32[384,384]{1,0:T(8,128)S(1)} %get-tuple-element.15.s.s1, bf16[384,384]{1,0:T(8,128)(2,1)S(1)} %get-tuple-element.20.coup_a.a0.a1, bf16[384,384]{1,0:T(8,128)(2,1)S(1)} %get-tuple-element.16.coup_b.b0.b1, bf16[384,384]{1,0:T(8,128)(2,1)S(1)} %collective-permute-done.6.rest_0_, ...), custom_call_target="tpu_custom_call" | custom-call | tf_op jit(solution)/shard_map/pallas_call | solution.py:420
  37.9 0.8 %shard_map.98.s2 = f32[384,384]{1,0:T(8,128)S(1)} custom-call(f32[384,384]{1,0:T(8,128)S(1)} %shard_map.96.s1, bf16[384,384]{1,0:T(8,128)(2,1)S(1)} %get-tuple-element.25.coup_a.a1, bf16[384,384]{1,0:T(8,128)(2,1)S(1)} %get-tuple-element.24.coup_b.b1, bf16[384,384]{1,0:T(8,128)(2,1)S(1)} %collective-permute-done.10.rest_0_, ...), custom_call_target="tpu_custom_call" | custom-call | tf_op jit(solution)/shard_map/pallas_call | solution.py:420
  38.7 1.3 %collective-permute-done.14.rest_0_.rest_1_ = bf16[384,384]{1,0:T(8,128)(2,1)S(1)} collective-permute-done((bf16[384,384]{1,0:T(8,128)(2,1)S(1)}, bf16[384,384]{1,0:T(8,128)(2,1)S(1)}, u32[]{:S(2)}, u32[]{:S(2)}) %collective-permute-start.14) | collective-permute-done | bytes 294944 | tf_op jit(solution)/shard_map/ppermute | solution.py:384
  40.4 1.1 %shard_map.101 = f32[384,384]{1,0:T(8,128)} custom-call(f32[384,384]{1,0:T(8,128)S(1)} %shard_map.99.s3, bf16[384,384]{1,0:T(8,128)(2,1)S(1)} %get-tuple-element.27.b2, bf16[384,384]{1,0:T(8,128)(2,1)S(1)} %collective-permute-done.17.rest_0_, bf16[384,384]{1,0:T(8,128)(2,1)S(1)} %collective-permute-done.14.rest_0_.rest_1_, ...), custom_call_target="tpu_custom_call" | custom-call | tf_op jit(solution)/shard_map/pallas_call | solution.py:420
  (32 shorter events, 3.5 us)
Async XLA Ops:
  0.7 5.7 %collective-permute-start.1 = (bf16[384,384]{1,0:T(8,128)(2,1)S(1)}, bf16[384,384]{1,0:T(8,128)(2,1)S(1)}, u32[]{:S(2)}, u32[]{:S(2)}) collective-permute-start(bf16[384,384]{1,0:T(8,128)(2,1)S(1)} %shard_map.86.f0.own), channel_id=1, source_target_pairs={{1,2},{10,11},{19,20},{28,29}} | collective-permute-start | bytes 884744 | tf_op jit(solution)/shard_map/ppermute | solution.py:384
  1.4 5.1 %collective-permute-start = (bf16[384,384]{1,0:T(8,128)(2,1)S(1)}, bf16[384,384]{1,0:T(8,128)(2,1)S(1)}, u32[]{:S(2)}, u32[]{:S(2)}) collective-permute-start(bf16[384,384]{1,0:T(8,128)(2,1)S(1)} %shard_map.86.f0.own), channel_id=1, source_target_pairs={{10,2},{19,11},{28,20}} | collective-permute-start | bytes 884744 | tf_op jit(solution)/shard_map/ppermute | solution.py:384
  2.1 15.7 %collective-permute-start.6 = (bf16[384,384]{1,0:T(8,128)(2,1)S(1)}, bf16[384,384]{1,0:T(8,128)(2,1)S(1)}, u32[]{:S(2)}, u32[]{:S(2)}) collective-permute-start(bf16[384,384]{1,0:T(8,128)(2,1)S(1)} %shard_map.86.f0.own), channel_id=1, source_target_pairs={{1,5},{10,15},{19,23},{28,4}} | collective-permute-start | bytes 884744 | tf_op jit(solution)/shard_map/ppermute | solution.py:384
  3.4 15.1 %collective-permute-start.5 = (bf16[384,384]{1,0:T(8,128)(2,1)S(1)}, bf16[384,384]{1,0:T(8,128)(2,1)S(1)}, u32[]{:S(2)}, u32[]{:S(2)}) collective-permute-start(bf16[384,384]{1,0:T(8,128)(2,1)S(1)} %shard_map.86.f0.own), channel_id=1, source_target_pairs={{1,3},{10,12},{19,21},{28,30}} | collective-permute-start | bytes 884744 | tf_op jit(solution)/shard_map/ppermute | solution.py:384
  4.1 15.1 %collective-permute-start.4 = (bf16[384,384]{1,0:T(8,128)(2,1)S(1)}, bf16[384,384]{1,0:T(8,128)(2,1)S(1)}, u32[]{:S(2)}, u32[]{:S(2)}) collective-permute-start(bf16[384,384]{1,0:T(8,128)(2,1)S(1)} %shard_map.86.f0.own), channel_id=1, source_target_pairs={{19,3},{28,12}} | collective-permute-start | bytes 884744 | tf_op jit(solution)/shard_map/ppermute | solution.py:384
  6.5 14.0 %collective-permute-start.3 = (bf16[384,384]{1,0:T(8,128)(2,1)S(1)}, bf16[384,384]{1,0:T(8,128)(2,1)S(1)}, u32[]{:S(2)}, u32[]{:S(2)}) collective-permute-start(bf16[384,384]{1,0:T(8,128)(2,1)S(1)} %shard_map.89.f1.own), channel_id=1, source_target_pairs={{2,3},{11,12},{20,21},{29,30}} | collective-permute-start | bytes 884744 | tf_op jit(solution)/shard_map/ppermute | solution.py:384
  7.2 14.7 %collective-permute-start.2 = (bf16[384,384]{1,0:T(8,128)(2,1)S(1)}, bf16[384,384]{1,0:T(8,128)(2,1)S(1)}, u32[]{:S(2)}, u32[]{:S(2)}) collective-permute-start(bf16[384,384]{1,0:T(8,128)(2,1)S(1)} %shard_map.89.f1.own), channel_id=1, source_target_pairs={{11,3},{20,12},{29,21}} | collective-permute-start | bytes 884744 | tf_op jit(solution)/shard_map/ppermute | solution.py:384
  17.8 4.8 %collective-permute-start.10 = (bf16[384,384]{1,0:T(8,128)(2,1)S(1)}, bf16[384,384]{1,0:T(8,128)(2,1)S(1)}, u32[]{:S(2)}, u32[]{:S(2)}) collective-permute-start(bf16[384,384]{1,0:T(8,128)(2,1)S(1)} %shard_map.89.f1.own), channel_id=1, source_target_pairs={{2,7},{11,15},{20,23},{29,31}} | collective-permute-start | bytes 884744 | tf_op jit(solution)/shard_map/ppermute | solution.py:384
  18.5 4.8 %collective-permute-start.7 = (bf16[384,384]{1,0:T(8,128)(2,1)S(1)}, bf16[384,384]{1,0:T(8,128)(2,1)S(1)}, u32[]{:S(2)}, u32[]{:S(2)}) collective-permute-start(bf16[384,384]{1,0:T(8,128)(2,1)S(1)} %shard_map.94), channel_id=1, source_target_pairs={{5,7},{15,14},{23,22}} | collective-permute-start | bytes 884744 | tf_op jit(solution)/shard_map/ppermute | solution.py:384
  19.2 8.6 %collective-permute-start.11 = (bf16[384,384]{1,0:T(8,128)(2,1)S(1)}, bf16[384,384]{1,0:T(8,128)(2,1)S(1)}, u32[]{:S(2)}, u32[]{:S(2)}) collective-permute-start(bf16[384,384]{1,0:T(8,128)(2,1)S(1)} %shard_map.89.f1.own), channel_id=1, source_target_pairs={{2,4},{11,13},{29,5}} | collective-permute-start | bytes 884744 | tf_op jit(solution)/shard_map/ppermute | solution.py:384
  20.5 10.1 %collective-permute-start.12 = (bf16[384,384]{1,0:T(8,128)(2,1)S(1)}, bf16[384,384]{1,0:T(8,128)(2,1)S(1)}, u32[]{:S(2)}, u32[]{:S(2)}) collective-permute-start(bf16[384,384]{1,0:T(8,128)(2,1)S(1)} %shard_map.89.f1.own), channel_id=1, source_target_pairs={{20,4},{29,13}} | collective-permute-start | bytes 884744 | tf_op jit(solution)/shard_map/ppermute | solution.py:384
  21.9 7.5 %collective-permute-start.9 = (bf16[384,384]{1,0:T(8,128)(2,1)S(1)}, bf16[384,384]{1,0:T(8,128)(2,1)S(1)}, u32[]{:S(2)}, u32[]{:S(2)}) collective-permute-start(bf16[384,384]{1,0:T(8,128)(2,1)S(1)} %collective-permute-done.5.left), channel_id=1, source_target_pairs={{12,13},{30,31}} | collective-permute-start | bytes 884744 | tf_op jit(solution)/shard_map/ppermute | solution.py:384
  22.6 10.9 %collective-permute-start.17 = (bf16[384,384]{1,0:T(8,128)(2,1)S(1)}, bf16[384,384]{1,0:T(8,128)(2,1)S(1)}, u32[]{:S(2)}, u32[]{:S(2)}) collective-permute-start(bf16[384,384]{1,0:T(8,128)(2,1)S(1)} %shard_map.92.f2.own), channel_id=1, source_target_pairs={{3,7},{12,15},{21,23},{30,31}} | collective-permute-start | bytes 884744 | tf_op jit(solution)/shard_map/ppermute | solution.py:384
  23.3 10.9 %collective-permute-start.18 = (bf16[384,384]{1,0:T(8,128)(2,1)S(1)}, bf16[384,384]{1,0:T(8,128)(2,1)S(1)}, u32[]{:S(2)}, u32[]{:S(2)}) collective-permute-start(bf16[384,384]{1,0:T(8,128)(2,1)S(1)} %shard_map.92.f2.own), channel_id=1, source_target_pairs={{3,5},{12,13}} | collective-permute-start | bytes 884744 | tf_op jit(solution)/shard_map/ppermute | solution.py:384
  27.8 7.2 %collective-permute-start.8 = (bf16[384,384]{1,0:T(8,128)(2,1)S(1)}, bf16[384,384]{1,0:T(8,128)(2,1)S(1)}, u32[]{:S(2)}, u32[]{:S(2)}) collective-permute-start(bf16[384,384]{1,0:T(8,128)(2,1)S(1)} %shard_map.95), channel_id=1, source_target_pairs={{5,4},{7,6}} | collective-permute-start | bytes 884744 | tf_op jit(solution)/shard_map/ppermute | solution.py:384
  29.4 10.6 %collective-permute-start.14 = (bf16[384,384]{1,0:T(8,128)(2,1)S(1)}, bf16[384,384]{1,0:T(8,128)(2,1)S(1)}, u32[]{:S(2)}, u32[]{:S(2)}) collective-permute-start(bf16[384,384]{1,0:T(8,128)(2,1)S(1)} %shard_map.92.f2.own), channel_id=1, source_target_pairs={{12,4},{21,5},{30,6}} | collective-permute-start | bytes 884744 | tf_op jit(solution)/shard_map/ppermute | solution.py:384
  30.7 7.2 %collective-permute-start.13 = (bf16[384,384]{1,0:T(8,128)(2,1)S(1)}, bf16[384,384]{1,0:T(8,128)(2,1)S(1)}, u32[]{:S(2)}, u32[]{:S(2)}) collective-permute-start(bf16[384,384]{1,0:T(8,128)(2,1)S(1)} %shard_map.97), channel_id=1, source_target_pairs={{7,6},{15,14},{23,22},{4,5}} | collective-permute-start | bytes 884744 | tf_op jit(solution)/shard_map/ppermute | solution.py:384
  33.6 6.4 %collective-permute-start.15 = (bf16[384,384]{1,0:T(8,128)(2,1)S(1)}, bf16[384,384]{1,0:T(8,128)(2,1)S(1)}, u32[]{:S(2)}, u32[]{:S(2)}) collective-permute-start(bf16[384,384]{1,0:T(8,128)(2,1)S(1)} %shard_map.92.f2.own), channel_id=1, source_target_pairs={{21,13},{30,14}} | collective-permute-start | bytes 884744 | tf_op jit(solution)/shard_map/ppermute | solution.py:384
  34.3 5.7 %collective-permute-start.16 = (bf16[384,384]{1,0:T(8,128)(2,1)S(1)}, bf16[384,384]{1,0:T(8,128)(2,1)S(1)}, u32[]{:S(2)}, u32[]{:S(2)}) collective-permute-start(bf16[384,384]{1,0:T(8,128)(2,1)S(1)} %shard_map.92.f2.own), channel_id=1, source_target_pairs={{30,22}} | collective-permute-start | bytes 884744 | tf_op jit(solution)/shard_map/ppermute | solution.py:384
  35.0 5.4 %collective-permute-start.19 = (bf16[384,384]{1,0:T(8,128)(2,1)S(1)}, bf16[384,384]{1,0:T(8,128)(2,1)S(1)}, u32[]{:S(2)}, u32[]{:S(2)}) collective-permute-start(bf16[384,384]{1,0:T(8,128)(2,1)S(1)} %shard_map.100), channel_id=1, source_target_pairs={{7,6},{15,14},{23,22},{5,4}} | collective-permute-start | bytes 884744 | tf_op jit(solution)/shard_map/ppermute | solution.py:384

commit v8 on v7

--- a/solution.py
+++ b/solution.py
@@ -19,10 +19,11 @@
         m = i + offset
         if 0 <= m < cols_n:
             targets = range(m + gap, cols_n)
-            for chip in sorted({j // 2 for j in targets}, reverse=True):
+            for chip in sorted({j // 2 for j in targets}, reverse=apart):
                 some = [(i, j) for j in targets if j // 2 == chip]
                 (last if chip == m // 2 else rights).append(((i, m), some, "left"))
-            ups += [((i, m), [(k, m)], "down") for k in range(i - up_gap + 1)]
+            above = list(range(i - up_gap + 1))
+            ups += [((i, m), [(k, m)], "down") for k in above[:1] + above[1:][-1:] + above[1:-1]]
     todo = rights + ups + last
     ops, forwards = [], []
     while todo:
@@ -35,7 +36,7 @@
         waiting = {targets[0]: busy.count(source) for source, targets, kind in todo if kind == "down"}
         for item in list(todo):
             source, targets, kind = item
-            if kind not in allowed:
+            if kind not in allowed or (apart and not ops and item in last and rights):
                 continue
             for target in sorted(targets, key=lambda t: (waiting.get(t, 0), -t[1])):
                 if source not in used_from and target not in used_to:

time: 42.1 us -> 42.6 us (1.012)
  the two profiles are of different devices: /device:TPU:16 before, /device:TPU:19 now
where the time goes in v8:
time: 42.6 us; the launch traced here: 42.3 us
  waiting for transfers between devices  18.7 us (44%)
  starting transfers between devices  16.8 us (39%)
  Pallas kernels  5.59 us (13%)
  between operations  1.18 us (3%)
    ppermute x20, waiting for transfers between devices, move(): return lax.ppermute(value, AXES, pairs)  18.7 us
    ppermute x20, starting transfers between devices, move(): return lax.ppermute(value, AXES, pairs)  16.8 us
    pallas_call x16, Pallas kernels, call(): pl.pallas_call(kernel, out_shape=outs, in_specs=[FAR_SPEC] * len(far) + [...  5.59 us
  transfers between devices with their start and end apart: 20, of which 4 were waited for; matrix products, arithmetic and copies ran while one was open for 0% of the time, Pallas kernels for 10%

profile of v8, /device:TPU:19, one launch (start us, length us, event | category | flops | bytes accessed | tf_op | source)
XLA Modules:
  0.0 42.3 jit_solution(2407795987946878879)
XLA Ops:
  0.7 0.7 %collective-permute-start.1 = (bf16[384,384]{1,0:T(8,128)(2,1)S(1)}, bf16[384,384]{1,0:T(8,128)(2,1)S(1)}, u32[]{:S(2)}, u32[]{:S(2)}) collective-permute-start(bf16[384,384]{1,0:T(8,128)(2,1)S(1)} %shard_map.86.f0.own), channel_id=1, source_target_pairs={{1,2},{10,11},{19,20},{28,29}} | collective-permute-start | bytes 884744 | tf_op jit(solution)/shard_map/ppermute | solution.py:385
  1.4 0.7 %collective-permute-start = (bf16[384,384]{1,0:T(8,128)(2,1)S(1)}, bf16[384,384]{1,0:T(8,128)(2,1)S(1)}, u32[]{:S(2)}, u32[]{:S(2)}) collective-permute-start(bf16[384,384]{1,0:T(8,128)(2,1)S(1)} %shard_map.86.f0.own), channel_id=1, source_target_pairs={{10,2},{19,11},{28,20}} | collective-permute-start | bytes 884744 | tf_op jit(solution)/shard_map/ppermute | solution.py:385
  2.1 0.7 %collective-permute-start.6 = (bf16[384,384]{1,0:T(8,128)(2,1)S(1)}, bf16[384,384]{1,0:T(8,128)(2,1)S(1)}, u32[]{:S(2)}, u32[]{:S(2)}) collective-permute-start(bf16[384,384]{1,0:T(8,128)(2,1)S(1)} %shard_map.86.f0.own), channel_id=1, source_target_pairs={{1,5},{10,15},{19,23},{28,4}} | collective-permute-start | bytes 884744 | tf_op jit(solution)/shard_map/ppermute | solution.py:385
  3.4 0.7 %collective-permute-start.4 = (bf16[384,384]{1,0:T(8,128)(2,1)S(1)}, bf16[384,384]{1,0:T(8,128)(2,1)S(1)}, u32[]{:S(2)}, u32[]{:S(2)}) collective-permute-start(bf16[384,384]{1,0:T(8,128)(2,1)S(1)} %shard_map.86.f0.own), channel_id=1, source_target_pairs={{19,3},{28,12}} | collective-permute-start | bytes 884744 | tf_op jit(solution)/shard_map/ppermute | solution.py:385
  4.1 1.7 %shard_map.87 = (bf16[384,1152]{1,0:T(8,128)(2,1)S(1)}, bf16[384,1152]{1,0:T(8,128)(2,1)S(1)}, bf16[1152,384]{1,0:T(8,128)(2,1)S(1)}, bf16[384,1152]{1,0:T(8,128...) custom-call(f32[384,384]{1,0:T(8,128)} %rhs.3, ...), custom_call_target="tpu_custom_call" | custom-call | tf_op jit(solution)/shard_map/pallas_call | solution.py:421
  5.9 0.7 %collective-permute-start.3 = (bf16[384,384]{1,0:T(8,128)(2,1)S(1)}, bf16[384,384]{1,0:T(8,128)(2,1)S(1)}, u32[]{:S(2)}, u32[]{:S(2)}) collective-permute-start(bf16[384,384]{1,0:T(8,128)(2,1)S(1)} %shard_map.89.f1.own), channel_id=1, source_target_pairs={{2,3},{11,12},{20,21},{29,30}} | collective-permute-start | bytes 884744 | tf_op jit(solution)/shard_map/ppermute | solution.py:385
  6.6 0.7 %collective-permute-start.2 = (bf16[384,384]{1,0:T(8,128)(2,1)S(1)}, bf16[384,384]{1,0:T(8,128)(2,1)S(1)}, u32[]{:S(2)}, u32[]{:S(2)}) collective-permute-start(bf16[384,384]{1,0:T(8,128)(2,1)S(1)} %shard_map.89.f1.own), channel_id=1, source_target_pairs={{11,3},{20,12},{29,21}} | collective-permute-start | bytes 884744 | tf_op jit(solution)/shard_map/ppermute | solution.py:385
  7.3 1.3 %collective-permute-start.10 = (bf16[384,384]{1,0:T(8,128)(2,1)S(1)}, bf16[384,384]{1,0:T(8,128)(2,1)S(1)}, u32[]{:S(2)}, u32[]{:S(2)}) collective-permute-start(bf16[384,384]{1,0:T(8,128)(2,1)S(1)} %shard_map.89.f1.own), channel_id=1, source_target_pairs={{2,4},{11,13},{20,23},{29,31}} | collective-permute-start | bytes 884744 | tf_op jit(solution)/shard_map/ppermute | solution.py:385
  8.7 0.7 %collective-permute-start.7 = (bf16[384,384]{1,0:T(8,128)(2,1)S(1)}, bf16[384,384]{1,0:T(8,128)(2,1)S(1)}, u32[]{:S(2)}, u32[]{:S(2)}) collective-permute-start(bf16[384,384]{1,0:T(8,128)(2,1)S(1)} %shard_map.94), channel_id=1, source_target_pairs={{5,7},{15,14},{23,22}} | collective-permute-start | bytes 884744 | tf_op jit(solution)/shard_map/ppermute | solution.py:385
  9.4 0.7 %collective-permute-start.11 = (bf16[384,384]{1,0:T(8,128)(2,1)S(1)}, bf16[384,384]{1,0:T(8,128)(2,1)S(1)}, u32[]{:S(2)}, u32[]{:S(2)}) collective-permute-start(bf16[384,384]{1,0:T(8,128)(2,1)S(1)} %shard_map.89.f1.own), channel_id=1, source_target_pairs={{2,7},{11,15},{20,4},{29,5}} | collective-permute-start | bytes 884744 | tf_op jit(solution)/shard_map/ppermute | solution.py:385
  10.1 1.3 %collective-permute-start.12 = (bf16[384,384]{1,0:T(8,128)(2,1)S(1)}, bf16[384,384]{1,0:T(8,128)(2,1)S(1)}, u32[]{:S(2)}, u32[]{:S(2)}) collective-permute-start(bf16[384,384]{1,0:T(8,128)(2,1)S(1)} %shard_map.89.f1.own), channel_id=1, source_target_pairs={{29,13}} | collective-permute-start | bytes 884744 | tf_op jit(solution)/shard_map/ppermute | solution.py:385
  11.4 1.3 %collective-permute-start.9 = (bf16[384,384]{1,0:T(8,128)(2,1)S(1)}, bf16[384,384]{1,0:T(8,128)(2,1)S(1)}, u32[]{:S(2)}, u32[]{:S(2)}) collective-permute-start(bf16[384,384]{1,0:T(8,128)(2,1)S(1)} %collective-permute-done.5.left), channel_id=1, source_target_pairs={{12,13},{30,31}} | collective-permute-start | bytes 884744 | tf_op jit(solution)/shard_map/ppermute | solution.py:385
  12.8 11.1 %collective-permute-done.10.rest_0_ = bf16[384,384]{1,0:T(8,128)(2,1)S(1)} collective-permute-done((bf16[384,384]{1,0:T(8,128)(2,1)S(1)}, bf16[384,384]{1,0:T(8,128)(2,1)S(1)}, u32[]{:S(2)}, u32[]{:S(2)}) %collective-permute-start.10) | collective-permute-done | bytes 294944 | tf_op jit(solution)/shard_map/ppermute | solution.py:385
  24.6 1.3 %collective-permute-start.18 = (bf16[384,384]{1,0:T(8,128)(2,1)S(1)}, bf16[384,384]{1,0:T(8,128)(2,1)S(1)}, u32[]{:S(2)}, u32[]{:S(2)}) collective-permute-start(bf16[384,384]{1,0:T(8,128)(2,1)S(1)} %shard_map.92.f2.own), channel_id=1, source_target_pairs={{3,5},{12,13},{30,31}} | collective-permute-start | bytes 884744 | tf_op jit(solution)/shard_map/ppermute | solution.py:385
  25.9 0.9 %collective-permute-start.8 = (bf16[384,384]{1,0:T(8,128)(2,1)S(1)}, bf16[384,384]{1,0:T(8,128)(2,1)S(1)}, u32[]{:S(2)}, u32[]{:S(2)}) collective-permute-start(bf16[384,384]{1,0:T(8,128)(2,1)S(1)} %shard_map.95), channel_id=1, source_target_pairs={{5,4},{7,6}} | collective-permute-start | bytes 884744 | tf_op jit(solution)/shard_map/ppermute | solution.py:385
  26.9 0.8 %collective-permute-done.9.rest_3_ = bf16[384,384]{1,0:T(8,128)(2,1)S(1)} collective-permute-done((bf16[384,384]{1,0:T(8,128)(2,1)S(1)}, bf16[384,384]{1,0:T(8,128)(2,1)S(1)}, u32[]{:S(2)}, u32[]{:S(2)}) %collective-permute-start.9) | collective-permute-done | bytes 294944 | tf_op jit(solution)/shard_map/ppermute | solution.py:385
  28.3 0.7 %collective-permute-start.13 = (bf16[384,384]{1,0:T(8,128)(2,1)S(1)}, bf16[384,384]{1,0:T(8,128)(2,1)S(1)}, u32[]{:S(2)}, u32[]{:S(2)}) collective-permute-start(bf16[384,384]{1,0:T(8,128)(2,1)S(1)} %shard_map.97), channel_id=1, source_target_pairs={{4,5},{23,22},{7,6},{15,14}} | collective-permute-start | bytes 884744 | tf_op jit(solution)/shard_map/ppermute | solution.py:385
  29.0 1.3 %collective-permute-start.15 = (bf16[384,384]{1,0:T(8,128)(2,1)S(1)}, bf16[384,384]{1,0:T(8,128)(2,1)S(1)}, u32[]{:S(2)}, u32[]{:S(2)}) collective-permute-start(bf16[384,384]{1,0:T(8,128)(2,1)S(1)} %shard_map.92.f2.own), channel_id=1, source_target_pairs={{21,13},{30,22}} | collective-permute-start | bytes 884744 | tf_op jit(solution)/shard_map/ppermute | solution.py:385
  30.3 2.9 %collective-permute-done.18.rest_1_.rest_4_ = bf16[384,384]{1,0:T(8,128)(2,1)S(1)} collective-permute-done((bf16[384,384]{1,0:T(8,128)(2,1)S(1)}, bf16[384,384]{1,0:T(8,128)(2,1)S(1)}, u32[]{:S(2)}, u32[]{:S(2)}) %collective-permute-start.18) | collective-permute-done | bytes 294944 | tf_op jit(solution)/shard_map/ppermute | solution.py:385
  34.0 0.7 %collective-permute-start.19 = (bf16[384,384]{1,0:T(8,128)(2,1)S(1)}, bf16[384,384]{1,0:T(8,128)(2,1)S(1)}, u32[]{:S(2)}, u32[]{:S(2)}) collective-permute-start(bf16[384,384]{1,0:T(8,128)(2,1)S(1)} %shard_map.100), channel_id=1, source_target_pairs={{7,6},{15,14},{23,22},{5,4}} | collective-permute-start | bytes 884744 | tf_op jit(solution)/shard_map/ppermute | solution.py:385
  34.7 0.8 %shard_map.93 = bf16[384,384]{1,0:T(8,128)(2,1)} custom-call(bf16[384,384]{1,0:T(8,128)(2,1)S(1)} %shard_map.86.f0.own, bf16[384,384]{1,0:T(8,128)(2,1)S(1)} %shard_map.89.f1.own, bf16[384,384]{1,0:T(8,128)(2,1)S(1)} %shard_map.92.f2.own), custom_call_target="tpu_custom_call" | custom-call | tf_op jit(solution)/shard_map/pallas_call | solution.py:421
  35.9 0.8 %shard_map.98.s2 = f32[384,384]{1,0:T(8,128)S(1)} custom-call(f32[384,384]{1,0:T(8,128)S(1)} %shard_map.96.s1, bf16[384,384]{1,0:T(8,128)(2,1)S(1)} %get-tuple-element.25.coup_a.a1, bf16[384,384]{1,0:T(8,128)(2,1)S(1)} %get-tuple-element.24.coup_b.b1, bf16[384,384]{1,0:T(8,128)(2,1)S(1)} %collective-permute-done.10.rest_0_, ...), custom_call_target="tpu_custom_call" | custom-call | tf_op jit(solution)/shard_map/pallas_call | solution.py:421
  36.7 3.9 %collective-permute-done.15.rest_1_.rest_2_ = bf16[384,384]{1,0:T(8,128)(2,1)S(1)} collective-permute-done((bf16[384,384]{1,0:T(8,128)(2,1)S(1)}, bf16[384,384]{1,0:T(8,128)(2,1)S(1)}, u32[]{:S(2)}, u32[]{:S(2)}) %collective-permute-start.15) | collective-permute-done | bytes 294944 | tf_op jit(solution)/shard_map/ppermute | solution.py:385
  41.0 1.1 %shard_map.101 = f32[384,384]{1,0:T(8,128)} custom-call(f32[384,384]{1,0:T(8,128)S(1)} %shard_map.99.s3, bf16[384,384]{1,0:T(8,128)(2,1)S(1)} %get-tuple-element.27.b2, bf16[384,384]{1,0:T(8,128)(2,1)S(1)} %collective-permute-done.17.rest_0_, bf16[384,384]{1,0:T(8,128)(2,1)S(1)} %collective-permute-done.14.rest_0_.rest_1_, ...), custom_call_target="tpu_custom_call" | custom-call | tf_op jit(solution)/shard_map/pallas_call | solution.py:421
  (32 shorter events, 3.9 us)
Async XLA Ops:
  0.7 5.1 %collective-permute-start.1 = (bf16[384,384]{1,0:T(8,128)(2,1)S(1)}, bf16[384,384]{1,0:T(8,128)(2,1)S(1)}, u32[]{:S(2)}, u32[]{:S(2)}) collective-permute-start(bf16[384,384]{1,0:T(8,128)(2,1)S(1)} %shard_map.86.f0.own), channel_id=1, source_target_pairs={{1,2},{10,11},{19,20},{28,29}} | collective-permute-start | bytes 884744 | tf_op jit(solution)/shard_map/ppermute | solution.py:385
  1.4 4.5 %collective-permute-start = (bf16[384,384]{1,0:T(8,128)(2,1)S(1)}, bf16[384,384]{1,0:T(8,128)(2,1)S(1)}, u32[]{:S(2)}, u32[]{:S(2)}) collective-permute-start(bf16[384,384]{1,0:T(8,128)(2,1)S(1)} %shard_map.86.f0.own), channel_id=1, source_target_pairs={{10,2},{19,11},{28,20}} | collective-permute-start | bytes 884744 | tf_op jit(solution)/shard_map/ppermute | solution.py:385
  2.1 5.2 %collective-permute-start.6 = (bf16[384,384]{1,0:T(8,128)(2,1)S(1)}, bf16[384,384]{1,0:T(8,128)(2,1)S(1)}, u32[]{:S(2)}, u32[]{:S(2)}) collective-permute-start(bf16[384,384]{1,0:T(8,128)(2,1)S(1)} %shard_map.86.f0.own), channel_id=1, source_target_pairs={{1,5},{10,15},{19,23},{28,4}} | collective-permute-start | bytes 884744 | tf_op jit(solution)/shard_map/ppermute | solution.py:385
  2.8 5.9 %collective-permute-start.5 = (bf16[384,384]{1,0:T(8,128)(2,1)S(1)}, bf16[384,384]{1,0:T(8,128)(2,1)S(1)}, u32[]{:S(2)}, u32[]{:S(2)}) collective-permute-start(bf16[384,384]{1,0:T(8,128)(2,1)S(1)} %shard_map.86.f0.own), channel_id=1, source_target_pairs={{1,3},{10,12},{19,21},{28,30}} | collective-permute-start | bytes 884744 | tf_op jit(solution)/shard_map/ppermute | solution.py:385
  3.4 5.9 %collective-permute-start.4 = (bf16[384,384]{1,0:T(8,128)(2,1)S(1)}, bf16[384,384]{1,0:T(8,128)(2,1)S(1)}, u32[]{:S(2)}, u32[]{:S(2)}) collective-permute-start(bf16[384,384]{1,0:T(8,128)(2,1)S(1)} %shard_map.86.f0.own), channel_id=1, source_target_pairs={{19,3},{28,12}} | collective-permute-start | bytes 884744 | tf_op jit(solution)/shard_map/ppermute | solution.py:385
  5.9 4.2 %collective-permute-start.3 = (bf16[384,384]{1,0:T(8,128)(2,1)S(1)}, bf16[384,384]{1,0:T(8,128)(2,1)S(1)}, u32[]{:S(2)}, u32[]{:S(2)}) collective-permute-start(bf16[384,384]{1,0:T(8,128)(2,1)S(1)} %shard_map.89.f1.own), channel_id=1, source_target_pairs={{2,3},{11,12},{20,21},{29,30}} | collective-permute-start | bytes 884744 | tf_op jit(solution)/shard_map/ppermute | solution.py:385
  6.6 4.8 %collective-permute-start.2 = (bf16[384,384]{1,0:T(8,128)(2,1)S(1)}, bf16[384,384]{1,0:T(8,128)(2,1)S(1)}, u32[]{:S(2)}, u32[]{:S(2)}) collective-permute-start(bf16[384,384]{1,0:T(8,128)(2,1)S(1)} %shard_map.89.f1.own), channel_id=1, source_target_pairs={{11,3},{20,12},{29,21}} | collective-permute-start | bytes 884744 | tf_op jit(solution)/shard_map/ppermute | solution.py:385
  7.3 16.6 %collective-permute-start.10 = (bf16[384,384]{1,0:T(8,128)(2,1)S(1)}, bf16[384,384]{1,0:T(8,128)(2,1)S(1)}, u32[]{:S(2)}, u32[]{:S(2)}) collective-permute-start(bf16[384,384]{1,0:T(8,128)(2,1)S(1)} %shard_map.89.f1.own), channel_id=1, source_target_pairs={{2,4},{11,13},{20,23},{29,31}} | collective-permute-start | bytes 884744 | tf_op jit(solution)/shard_map/ppermute | solution.py:385
  8.7 15.9 %collective-permute-start.7 = (bf16[384,384]{1,0:T(8,128)(2,1)S(1)}, bf16[384,384]{1,0:T(8,128)(2,1)S(1)}, u32[]{:S(2)}, u32[]{:S(2)}) collective-permute-start(bf16[384,384]{1,0:T(8,128)(2,1)S(1)} %shard_map.94), channel_id=1, source_target_pairs={{5,7},{15,14},{23,22}} | collective-permute-start | bytes 884744 | tf_op jit(solution)/shard_map/ppermute | solution.py:385
  9.4 16.6 %collective-permute-start.11 = (bf16[384,384]{1,0:T(8,128)(2,1)S(1)}, bf16[384,384]{1,0:T(8,128)(2,1)S(1)}, u32[]{:S(2)}, u32[]{:S(2)}) collective-permute-start(bf16[384,384]{1,0:T(8,128)(2,1)S(1)} %shard_map.89.f1.own), channel_id=1, source_target_pairs={{2,7},{11,15},{20,4},{29,5}} | collective-permute-start | bytes 884744 | tf_op jit(solution)/shard_map/ppermute | solution.py:385
  10.1 18.2 %collective-permute-start.12 = (bf16[384,384]{1,0:T(8,128)(2,1)S(1)}, bf16[384,384]{1,0:T(8,128)(2,1)S(1)}, u32[]{:S(2)}, u32[]{:S(2)}) collective-permute-start(bf16[384,384]{1,0:T(8,128)(2,1)S(1)} %shard_map.89.f1.own), channel_id=1, source_target_pairs={{29,13}} | collective-permute-start | bytes 884744 | tf_op jit(solution)/shard_map/ppermute | solution.py:385
  11.4 16.2 %collective-permute-start.9 = (bf16[384,384]{1,0:T(8,128)(2,1)S(1)}, bf16[384,384]{1,0:T(8,128)(2,1)S(1)}, u32[]{:S(2)}, u32[]{:S(2)}) collective-permute-start(bf16[384,384]{1,0:T(8,128)(2,1)S(1)} %collective-permute-done.5.left), channel_id=1, source_target_pairs={{12,13},{30,31}} | collective-permute-start | bytes 884744 | tf_op jit(solution)/shard_map/ppermute | solution.py:385
  23.9 5.1 %collective-permute-start.17 = (bf16[384,384]{1,0:T(8,128)(2,1)S(1)}, bf16[384,384]{1,0:T(8,128)(2,1)S(1)}, u32[]{:S(2)}, u32[]{:S(2)}) collective-permute-start(bf16[384,384]{1,0:T(8,128)(2,1)S(1)} %shard_map.92.f2.own), channel_id=1, source_target_pairs={{3,7},{12,15},{21,23}} | collective-permute-start | bytes 884744 | tf_op jit(solution)/shard_map/ppermute | solution.py:385
  24.6 8.7 %collective-permute-start.18 = (bf16[384,384]{1,0:T(8,128)(2,1)S(1)}, bf16[384,384]{1,0:T(8,128)(2,1)S(1)}, u32[]{:S(2)}, u32[]{:S(2)}) collective-permute-start(bf16[384,384]{1,0:T(8,128)(2,1)S(1)} %shard_map.92.f2.own), channel_id=1, source_target_pairs={{3,5},{12,13},{30,31}} | collective-permute-start | bytes 884744 | tf_op jit(solution)/shard_map/ppermute | solution.py:385
  25.9 8.0 %collective-permute-start.8 = (bf16[384,384]{1,0:T(8,128)(2,1)S(1)}, bf16[384,384]{1,0:T(8,128)(2,1)S(1)}, u32[]{:S(2)}, u32[]{:S(2)}) collective-permute-start(bf16[384,384]{1,0:T(8,128)(2,1)S(1)} %shard_map.95), channel_id=1, source_target_pairs={{5,4},{7,6}} | collective-permute-start | bytes 884744 | tf_op jit(solution)/shard_map/ppermute | solution.py:385
  27.6 9.1 %collective-permute-start.14 = (bf16[384,384]{1,0:T(8,128)(2,1)S(1)}, bf16[384,384]{1,0:T(8,128)(2,1)S(1)}, u32[]{:S(2)}, u32[]{:S(2)}) collective-permute-start(bf16[384,384]{1,0:T(8,128)(2,1)S(1)} %shard_map.92.f2.own), channel_id=1, source_target_pairs={{12,4},{21,5},{30,6}} | collective-permute-start | bytes 884744 | tf_op jit(solution)/shard_map/ppermute | solution.py:385
  28.3 7.6 %collective-permute-start.13 = (bf16[384,384]{1,0:T(8,128)(2,1)S(1)}, bf16[384,384]{1,0:T(8,128)(2,1)S(1)}, u32[]{:S(2)}, u32[]{:S(2)}) collective-permute-start(bf16[384,384]{1,0:T(8,128)(2,1)S(1)} %shard_map.97), channel_id=1, source_target_pairs={{4,5},{23,22},{7,6},{15,14}} | collective-permute-start | bytes 884744 | tf_op jit(solution)/shard_map/ppermute | solution.py:385
  29.0 11.5 %collective-permute-start.15 = (bf16[384,384]{1,0:T(8,128)(2,1)S(1)}, bf16[384,384]{1,0:T(8,128)(2,1)S(1)}, u32[]{:S(2)}, u32[]{:S(2)}) collective-permute-start(bf16[384,384]{1,0:T(8,128)(2,1)S(1)} %shard_map.92.f2.own), channel_id=1, source_target_pairs={{21,13},{30,22}} | collective-permute-start | bytes 884744 | tf_op jit(solution)/shard_map/ppermute | solution.py:385
  33.2 7.3 %collective-permute-start.16 = (bf16[384,384]{1,0:T(8,128)(2,1)S(1)}, bf16[384,384]{1,0:T(8,128)(2,1)S(1)}, u32[]{:S(2)}, u32[]{:S(2)}) collective-permute-start(bf16[384,384]{1,0:T(8,128)(2,1)S(1)} %shard_map.92.f2.own), channel_id=1, source_target_pairs={{30,14}} | collective-permute-start | bytes 884744 | tf_op jit(solution)/shard_map/ppermute | solution.py:385
  34.0 7.0 %collective-permute-start.19 = (bf16[384,384]{1,0:T(8,128)(2,1)S(1)}, bf16[384,384]{1,0:T(8,128)(2,1)S(1)}, u32[]{:S(2)}, u32[]{:S(2)}) collective-permute-start(bf16[384,384]{1,0:T(8,128)(2,1)S(1)} %shard_map.100), channel_id=1, source_target_pairs={{7,6},{15,14},{23,22},{5,4}} | collective-permute-start | bytes 884744 | tf_op jit(solution)/shard_map/ppermute | solution.py:385

commit v9 on v6

--- a/solution.py
+++ b/solution.py
@@ -13,16 +13,17 @@
 FAR_SPEC = pl.BlockSpec(memory_space=pltpu.HBM)
 
 
-def plan(rows_n, cols_n, offset, gap, up_gap, apart=False):
+def plan(rows_n, cols_n, offset, gap, up_gap, apart=False, served=None):
     rights, ups, last = [], [], []
     for i in range(rows_n):
         m = i + offset
         if 0 <= m < cols_n:
-            targets = range(m + gap, cols_n)
+            targets = [j for j in range(m + gap, cols_n) if served is None or j // 2 != (m + served) // 2]
             for chip in sorted({j // 2 for j in targets}, reverse=True):
                 some = [(i, j) for j in targets if j // 2 == chip]
                 (last if chip == m // 2 else rights).append(((i, m), some, "left"))
-            ups += [((i, m), [(k, m)], "down") for k in range(i - up_gap + 1)]
+            above = list(range(i - up_gap + 1))
+            ups += [((i, m), [(k, m)], "down") for k in above[:1] + above[1:][-1:] + above[1:-1]]
     todo = rights + ups + last
     ops, forwards = [], []
     while todo:
@@ -30,12 +31,12 @@
         allowed = {"left", "down"}
         if apart:
             turn = {kind for _, _, kind in todo}
-            allowed = turn if len(turn) == 1 else {"left" if len(ops) % 2 == 0 else "down"}
+            allowed = turn if len(turn) == 1 else {"down" if 0 < len(ops) < 4 else "left"}
         busy = [source for source, _, _ in todo]
         waiting = {targets[0]: busy.count(source) for source, targets, kind in todo if kind == "down"}
         for item in list(todo):
             source, targets, kind = item
-            if kind not in allowed:
+            if kind not in allowed or (apart and not ops and item in last and rights):
                 continue
             for target in sorted(targets, key=lambda t: (waiting.get(t, 0), -t[1])):
                 if source not in used_from and target not in used_to:
@@ -352,12 +353,16 @@
     rows_n, cols_n = mesh.shape["row"], mesh.shape["col"]
     first = (rows_n + cols_n) // 2 - 2
     offset = first - rows_n + 1
-    ops0 = plan(rows_n, cols_n, offset, 3, 3)
+    ops0 = plan(rows_n, cols_n, offset, 3, 3, served=2)
     ops1 = plan(rows_n, cols_n, offset + 1, 2, 2)
     ops2 = plan(rows_n, cols_n, offset + 2, 1, 1, True)
 
     def owners(t):
         return [(i, i + offset + t) for i in range(rows_n) if 0 <= i + offset + t < cols_n]
+
+    beside = [
+        ((i, j + 2), (i, j + 3), "left", None) for i, j in owners(0) if (j + 2) % 2 == 0 and j + 3 < cols_n
+    ]
 
     def up(t, far):
         return [(i * cols_n + j, (i - far) * cols_n + j) for i, j in owners(t) if i >= far]
@@ -420,6 +425,7 @@
         down_far = move(f0, up(0, 2))
         left_far = move(f0, right(0, 2))
         far0 = spread(ops0, cols_n, f0, "a", call)
+        far0.append(move(left_far, [(a[0] * cols_n + a[1], b[0] * cols_n + b[1]) for a, b, _, _ in beside]))
         *basis, coup, s, a0, b0, a1, b1, a2, b2 = call(
             functools.partial(prepare, rows_n, first),
             [rhs, a_c, b_c, u, v, a_vals, b_vals],
@@ -441,7 +447,7 @@
         )
         far1 = spread(ops1, cols_n, f1, "b", call)
         (f2,) = advance(1, down, left, s1, a1, b1)
-        for k, (ops, far, a, b) in enumerate(((ops0, far0, a0, b0), (ops1, far1, a1, b1))):
+        for k, (ops, far, a, b) in enumerate(((ops0 + [beside], far0, a0, b0), (ops1, far1, a1, b1))):
             (s,) = call(
                 functools.partial(middle, rows_n, cols_n, first, ops),
                 [],

time: 42.4 us -> 45.4 us (1.071)
  starting transfers between devices: 20.6 us -> 23.8 us
    ppermute x19 -> x20, starting transfers between devices: 20.6 us -> 23.8 us  [move(): return lax.ppermute(value, AXES, pairs)]
    ppermute x19 -> x20, waiting for transfers between devices: 14.7 us -> 14.5 us  [move(): return lax.ppermute(value, AXES, pairs)]
  transfers between devices with their start and end apart: 19 -> 20, of which waited for: 2 -> 3; matrix products, arithmetic and copies ran while one was open for 0% -> 0% of each run, Pallas kernels for 10% -> 10%
where the time goes in v9:
time: 45.4 us; the launch traced here: 45 us
  starting transfers between devices  23.8 us (52%)
  waiting for transfers between devices  14.5 us (32%)
  Pallas kernels  5.56 us (12%)
  between operations  1.19 us (3%)
    ppermute x20, starting transfers between devices, move(): return lax.ppermute(value, AXES, pairs)  23.8 us
    ppermute x20, waiting for transfers between devices, move(): return lax.ppermute(value, AXES, pairs)  14.5 us
    pallas_call x15, Pallas kernels, call(): pl.pallas_call(kernel, out_shape=outs, in_specs=[FAR_SPEC] * len(far) + [...  5.56 us
  transfers between devices with their start and end apart: 20, of which 3 were waited for; matrix products, arithmetic and copies ran while one was open for 0% of the time, Pallas kernels for 10%

profile of v9, /device:TPU:17, one launch (start us, length us, event | category | flops | bytes accessed | tf_op | source)
XLA Modules:
  0.0 45.0 jit_solution(17871457861553367893)
XLA Ops:
  0.7 0.7 %collective-permute-start.1 = (bf16[384,384]{1,0:T(8,128)(2,1)S(1)}, bf16[384,384]{1,0:T(8,128)(2,1)S(1)}, u32[]{:S(2)}, u32[]{:S(2)}) collective-permute-start(bf16[384,384]{1,0:T(8,128)(2,1)S(1)} %shard_map.86.f0.own), channel_id=1, source_target_pairs={{1,2},{10,11},{19,20},{28,29}} | collective-permute-start | bytes 884744 | tf_op jit(solution)/shard_map/ppermute | solution.py:349
  1.4 0.7 %collective-permute-start = (bf16[384,384]{1,0:T(8,128)(2,1)S(1)}, bf16[384,384]{1,0:T(8,128)(2,1)S(1)}, u32[]{:S(2)}, u32[]{:S(2)}) collective-permute-start(bf16[384,384]{1,0:T(8,128)(2,1)S(1)} %shard_map.86.f0.own), channel_id=1, source_target_pairs={{10,2},{19,11},{28,20}} | collective-permute-start | bytes 884744 | tf_op jit(solution)/shard_map/ppermute | solution.py:349
  2.1 0.7 %collective-permute-start.5 = (bf16[384,384]{1,0:T(8,128)(2,1)S(1)}, bf16[384,384]{1,0:T(8,128)(2,1)S(1)}, u32[]{:S(2)}, u32[]{:S(2)}) collective-permute-start(bf16[384,384]{1,0:T(8,128)(2,1)S(1)} %shard_map.86.f0.own), channel_id=1, source_target_pairs={{1,3},{10,12},{19,21},{28,30}} | collective-permute-start | bytes 884744 | tf_op jit(solution)/shard_map/ppermute | solution.py:349
  2.8 0.7 %collective-permute-start.6 = (bf16[384,384]{1,0:T(8,128)(2,1)S(1)}, bf16[384,384]{1,0:T(8,128)(2,1)S(1)}, u32[]{:S(2)}, u32[]{:S(2)}) collective-permute-start(bf16[384,384]{1,0:T(8,128)(2,1)S(1)} %shard_map.86.f0.own), channel_id=1, source_target_pairs={{1,7},{10,15},{19,23},{28,4}} | collective-permute-start | bytes 884744 | tf_op jit(solution)/shard_map/ppermute | solution.py:349
  3.4 1.3 %collective-permute-start.7 = (bf16[384,384]{1,0:T(8,128)(2,1)S(1)}, bf16[384,384]{1,0:T(8,128)(2,1)S(1)}, u32[]{:S(2)}, u32[]{:S(2)}) collective-permute-start(bf16[384,384]{1,0:T(8,128)(2,1)S(1)} %shard_map.86.f0.own), channel_id=1, source_target_pairs={{1,5}} | collective-permute-start | bytes 884744 | tf_op jit(solution)/shard_map/ppermute | solution.py:349
  4.7 1.7 %shard_map.87 = (bf16[384,1152]{1,0:T(8,128)(2,1)S(1)}, bf16[384,1152]{1,0:T(8,128)(2,1)S(1)}, bf16[1152,384]{1,0:T(8,128)(2,1)S(1)}, bf16[384,1152]{1,0:T(8,128...) custom-call(f32[384,384]{1,0:T(8,128)} %rhs.3, ...), custom_call_target="tpu_custom_call" | custom-call | tf_op jit(solution)/shard_map/pallas_call | solution.py:385
  7.2 0.7 %collective-permute-start.3 = (bf16[384,384]{1,0:T(8,128)(2,1)S(1)}, bf16[384,384]{1,0:T(8,128)(2,1)S(1)}, u32[]{:S(2)}, u32[]{:S(2)}) collective-permute-start(bf16[384,384]{1,0:T(8,128)(2,1)S(1)} %shard_map.89.f1.own), channel_id=1, source_target_pairs={{2,3},{11,12},{20,21},{29,30}} | collective-permute-start | bytes 884744 | tf_op jit(solution)/shard_map/ppermute | solution.py:349
  7.9 0.7 %collective-permute-start.2 = (bf16[384,384]{1,0:T(8,128)(2,1)S(1)}, bf16[384,384]{1,0:T(8,128)(2,1)S(1)}, u32[]{:S(2)}, u32[]{:S(2)}) collective-permute-start(bf16[384,384]{1,0:T(8,128)(2,1)S(1)} %shard_map.89.f1.own), channel_id=1, source_target_pairs={{11,3},{20,12},{29,21}} | collective-permute-start | bytes 884744 | tf_op jit(solution)/shard_map/ppermute | solution.py:349
  9.3 9.4 %collective-permute-done.7.rest_1_ = bf16[384,384]{1,0:T(8,128)(2,1)S(1)} collective-permute-done((bf16[384,384]{1,0:T(8,128)(2,1)S(1)}, bf16[384,384]{1,0:T(8,128)(2,1)S(1)}, u32[]{:S(2)}, u32[]{:S(2)}) %collective-permute-start.7) | collective-permute-done | bytes 294944 | tf_op jit(solution)/shard_map/ppermute | solution.py:349
  18.7 1.3 %collective-permute-start.11 = (bf16[384,384]{1,0:T(8,128)(2,1)S(1)}, bf16[384,384]{1,0:T(8,128)(2,1)S(1)}, u32[]{:S(2)}, u32[]{:S(2)}) collective-permute-start(bf16[384,384]{1,0:T(8,128)(2,1)S(1)} %shard_map.89.f1.own), channel_id=1, source_target_pairs={{2,4},{11,13},{29,5}} | collective-permute-start | bytes 884744 | tf_op jit(solution)/shard_map/ppermute | solution.py:349
  20.1 2.1 %collective-permute-start.8 = (bf16[384,384]{1,0:T(8,128)(2,1)S(1)}, bf16[384,384]{1,0:T(8,128)(2,1)S(1)}, u32[]{:S(2)}, u32[]{:S(2)}) collective-permute-start(bf16[384,384]{1,0:T(8,128)(2,1)S(1)} %shard_map.94), channel_id=1, source_target_pairs={{7,6},{15,14},{23,22},{5,4}} | collective-permute-start | bytes 884744 | tf_op jit(solution)/shard_map/ppermute | solution.py:349
  22.2 0.7 %collective-permute-start.9 = (bf16[384,384]{1,0:T(8,128)(2,1)S(1)}, bf16[384,384]{1,0:T(8,128)(2,1)S(1)}, u32[]{:S(2)}, u32[]{:S(2)}) collective-permute-start(bf16[384,384]{1,0:T(8,128)(2,1)S(1)} %collective-permute-done.5.left), channel_id=1, source_target_pairs={{12,13},{30,31}} | collective-permute-start | bytes 884744 | tf_op jit(solution)/shard_map/ppermute | solution.py:349
  23.0 0.7 %collective-permute-start.17 = (bf16[384,384]{1,0:T(8,128)(2,1)S(1)}, bf16[384,384]{1,0:T(8,128)(2,1)S(1)}, u32[]{:S(2)}, u32[]{:S(2)}) collective-permute-start(bf16[384,384]{1,0:T(8,128)(2,1)S(1)} %shard_map.92.f2.own), channel_id=1, source_target_pairs={{3,7},{12,15},{21,23}} | collective-permute-start | bytes 884744 | tf_op jit(solution)/shard_map/ppermute | solution.py:349
  23.7 1.3 %collective-permute-start.18 = (bf16[384,384]{1,0:T(8,128)(2,1)S(1)}, bf16[384,384]{1,0:T(8,128)(2,1)S(1)}, u32[]{:S(2)}, u32[]{:S(2)}) collective-permute-start(bf16[384,384]{1,0:T(8,128)(2,1)S(1)} %shard_map.92.f2.own), channel_id=1, source_target_pairs={{3,5},{12,13},{30,31}} | collective-permute-start | bytes 884744 | tf_op jit(solution)/shard_map/ppermute | solution.py:349
  25.0 2.1 %collective-permute-done.11.rest_1_ = bf16[384,384]{1,0:T(8,128)(2,1)S(1)} collective-permute-done((bf16[384,384]{1,0:T(8,128)(2,1)S(1)}, bf16[384,384]{1,0:T(8,128)(2,1)S(1)}, u32[]{:S(2)}, u32[]{:S(2)}) %collective-permute-start.11) | collective-permute-done | bytes 294944 | tf_op jit(solution)/shard_map/ppermute | solution.py:349
  27.1 0.8 %collective-permute-start.12 = (bf16[384,384]{1,0:T(8,128)(2,1)S(1)}, bf16[384,384]{1,0:T(8,128)(2,1)S(1)}, u32[]{:S(2)}, u32[]{:S(2)}) collective-permute-start(bf16[384,384]{1,0:T(8,128)(2,1)S(1)} %shard_map.89.f1.own), channel_id=1, source_target_pairs={{20,4},{29,13}} | collective-permute-start | bytes 884744 | tf_op jit(solution)/shard_map/ppermute | solution.py:349
  28.0 1.3 %collective-permute-start.14 = (bf16[384,384]{1,0:T(8,128)(2,1)S(1)}, bf16[384,384]{1,0:T(8,128)(2,1)S(1)}, u32[]{:S(2)}, u32[]{:S(2)}) collective-permute-start(bf16[384,384]{1,0:T(8,128)(2,1)S(1)} %shard_map.92.f2.own), channel_id=1, source_target_pairs={{12,4},{21,5},{30,6}} | collective-permute-start | bytes 884744 | tf_op jit(solution)/shard_map/ppermute | solution.py:349
  29.3 1.3 %collective-permute-start.13 = (bf16[384,384]{1,0:T(8,128)(2,1)S(1)}, bf16[384,384]{1,0:T(8,128)(2,1)S(1)}, u32[]{:S(2)}, u32[]{:S(2)}) collective-permute-start(bf16[384,384]{1,0:T(8,128)(2,1)S(1)} %shard_map.96), channel_id=1, source_target_pairs={{7,6},{15,14},{23,22},{4,5}} | collective-permute-start | bytes 884744 | tf_op jit(solution)/shard_map/ppermute | solution.py:349
  30.6 0.7 %collective-permute-start.15 = (bf16[384,384]{1,0:T(8,128)(2,1)S(1)}, bf16[384,384]{1,0:T(8,128)(2,1)S(1)}, u32[]{:S(2)}, u32[]{:S(2)}) collective-permute-start(bf16[384,384]{1,0:T(8,128)(2,1)S(1)} %shard_map.92.f2.own), channel_id=1, source_target_pairs={{21,13},{30,22}} | collective-permute-start | bytes 884744 | tf_op jit(solution)/shard_map/ppermute | solution.py:349
  31.3 3.0 %collective-permute-done.18.rest_1_.rest_4_ = bf16[384,384]{1,0:T(8,128)(2,1)S(1)} collective-permute-done((bf16[384,384]{1,0:T(8,128)(2,1)S(1)}, bf16[384,384]{1,0:T(8,128)(2,1)S(1)}, u32[]{:S(2)}, u32[]{:S(2)}) %collective-permute-start.18) | collective-permute-done | bytes 294944 | tf_op jit(solution)/shard_map/ppermute | solution.py:349
  35.0 6.2 %collective-permute-start.19 = (bf16[384,384]{1,0:T(8,128)(2,1)S(1)}, bf16[384,384]{1,0:T(8,128)(2,1)S(1)}, u32[]{:S(2)}, u32[]{:S(2)}) collective-permute-start(bf16[384,384]{1,0:T(8,128)(2,1)S(1)} %shard_map.99), channel_id=1, source_target_pairs={{7,6},{15,14},{23,22},{5,4}} | collective-permute-start | bytes 884744 | tf_op jit(solution)/shard_map/ppermute | solution.py:349
  41.3 0.8 %shard_map.93 = bf16[384,384]{1,0:T(8,128)(2,1)} custom-call(bf16[384,384]{1,0:T(8,128)(2,1)S(1)} %shard_map.86.f0.own, bf16[384,384]{1,0:T(8,128)(2,1)S(1)} %shard_map.89.f1.own, bf16[384,384]{1,0:T(8,128)(2,1)S(1)} %shard_map.92.f2.own), custom_call_target="tpu_custom_call" | custom-call | tf_op jit(solution)/shard_map/pallas_call | solution.py:385
  42.5 0.8 %shard_map.97.s2 = f32[384,384]{1,0:T(8,128)S(1)} custom-call(f32[384,384]{1,0:T(8,128)S(1)} %shard_map.95.s1, bf16[384,384]{1,0:T(8,128)(2,1)S(1)} %get-tuple-element.25.coup_a.a1, bf16[384,384]{1,0:T(8,128)(2,1)S(1)} %get-tuple-element.24.coup_b.b1, bf16[384,384]{1,0:T(8,128)(2,1)S(1)} %collective-permute-done.10.rest_0_, ...), custom_call_target="tpu_custom_call" | custom-call | tf_op jit(solution)/shard_map/pallas_call | solution.py:385
  43.8 1.1 %shard_map.100 = f32[384,384]{1,0:T(8,128)} custom-call(f32[384,384]{1,0:T(8,128)S(1)} %shard_map.98.s3, bf16[384,384]{1,0:T(8,128)(2,1)S(1)} %get-tuple-element.27.b2, bf16[384,384]{1,0:T(8,128)(2,1)S(1)} %collective-permute-done.17.rest_0_, bf16[384,384]{1,0:T(8,128)(2,1)S(1)} %collective-permute-done.14.rest_0_.rest_1_, ...), custom_call_target="tpu_custom_call" | custom-call | tf_op jit(solution)/shard_map/pallas_call | solution.py:385
  (31 shorter events, 3.3 us)
Async XLA Ops:
  0.7 5.7 %collective-permute-start.1 = (bf16[384,384]{1,0:T(8,128)(2,1)S(1)}, bf16[384,384]{1,0:T(8,128)(2,1)S(1)}, u32[]{:S(2)}, u32[]{:S(2)}) collective-permute-start(bf16[384,384]{1,0:T(8,128)(2,1)S(1)} %shard_map.86.f0.own), channel_id=1, source_target_pairs={{1,2},{10,11},{19,20},{28,29}} | collective-permute-start | bytes 884744 | tf_op jit(solution)/shard_map/ppermute | solution.py:349
  1.4 5.8 %collective-permute-start = (bf16[384,384]{1,0:T(8,128)(2,1)S(1)}, bf16[384,384]{1,0:T(8,128)(2,1)S(1)}, u32[]{:S(2)}, u32[]{:S(2)}) collective-permute-start(bf16[384,384]{1,0:T(8,128)(2,1)S(1)} %shard_map.86.f0.own), channel_id=1, source_target_pairs={{10,2},{19,11},{28,20}} | collective-permute-start | bytes 884744 | tf_op jit(solution)/shard_map/ppermute | solution.py:349
  2.1 5.8 %collective-permute-start.5 = (bf16[384,384]{1,0:T(8,128)(2,1)S(1)}, bf16[384,384]{1,0:T(8,128)(2,1)S(1)}, u32[]{:S(2)}, u32[]{:S(2)}) collective-permute-start(bf16[384,384]{1,0:T(8,128)(2,1)S(1)} %shard_map.86.f0.own), channel_id=1, source_target_pairs={{1,3},{10,12},{19,21},{28,30}} | collective-permute-start | bytes 884744 | tf_op jit(solution)/shard_map/ppermute | solution.py:349
  2.8 5.8 %collective-permute-start.6 = (bf16[384,384]{1,0:T(8,128)(2,1)S(1)}, bf16[384,384]{1,0:T(8,128)(2,1)S(1)}, u32[]{:S(2)}, u32[]{:S(2)}) collective-permute-start(bf16[384,384]{1,0:T(8,128)(2,1)S(1)} %shard_map.86.f0.own), channel_id=1, source_target_pairs={{1,7},{10,15},{19,23},{28,4}} | collective-permute-start | bytes 884744 | tf_op jit(solution)/shard_map/ppermute | solution.py:349
  3.4 15.3 %collective-permute-start.7 = (bf16[384,384]{1,0:T(8,128)(2,1)S(1)}, bf16[384,384]{1,0:T(8,128)(2,1)S(1)}, u32[]{:S(2)}, u32[]{:S(2)}) collective-permute-start(bf16[384,384]{1,0:T(8,128)(2,1)S(1)} %shard_map.86.f0.own), channel_id=1, source_target_pairs={{1,5}} | collective-permute-start | bytes 884744 | tf_op jit(solution)/shard_map/ppermute | solution.py:349
  6.5 13.6 %collective-permute-start.4 = (bf16[384,384]{1,0:T(8,128)(2,1)S(1)}, bf16[384,384]{1,0:T(8,128)(2,1)S(1)}, u32[]{:S(2)}, u32[]{:S(2)}) collective-permute-start(bf16[384,384]{1,0:T(8,128)(2,1)S(1)} %shard_map.86.f0.own), channel_id=1, source_target_pairs={{19,3},{28,12}} | collective-permute-start | bytes 884744 | tf_op jit(solution)/shard_map/ppermute | solution.py:349
  7.2 15.0 %collective-permute-start.3 = (bf16[384,384]{1,0:T(8,128)(2,1)S(1)}, bf16[384,384]{1,0:T(8,128)(2,1)S(1)}, u32[]{:S(2)}, u32[]{:S(2)}) collective-permute-start(bf16[384,384]{1,0:T(8,128)(2,1)S(1)} %shard_map.89.f1.own), channel_id=1, source_target_pairs={{2,3},{11,12},{20,21},{29,30}} | collective-permute-start | bytes 884744 | tf_op jit(solution)/shard_map/ppermute | solution.py:349
  7.9 15.1 %collective-permute-start.2 = (bf16[384,384]{1,0:T(8,128)(2,1)S(1)}, bf16[384,384]{1,0:T(8,128)(2,1)S(1)}, u32[]{:S(2)}, u32[]{:S(2)}) collective-permute-start(bf16[384,384]{1,0:T(8,128)(2,1)S(1)} %shard_map.89.f1.own), channel_id=1, source_target_pairs={{11,3},{20,12},{29,21}} | collective-permute-start | bytes 884744 | tf_op jit(solution)/shard_map/ppermute | solution.py:349
  8.6 15.1 %collective-permute-start.10 = (bf16[384,384]{1,0:T(8,128)(2,1)S(1)}, bf16[384,384]{1,0:T(8,128)(2,1)S(1)}, u32[]{:S(2)}, u32[]{:S(2)}) collective-permute-start(bf16[384,384]{1,0:T(8,128)(2,1)S(1)} %shard_map.89.f1.own), channel_id=1, source_target_pairs={{2,7},{11,15},{20,23},{29,31}} | collective-permute-start | bytes 884744 | tf_op jit(solution)/shard_map/ppermute | solution.py:349
  18.7 8.4 %collective-permute-start.11 = (bf16[384,384]{1,0:T(8,128)(2,1)S(1)}, bf16[384,384]{1,0:T(8,128)(2,1)S(1)}, u32[]{:S(2)}, u32[]{:S(2)}) collective-permute-start(bf16[384,384]{1,0:T(8,128)(2,1)S(1)} %shard_map.89.f1.own), channel_id=1, source_target_pairs={{2,4},{11,13},{29,5}} | collective-permute-start | bytes 884744 | tf_op jit(solution)/shard_map/ppermute | solution.py:349
  20.1 7.9 %collective-permute-start.8 = (bf16[384,384]{1,0:T(8,128)(2,1)S(1)}, bf16[384,384]{1,0:T(8,128)(2,1)S(1)}, u32[]{:S(2)}, u32[]{:S(2)}) collective-permute-start(bf16[384,384]{1,0:T(8,128)(2,1)S(1)} %shard_map.94), channel_id=1, source_target_pairs={{7,6},{15,14},{23,22},{5,4}} | collective-permute-start | bytes 884744 | tf_op jit(solution)/shard_map/ppermute | solution.py:349
  22.2 7.1 %collective-permute-start.9 = (bf16[384,384]{1,0:T(8,128)(2,1)S(1)}, bf16[384,384]{1,0:T(8,128)(2,1)S(1)}, u32[]{:S(2)}, u32[]{:S(2)}) collective-permute-start(bf16[384,384]{1,0:T(8,128)(2,1)S(1)} %collective-permute-done.5.left), channel_id=1, source_target_pairs={{12,13},{30,31}} | collective-permute-start | bytes 884744 | tf_op jit(solution)/shard_map/ppermute | solution.py:349
  23.0 7.6 %collective-permute-start.17 = (bf16[384,384]{1,0:T(8,128)(2,1)S(1)}, bf16[384,384]{1,0:T(8,128)(2,1)S(1)}, u32[]{:S(2)}, u32[]{:S(2)}) collective-permute-start(bf16[384,384]{1,0:T(8,128)(2,1)S(1)} %shard_map.92.f2.own), channel_id=1, source_target_pairs={{3,7},{12,15},{21,23}} | collective-permute-start | bytes 884744 | tf_op jit(solution)/shard_map/ppermute | solution.py:349
  23.7 10.6 %collective-permute-start.18 = (bf16[384,384]{1,0:T(8,128)(2,1)S(1)}, bf16[384,384]{1,0:T(8,128)(2,1)S(1)}, u32[]{:S(2)}, u32[]{:S(2)}) collective-permute-start(bf16[384,384]{1,0:T(8,128)(2,1)S(1)} %shard_map.92.f2.own), channel_id=1, source_target_pairs={{3,5},{12,13},{30,31}} | collective-permute-start | bytes 884744 | tf_op jit(solution)/shard_map/ppermute | solution.py:349
  27.1 7.9 %collective-permute-start.12 = (bf16[384,384]{1,0:T(8,128)(2,1)S(1)}, bf16[384,384]{1,0:T(8,128)(2,1)S(1)}, u32[]{:S(2)}, u32[]{:S(2)}) collective-permute-start(bf16[384,384]{1,0:T(8,128)(2,1)S(1)} %shard_map.89.f1.own), channel_id=1, source_target_pairs={{20,4},{29,13}} | collective-permute-start | bytes 884744 | tf_op jit(solution)/shard_map/ppermute | solution.py:349
  28.0 15.3 %collective-permute-start.14 = (bf16[384,384]{1,0:T(8,128)(2,1)S(1)}, bf16[384,384]{1,0:T(8,128)(2,1)S(1)}, u32[]{:S(2)}, u32[]{:S(2)}) collective-permute-start(bf16[384,384]{1,0:T(8,128)(2,1)S(1)} %shard_map.92.f2.own), channel_id=1, source_target_pairs={{12,4},{21,5},{30,6}} | collective-permute-start | bytes 884744 | tf_op jit(solution)/shard_map/ppermute | solution.py:349
  29.3 13.1 %collective-permute-start.13 = (bf16[384,384]{1,0:T(8,128)(2,1)S(1)}, bf16[384,384]{1,0:T(8,128)(2,1)S(1)}, u32[]{:S(2)}, u32[]{:S(2)}) collective-permute-start(bf16[384,384]{1,0:T(8,128)(2,1)S(1)} %shard_map.96), channel_id=1, source_target_pairs={{7,6},{15,14},{23,22},{4,5}} | collective-permute-start | bytes 884744 | tf_op jit(solution)/shard_map/ppermute | solution.py:349
  30.6 12.7 %collective-permute-start.15 = (bf16[384,384]{1,0:T(8,128)(2,1)S(1)}, bf16[384,384]{1,0:T(8,128)(2,1)S(1)}, u32[]{:S(2)}, u32[]{:S(2)}) collective-permute-start(bf16[384,384]{1,0:T(8,128)(2,1)S(1)} %shard_map.92.f2.own), channel_id=1, source_target_pairs={{21,13},{30,22}} | collective-permute-start | bytes 884744 | tf_op jit(solution)/shard_map/ppermute | solution.py:349
  34.3 9.0 %collective-permute-start.16 = (bf16[384,384]{1,0:T(8,128)(2,1)S(1)}, bf16[384,384]{1,0:T(8,128)(2,1)S(1)}, u32[]{:S(2)}, u32[]{:S(2)}) collective-permute-start(bf16[384,384]{1,0:T(8,128)(2,1)S(1)} %shard_map.92.f2.own), channel_id=1, source_target_pairs={{30,14}} | collective-permute-start | bytes 884744 | tf_op jit(solution)/shard_map/ppermute | solution.py:349
  35.0 8.7 %collective-permute-start.19 = (bf16[384,384]{1,0:T(8,128)(2,1)S(1)}, bf16[384,384]{1,0:T(8,128)(2,1)S(1)}, u32[]{:S(2)}, u32[]{:S(2)}) collective-permute-start(bf16[384,384]{1,0:T(8,128)(2,1)S(1)} %shard_map.99), channel_id=1, source_target_pairs={{7,6},{15,14},{23,22},{5,4}} | collective-permute-start | bytes 884744 | tf_op jit(solution)/shard_map/ppermute | solution.py:349
